TPU v7x, 256 devices: a whole 4x4x8 slice. The times are simulated.
256 devices in a mesh: dp: 4 (over x), expert: 64 (over y, z, core).
Axes of the slice: x: 4, y: 4, z: 8, core: 2. Of those that a mesh axis runs over, the one named last changes fastest.
Arguments:
- tokens: bfloat16 [32768, 2048], P(('dp', 'expert')), may hold values from -6 to 6
- out_grad: bfloat16 [32768, 2048], P(('dp', 'expert')), may hold values from -6 to 6
- gate_probs: bfloat16 [32768, 4], P(('dp', 'expert')), may hold values from 0.049804688 to 0.59765625
- expert_ids: int32 [32768, 4], P(('dp', 'expert')), may hold values from 0 to 63, all different within a row; in each aligned block of 128 rows (0 to 127, 128 to 255, ...) at most 9 rows name the same one
- w_gate: bfloat16 [64, 2048, 768], P('expert'), may hold values from -0.125 to 0.125
- w_up: bfloat16 [64, 2048, 768], P('expert'), may hold values from -0.125 to 0.125
- w_down: bfloat16 [64, 768, 2048], P('expert'), may hold values from -0.21875 to 0.21875
Outputs:
- tokens_grad: bfloat16 [32768, 2048], P(('dp', 'expert'))
- probs_grad: float32 [32768, 4], P(('dp', 'expert'))
- gate_weight_grad: bfloat16 [64, 2048, 768], P('expert', None, 'dp')
- up_weight_grad: bfloat16 [64, 2048, 768], P('expert', None, 'dp')
- down_weight_grad: bfloat16 [64, 768, 2048], P('expert', 'dp')
Inputs may be any that keep to these rules, and one draw needn't show every extreme that they name: `expert_ids`: each row names 4 different experts. In each aligned block of 128 rows (the rows of one device) no expert is named by more than 9 rows, a bound that some block reaches.
All inputs are finite; a program needn't handle non-finite values.
Results may differ from a plain program's by a relative error of at most 0.0057.
Values may be sent and summed in bfloat16 or wider, within the bound.
No kernel may reach another device: no remote copies, remote signals or barrier semaphores. Data moves between devices by JAX's collectives and lax.ppermute only.
A program may use at most 192 MiB of HBM per device.

v0:
```python
import jax
import jax.numpy as jnp
from jax import lax
from jax.sharding import PartitionSpec as P


def expert_work(x_slots, dy_slots, prob_slots, gate_mat, up_mat, down_mat):
    gate_pre = jnp.dot(x_slots, gate_mat, preferred_element_type=jnp.float32)
    up_pre = jnp.dot(x_slots, up_mat, preferred_element_type=jnp.float32)
    sigmoid_gate = jax.nn.sigmoid(gate_pre)
    silu_gate = gate_pre * sigmoid_gate
    hidden_act = silu_gate * up_pre
    hidden = hidden_act.astype(jnp.bfloat16)
    grad_hidden = lax.dot_general(
        dy_slots, down_mat, (((1,), (1,)), ((), ())), preferred_element_type=jnp.float32
    )
    prob_grad = jnp.sum(hidden_act * grad_hidden, axis=1)
    scaled_hidden = prob_slots[:, None] * grad_hidden
    grad_gate = (
        scaled_hidden * up_pre * sigmoid_gate * (1.0 + gate_pre * (1.0 - sigmoid_gate))
    ).astype(jnp.bfloat16)
    grad_up = (scaled_hidden * silu_gate).astype(jnp.bfloat16)
    scaled_dy = (prob_slots[:, None] * dy_slots.astype(jnp.float32)).astype(jnp.bfloat16)
    row_grad = lax.dot_general(
        grad_gate, gate_mat, (((1,), (1,)), ((), ())), preferred_element_type=jnp.float32
    )
    row_grad = row_grad + lax.dot_general(
        grad_up, up_mat, (((1,), (1,)), ((), ())), preferred_element_type=jnp.float32
    )
    return (hidden, grad_gate, grad_up, scaled_dy, row_grad, prob_grad)


def outer_rows(left, right):
    return lax.dot_general(
        left, right, (((0,), (0,)), ((), ())), preferred_element_type=jnp.float32
    )


def per_device(tokens, out_grad, gate_probs, expert_ids, w_gate, w_up, w_down):
    n_experts = lax.axis_size("expert")
    tok_rows, model_width = tokens.shape
    top_k = expert_ids.shape[1]
    capacity = tok_rows * top_k * 9 // (8 * n_experts)
    assigns = tok_rows * top_k
    flat_ids = expert_ids.reshape(assigns)
    onehot = (flat_ids[:, None] == jnp.arange(n_experts, dtype=jnp.int32)[None, :]).astype(
        jnp.int32
    )
    slot_rank = jnp.sum((jnp.cumsum(onehot, axis=0) - onehot) * onehot, axis=1)
    position = flat_ids * capacity + slot_rank
    table = (
        jnp.full((n_experts * capacity,), assigns, jnp.int32)
        .at[position]
        .set(jnp.arange(assigns, dtype=jnp.int32))
    )
    token_row = table // top_k
    tokens_pad = jnp.concatenate([tokens, jnp.zeros((1, model_width), jnp.bfloat16)], axis=0)
    grad_pad = jnp.concatenate([out_grad, jnp.zeros((1, model_width), jnp.bfloat16)], axis=0)
    probs_pad = jnp.concatenate(
        [gate_probs.reshape(assigns), jnp.zeros((1,), jnp.bfloat16)], axis=0
    )
    send_x = tokens_pad[token_row].reshape(n_experts, capacity, model_width)
    send_dy = grad_pad[token_row].reshape(n_experts, capacity, model_width)
    send_prob = probs_pad[table].reshape(n_experts, capacity)
    recv_x, recv_dy, recv_prob = (
        lax.all_to_all(send_x, "expert", split_axis=0, concat_axis=0, tiled=True),
        lax.all_to_all(send_dy, "expert", split_axis=0, concat_axis=0, tiled=True),
        lax.all_to_all(send_prob, "expert", split_axis=0, concat_axis=0, tiled=True),
    )
    slot_rows = n_experts * capacity
    x_slots = recv_x.reshape(slot_rows, model_width)
    dy_slots = recv_dy.reshape(slot_rows, model_width)
    prob_slots = recv_prob.reshape(slot_rows).astype(jnp.float32)
    gate_mat = w_gate[0]
    up_mat = w_up[0]
    down_mat = w_down[0]
    hidden, grad_gate, grad_up, scaled_dy, row_grad, prob_grad = expert_work(
        x_slots, dy_slots, prob_slots, gate_mat, up_mat, down_mat
    )
    back_rows, back_probs = (
        lax.all_to_all(
            row_grad.reshape(n_experts, capacity, model_width),
            "expert",
            split_axis=0,
            concat_axis=0,
            tiled=True,
        ),
        lax.all_to_all(
            prob_grad.reshape(n_experts, capacity),
            "expert",
            split_axis=0,
            concat_axis=0,
            tiled=True,
        ),
    )
    picked_rows = back_rows.reshape(slot_rows, model_width)[position]
    tokens_grad = jnp.sum(picked_rows.reshape(tok_rows, top_k, model_width), axis=1).astype(
        jnp.bfloat16
    )
    probs_grad = back_probs.reshape(slot_rows)[position].reshape(tok_rows, top_k)
    gate_term = outer_rows(x_slots, grad_gate)
    up_term = outer_rows(x_slots, grad_up)
    down_term = outer_rows(hidden, scaled_dy)
    gate_sum, up_sum, down_sum = (
        lax.psum_scatter(gate_term, "dp", scatter_dimension=1, tiled=True),
        lax.psum_scatter(up_term, "dp", scatter_dimension=1, tiled=True),
        lax.psum_scatter(down_term, "dp", scatter_dimension=0, tiled=True),
    )
    gate_weight_grad = gate_sum.astype(jnp.bfloat16)[None]
    up_weight_grad = up_sum.astype(jnp.bfloat16)[None]
    down_weight_grad = down_sum.astype(jnp.bfloat16)[None]
    return (tokens_grad, probs_grad, gate_weight_grad, up_weight_grad, down_weight_grad)


def solution(mesh):
    in_specs = (
        P(("dp", "expert"), None),
        P(("dp", "expert"), None),
        P(("dp", "expert"), None),
        P(("dp", "expert"), None),
        P("expert", None, None),
        P("expert", None, None),
        P("expert", None, None),
    )
    out_specs = (
        P(("dp", "expert"), None),
        P(("dp", "expert"), None),
        P("expert", None, "dp"),
        P("expert", None, "dp"),
        P("expert", "dp", None),
    )
    return jax.shard_map(
        per_device, mesh=mesh, in_specs=in_specs, out_specs=out_specs, check_vma=False
    )
```

profile of v0, /device:TPU:1, one launch (start us, length us, event | category | flops | bytes accessed | tf_op | source)
XLA Modules:
  0.0 543.5 jit_solution(4793516404988532871)
XLA Ops:
  7.2 0.8 broadcast_multiply_fusion
  8.0 0.9 copy.20
  9.1 0.8 copy.18
  10.3 1.2 reduce-window.6
  11.5 0.2 slice_reduce_fusion
  11.9 2.4 scatter_custom_fusion
  14.4 3.9 gather_fusion
  18.4 0.8 all_to_all.28
  19.2 13.1 %all-to-all-start = ((bf16[64,1,9]{2,1,0:T(2,128)(2,1)}), bf16[64,1,9]{2,1,0:T(2,128)(2,1)S(1)}, u32[]{:S(2)}, u32[]{:S(2)}) async-start(bf16[64,1,9]{2,1,0:T(2,128)(2,1)} %all_to_all.28), calls=%async_computation | async-start | bytes 65536 | tf_op jit(solution)/shard_map/all_to_all | solution.py:68
  32.3 1.9 concatenate.11
  34.2 8.0 %gather_fusion.2 = bf16[576,2048]{1,0:T(8,128)(2,1)} fusion(bf16[129,2048]{1,0:T(8,128)(2,1)} %concatenate.11, s32[1024]{0:T(1024)S(1)} %get-tuple-element.20), kind=kCustom, calls=%fused_computation.2 | custom fusion | bytes 4720896 | tf_op jit(solution)/shard_map/gather | solution.py:62
  42.2 4.6 reshape.108
  46.8 10.5 %all-to-all-start.2 = ((bf16[64,9,2048]{2,1,0:T(8,128)(2,1)}), bf16[64,9,2048]{2,1,0:T(8,128)(2,1)}, u32[]{:S(2)}, u32[]{:S(2)}) async-start(bf16[64,9,2048]{2,1,0:T(8,128)(2,1)} %reshape.108), calls=%async_computation.2 | async-start | bytes 8388608 | tf_op jit(solution)/shard_map/all_to_all | solution.py:66
  57.3 1.9 concatenate.10
  59.2 8.0 %gather_fusion.1 = bf16[576,2048]{1,0:T(8,128)(2,1)} fusion(bf16[129,2048]{1,0:T(8,128)(2,1)} %concatenate.10, s32[1024]{0:T(1024)S(1)} %get-tuple-element.20), kind=kCustom, calls=%fused_computation.1 | custom fusion | bytes 4720896 | tf_op jit(solution)/shard_map/gather | solution.py:63
  67.2 4.6 reshape.106
  71.8 81.4 %all-to-all-done.2 = bf16[64,9,2048]{2,1,0:T(8,128)(2,1)} async-done(((bf16[64,9,2048]{2,1,0:T(8,128)(2,1)}), bf16[64,9,2048]{2,1,0:T(8,128)(2,1)}, u32[]{:S(2)}, u32[]{:S(2)}) %all-to-all-start.2) | async-done | bytes 2359328 | tf_op jit(solution)/shard_map/all_to_all | solution.py:66
  153.2 5.9 %all-to-all-start.1 = ((bf16[64,9,2048]{2,1,0:T(8,128)(2,1)}), bf16[64,9,2048]{2,1,0:T(8,128)(2,1)}, u32[]{:S(2)}, u32[]{:S(2)}) async-start(bf16[64,9,2048]{2,1,0:T(8,128)(2,1)} %reshape.106), calls=%async_computation.1 | async-start | bytes 8388608 | tf_op jit(solution)/shard_map/all_to_all | solution.py:67
  159.1 0.2 reduce-scatter.8.cloned.1.call-start
  159.6 4.7 reshape.109
  164.3 5.1 fusion.2
  169.4 3.2 fusion.6
  172.6 82.4 %all-to-all-done.1 = bf16[64,9,2048]{2,1,0:T(8,128)(2,1)} async-done(((bf16[64,9,2048]{2,1,0:T(8,128)(2,1)}), bf16[64,9,2048]{2,1,0:T(8,128)(2,1)}, u32[]{:S(2)}, u32[]{:S(2)}) %all-to-all-start.1) | async-done | bytes 2359328 | tf_op jit(solution)/shard_map/all_to_all | solution.py:67
  255.0 4.7 reshape.107
  259.6 8.2 %fusion.13 = f32[768,2048]{1,0:T(8,128)} fusion(bf16[576,2048]{1,0:T(8,128)(2,1)} %reshape.107, f32[576]{0:T(1024)S(1)} %reshape.115, f32[576,768]{1,0:T(8,128)} %fusion.6, f32[576,768]{1,0:T(8,128)} %fusion.2), kind=kOutput, calls=%fused_computation.18 | convolution fusion | flops 1818132480 | bytes 12192000 | tf_op jit(solution)/shard_map/dot_general | solution.py:34
  267.9 7.4 %multiply_reduce_fusion = (f32[576]{0:T(1024)S(1)}, bf16[576,768]{1,0:T(8,128)(2,1)}, bf16[576,768]{1,0:T(8,128)(2,1)S(1)}) fusion(f32[576,768]{1,0:T(8,128)} %fusion.6, f32[576,768]{1,0:T(8,128)} %fusion.2, f32[576]{0:T(1024)S(1)} %reshape.115, bf16[576,2048]{1,0:T(8,128)(2,1)} %reshape.107, bf16[1,768,2048]{2,1,0:T(8,128)(2,1)} %param.13), kind=kOutput, calls=%fused_computation.20 | convolution fusion | flops 1819459072 | bytes 10818048 | tf_op jit(solution)/shard_map/dot_general | solution.py:14
  275.3 0.9 copy-done.5
  276.2 4.6 fusion.28
  280.8 0.3 reduce-scatter.4.cloned.1.call-start
  281.1 7.2 %fusion.27 = f32[2048,768]{0,1:T(8,128)} fusion(bf16[576,2048]{1,0:T(8,128)(2,1)} %reshape.109, bf16[576,768]{1,0:T(8,128)(2,1)} %get-tuple-element.16), kind=kOutput, calls=%fused_computation.57 | convolution fusion | flops 1811939328 | bytes 9535488 | tf_op jit(solution)/shard_map/dot_general | solution.py:34
  288.3 0.7 all_to_all.26
  289.1 6.1 %all-to-all-start.4 = ((f32[64,1,9]{2,1,0:T(1,128)}), f32[64,1,9]{2,1,0:T(1,128)S(1)}, u32[]{:S(2)}, u32[]{:S(2)}) async-start(f32[64,1,9]{2,1,0:T(1,128)} %bitcast.6), calls=%async_computation.4 | async-start | bytes 65536 | tf_op jit(solution)/shard_map/all_to_all | solution.py:88
  295.2 3.3 fusion
  298.5 4.2 fusion.10
  302.7 6.2 %reshape.110 = f32[64,9,2048]{2,1,0:T(8,128)} reshape(f32[576,2048]{1,0:T(8,128)} %fusion.10) | data formatting | bytes 9437184 | tf_op jit(solution)/shard_map/reshape | solution.py:82
  308.9 10.5 %all-to-all-start.3 = ((f32[64,9,2048]{2,1,0:T(8,128)}), f32[64,9,2048]{2,1,0:T(8,128)}, u32[]{:S(2)}, u32[]{:S(2)}) async-start(f32[64,9,2048]{2,1,0:T(8,128)} %reshape.110), calls=%async_computation.3 | async-start | bytes 16777216 | tf_op jit(solution)/shard_map/all_to_all | solution.py:81
  319.5 0.5 broadcast.108
  320.0 0.7 reduce.9
  320.8 2.3 gather_fusion.4
  323.2 0.7 copy.25
  323.9 181.3 %all-to-all-done.3 = f32[64,9,2048]{2,1,0:T(8,128)} async-done(((f32[64,9,2048]{2,1,0:T(8,128)}), f32[64,9,2048]{2,1,0:T(8,128)}, u32[]{:S(2)}, u32[]{:S(2)}) %all-to-all-start.3) | async-done | bytes 4718624 | tf_op jit(solution)/shard_map/all_to_all | solution.py:81
  505.2 6.1 %reshape.111 = f32[576,2048]{1,0:T(8,128)} reshape(f32[64,9,2048]{2,1,0:T(8,128)} %all-to-all-done.3) | data formatting | bytes 9437184 | tf_op jit(solution)/shard_map/reshape | solution.py:96
  511.2 7.7 %gather_fusion.3 = f32[512,2048]{1,0:T(8,128)} fusion(f32[576,2048]{1,0:T(8,128)} %reshape.111, s32[1024]{0:T(1024)S(1)} %pad_clamp_fusion), kind=kCustom, calls=%fused_computation.3 | custom fusion | bytes 8390656 | tf_op jit(solution)/shard_map/gather | solution.py:96
  518.9 5.2 reshape.112
  524.1 5.7 %reduce_sum.31 = bf16[128,2048]{1,0:T(8,128)(2,1)} reduce(f32[128,4,2048]{2,1,0:T(4,128)} %reshape.112, f32[]{:T(128)} %constant.40.clone.1), dimensions={1}, to_apply=%region_4.5 | reduce | flops 786432 | bytes 4718596 | tf_op jit(solution)/shard_map/reduce_sum | solution.py:97
  529.8 2.4 convert_bitcast_fusion
  532.2 2.4 convert_bitcast_fusion.1
  534.6 2.4 convert_bitcast_fusion.2
  (41 shorter events, 1.4 us)
Async XLA Ops:
  7.2 157.1 %copy-start = (bf16[1,2048,768]{2,1,0:T(8,128)(2,1)S(1)}, bf16[1,2048,768]{2,1,0:T(8,128)(2,1)}, u32[]{:S(2)}) copy-start(bf16[1,2048,768]{2,1,0:T(8,128)(2,1)} %param.11) | copy-start | bytes 9437188
  19.2 27.6 %all-to-all-start = ((bf16[64,1,9]{2,1,0:T(2,128)(2,1)}), bf16[64,1,9]{2,1,0:T(2,128)(2,1)S(1)}, u32[]{:S(2)}, u32[]{:S(2)}) async-start(bf16[64,1,9]{2,1,0:T(2,128)(2,1)} %all_to_all.28), calls=%async_computation | async-start | bytes 65536 | tf_op jit(solution)/shard_map/all_to_all | solution.py:68
  46.8 106.4 %all-to-all-start.2 = ((bf16[64,9,2048]{2,1,0:T(8,128)(2,1)}), bf16[64,9,2048]{2,1,0:T(8,128)(2,1)}, u32[]{:S(2)}, u32[]{:S(2)}) async-start(bf16[64,9,2048]{2,1,0:T(8,128)(2,1)} %reshape.108), calls=%async_computation.2 | async-start | bytes 8388608 | tf_op jit(solution)/shard_map/all_to_all | solution.py:66
  153.2 101.8 %all-to-all-start.1 = ((bf16[64,9,2048]{2,1,0:T(8,128)(2,1)}), bf16[64,9,2048]{2,1,0:T(8,128)(2,1)}, u32[]{:S(2)}, u32[]{:S(2)}) async-start(bf16[64,9,2048]{2,1,0:T(8,128)(2,1)} %reshape.106), calls=%async_computation.1 | async-start | bytes 8388608 | tf_op jit(solution)/shard_map/all_to_all | solution.py:67
  159.1 370.7 %reduce-scatter.8.cloned.1.call-start = ((), (), s32[]{:S(2)}) async-start(), calls=%async_computation.10 | async-start | bytes 7864320 | tf_op jit(solution)/shard_map/reduce_scatter | solution.py:107
  164.3 5.1 copy-start.1
  164.3 5.1 copy-start.3
  267.9 264.3 %reduce-scatter.6.cloned.1.call-start = ((), (), s32[]{:S(2)}) async-start(), calls=%async_computation.9 | async-start | bytes 7864320 | tf_op jit(solution)/shard_map/reduce_scatter | solution.py:106
  267.9 8.3 %copy-start.2 = (bf16[576,2048]{1,0:T(8,128)(2,1)S(1)}, bf16[576,2048]{1,0:T(8,128)(2,1)}, u32[]{:S(2)}) copy-start(bf16[576,2048]{1,0:T(8,128)(2,1)} %reshape.109) | copy-start | bytes 7077892
  275.3 0.9 copy-start.5
  280.8 253.8 %reduce-scatter.4.cloned.1.call-start = ((), (), s32[]{:S(2)}) async-start(), calls=%async_computation.8 | async-start | bytes 7864320 | tf_op jit(solution)/shard_map/reduce_scatter | solution.py:105
  289.1 19.9 %all-to-all-start.4 = ((f32[64,1,9]{2,1,0:T(1,128)}), f32[64,1,9]{2,1,0:T(1,128)S(1)}, u32[]{:S(2)}, u32[]{:S(2)}) async-start(f32[64,1,9]{2,1,0:T(1,128)} %bitcast.6), calls=%async_computation.4 | async-start | bytes 65536 | tf_op jit(solution)/shard_map/all_to_all | solution.py:88
  295.1 3.4 copy-start.4
  295.2 3.4 copy-start.6
  308.9 196.3 %all-to-all-start.3 = ((f32[64,9,2048]{2,1,0:T(8,128)}), f32[64,9,2048]{2,1,0:T(8,128)}, u32[]{:S(2)}, u32[]{:S(2)}) async-start(f32[64,9,2048]{2,1,0:T(8,128)} %reshape.110), calls=%async_computation.3 | async-start | bytes 16777216 | tf_op jit(solution)/shard_map/all_to_all | solution.py:81
Sparse Core Ops, SparseCore 0:
  268.0 62.8 reduce-scatter.7
  333.5 66.2 reduce-scatter.5
  402.3 66.2 reduce-scatter.3
where the time goes:
time: 545 us; the launch traced here: 544 us
  waiting for transfers between devices  345 us (63%)
  local copies, waits for them, and re-layouts  78.7 us (14%)
  starting transfers between devices  46.7 us (9%)
  matrix products  43.1 us (8%)
  other arithmetic  16 us (3%)
  between operations  14 us (3%)
    all_to_all x1, waiting for transfers between devices, per_device(): lax.all_to_all(row_grad.reshape(n_experts, capacity, model_width), 'exper...  181 us
    all_to_all x1, waiting for transfers between devices, per_device(): lax.all_to_all(send_dy, 'expert', split_axis=0, concat_axis=0, tiled=True)  82.4 us
    all_to_all x1, waiting for transfers between devices, per_device(): lax.all_to_all(send_x, 'expert', split_axis=0, concat_axis=0, tiled=True)  81.4 us
    dot_general x3, matrix products, outer_rows(): lax.dot_general(left, right, (((0,), (0,)), ((), ())), preferred_element_...  20 us
    all_to_all x1, starting transfers between devices, per_device(): lax.all_to_all(send_prob, 'expert', split_axis=0, concat_axis=0, tiled=True)  13.1 us
  transfers between devices with their start and end apart: 8, of which 3 were waited for; matrix products, arithmetic and copies ran while one was open for 20% of the time, Pallas kernels for 0%

commit v1 on v0

v1 whole, which is shorter than its diff:
```python
import jax
import jax.numpy as jnp
from jax import lax
from jax.experimental import pallas as pl
from jax.experimental.pallas import tpu as pltpu
from jax.sharding import PartitionSpec as P

BF = jnp.bfloat16
F32 = jnp.float32
TOP = 4
TOK = 128
EXP = 64
MAIN = 8
ROWS = EXP * MAIN
ALL = ROWS + EXP
D = 2048
H = 768
SEG = D // MAIN
N_DP = 4
HS = H // N_DP
X_COLS = D + SEG
Y_COLS = D + SEG + 128


def dot(a, b):
    return jnp.dot(a, b, preferred_element_type=F32)


def dot_nt(a, b):
    return lax.dot_general(a, b, (((1,), (1,)), ((), ())), preferred_element_type=F32)


def dot_tn(a, b):
    return lax.dot_general(a, b, (((0,), (0,)), ((), ())), preferred_element_type=F32)


def iota(shape, axis):
    return lax.broadcasted_iota(jnp.int32, shape, axis)


def one(mask):
    return jnp.where(mask, 1.0, 0.0)


def slot_masks(ids):
    lane_e = iota((EXP, TOK), 0)
    picks = [ids[k : k + 1, :] == lane_e for k in range(TOP)]
    member = picks[0] | picks[1] | picks[2] | picks[3]
    before = one(iota((TOK, TOK), 0) < iota((TOK, TOK), 1)).astype(BF)
    rank = jnp.where(member, dot(one(member).astype(BF), before), 200.0)
    spread = one((iota((ROWS, EXP), 0) >> 3) == iota((ROWS, EXP), 1)).astype(BF)
    rank_rows = dot(spread, rank.astype(BF))
    return picks, spread, rank_rows


def spare_masks(rank_rows):
    sub = iota((ROWS, TOK), 0) & (MAIN - 1)
    ninth = rank_rows == float(MAIN)
    return [one(ninth & (sub == j)).astype(BF) for j in range(MAIN)]


def main_mask(rank_rows):
    sub = iota((ROWS, TOK), 0) & (MAIN - 1)
    return rank_rows == sub.astype(F32)


def pack_kernel(ids_ref, data_ref, probs_ref, out_ref, *, with_probs):
    picks, spread, rank_rows = slot_masks(ids_ref[...])
    main = one(main_mask(rank_rows))
    out_ref[:, :D] = dot(main.astype(BF), data_ref[...]).astype(BF)
    spare = jnp.concatenate(spare_masks(rank_rows), axis=1)
    parts = jnp.concatenate([data_ref[:, j * SEG : (j + 1) * SEG] for j in range(MAIN)], axis=0)
    out_ref[:, D : D + SEG] = dot(spare, parts).astype(BF)
    if with_probs:
        chosen = jnp.zeros((EXP, TOK), F32)
        for k in range(TOP):
            chosen = chosen + jnp.where(picks[k], probs_ref[k : k + 1, :], 0.0)
        prob_rows = dot(spread, chosen.astype(BF))
        p_main = jnp.sum(main * prob_rows, axis=1, keepdims=True)
        p_ninth = jnp.sum(
            jnp.where(rank_rows == float(MAIN), prob_rows, 0.0), axis=1, keepdims=True
        )
        lane = iota((ROWS, 128), 1)
        out_ref[:, D + SEG :] = jnp.where(
            lane == 0, p_main, jnp.where(lane == 1, p_ninth, 0.0)
        ).astype(BF)


def pack(ids, data, probs, with_probs):
    cols = Y_COLS if with_probs else X_COLS

    def kernel(ids_ref, data_ref, probs_ref, out_ref):
        pack_kernel(ids_ref, data_ref, probs_ref, out_ref, with_probs=with_probs)

    return pl.pallas_call(
        kernel,
        out_shape=jax.ShapeDtypeStruct((ROWS, cols), BF),
        name="pack_dy" if with_probs else "pack_x",
    )(ids, data, probs)


def unfold_mask():
    row = iota((ROWS, ROWS), 0)
    col = iota((ROWS, ROWS), 1)
    return one(col == (row & (EXP - 1)) * MAIN + (row >> 6)).astype(BF)


def fold_mask():
    row = iota((ROWS, ROWS), 0)
    col = iota((ROWS, ROWS), 1)
    return one(col == (row & (MAIN - 1)) * EXP + (row >> 3)).astype(BF)


def fill_rows(recv_ref, rows_ref):
    rows_ref[:ROWS, :] = recv_ref[:, :D]
    spare = dot(unfold_mask(), recv_ref[:, D : D + SEG]).astype(BF)
    for j in range(MAIN):
        rows_ref[ROWS:, j * SEG : (j + 1) * SEG] = spare[j * EXP : (j + 1) * EXP, :]


def forward_kernel(recv_ref, gate_ref, up_ref, slope_ref, silu_ref, act_ref, rows_ref):
    @pl.when(pl.program_id(0) == 0)
    def _():
        fill_rows(recv_ref, rows_ref)

    gate_pre = dot(rows_ref[...], gate_ref[...])
    up_pre = dot(rows_ref[...], up_ref[...])
    sig = jax.nn.sigmoid(gate_pre)
    silu = gate_pre * sig
    silu_ref[...] = silu
    act_ref[...] = silu * up_pre
    slope_ref[...] = up_pre * sig * (1.0 + gate_pre * (1.0 - sig))


def forward(recv_x, gate_mat, up_mat):
    full = pl.BlockSpec((ROWS, X_COLS), lambda j: (0, 0))
    weight = pl.BlockSpec((D, 256), lambda j: (0, j))
    out = pl.BlockSpec((ALL, 256), lambda j: (0, j))
    shape = jax.ShapeDtypeStruct((ALL, H), F32)
    return pl.pallas_call(
        forward_kernel,
        grid=(H // 256,),
        in_specs=[full, weight, weight],
        out_specs=[out, out, out],
        out_shape=[shape, shape, shape],
        scratch_shapes=[pltpu.VMEM((ALL, D), BF)],
        name="forward",
    )(recv_x, gate_mat, up_mat)


def grads_kernel(
    recv_ref, down_ref, slope_ref, silu_ref, act_ref,
    grad_ref, scaled_ref, tail_ref, rows_ref, prob_ref, sum_ref,
):
    step = pl.program_id(0)

    @pl.when(step == 0)
    def _():
        fill_rows(recv_ref, rows_ref)
        tail = recv_ref[:, D + SEG :]
        pick = one(iota((EXP, ROWS), 1) == iota((EXP, ROWS), 0) * MAIN).astype(BF)
        prob_ref[:ROWS, :] = tail[:, 0:1].astype(F32)
        prob_ref[ROWS:, :] = dot(pick, tail)[:, 1:2]
        scaled_ref[...] = (prob_ref[...] * rows_ref[...].astype(F32)).astype(BF)
        sum_ref[...] = jnp.zeros_like(sum_ref)

    grad_hidden = dot_nt(rows_ref[...], down_ref[...])
    sum_ref[...] += jnp.sum(act_ref[...] * grad_hidden, axis=1, keepdims=True)
    scaled = prob_ref[...] * grad_hidden
    grad_ref[0] = (scaled * slope_ref[...]).astype(BF)
    grad_ref[1] = (scaled * silu_ref[...]).astype(BF)

    @pl.when(step == H // 256 - 1)
    def _():
        total = sum_ref[...]
        high = total.astype(BF)
        low = (total - high.astype(F32)).astype(BF)
        lane = iota((EXP, 128), 1)
        ninth = jnp.where(
            lane == 2,
            high[ROWS:].astype(F32),
            jnp.where(lane == 3, low[ROWS:].astype(F32), 0.0),
        ).astype(BF)
        spread = one((iota((ROWS, EXP), 0) >> 3) == iota((ROWS, EXP), 1)).astype(BF)
        lane_rows = iota((ROWS, 128), 1)
        tail_ref[...] = jnp.where(
            lane_rows == 0,
            high[:ROWS].astype(F32),
            jnp.where(lane_rows == 1, low[:ROWS].astype(F32), dot(spread, ninth)),
        ).astype(BF)


def grads(recv_dy, down_mat, slope, silu, act):
    full = pl.BlockSpec((ROWS, Y_COLS), lambda j: (0, 0))
    block = pl.BlockSpec((ALL, 256), lambda j: (0, j))
    return pl.pallas_call(
        grads_kernel,
        grid=(H // 256,),
        in_specs=[full, pl.BlockSpec((256, D), lambda j: (j, 0)), block, block, block],
        out_specs=[
            pl.BlockSpec((2, ALL, 256), lambda j: (0, 0, j)),
            pl.BlockSpec((ALL, D), lambda j: (0, 0)),
            pl.BlockSpec((ROWS, 128), lambda j: (0, 0)),
        ],
        out_shape=[
            jax.ShapeDtypeStruct((2, ALL, H), BF),
            jax.ShapeDtypeStruct((ALL, D), BF),
            jax.ShapeDtypeStruct((ROWS, 128), BF),
        ],
        scratch_shapes=[
            pltpu.VMEM((ALL, D), BF),
            pltpu.VMEM((ALL, 1), F32),
            pltpu.VMEM((ALL, 1), F32),
        ],
        name="grads",
    )(recv_dy, down_mat, slope, silu, act)


def back_kernel(grad_ref, gate_ref, up_ref, tail_ref, out_ref, spare_ref):
    step = pl.program_id(0)
    row = dot_nt(grad_ref[0], gate_ref[...]) + dot_nt(grad_ref[1], up_ref[...])
    row = row.astype(BF)
    out_ref[:, pl.ds(pl.multiple_of(step * 512, 512), 512)] = row[:ROWS]
    for h in range(2):
        spare_ref[pl.ds(pl.multiple_of((2 * step + h) * EXP, EXP), EXP), :] = row[
            ROWS:, h * SEG : (h + 1) * SEG
        ]

    @pl.when(step == D // 512 - 1)
    def _():
        out_ref[:, D : D + SEG] = dot(fold_mask(), spare_ref[...]).astype(BF)
        out_ref[:, D + SEG :] = tail_ref[...]


def back(grad, gate_mat, up_mat, tail):
    weight = pl.BlockSpec((512, H), lambda j: (j, 0))
    return pl.pallas_call(
        back_kernel,
        grid=(D // 512,),
        in_specs=[
            pl.BlockSpec((2, ALL, H), lambda j: (0, 0, 0)),
            weight,
            weight,
            pl.BlockSpec((ROWS, 128), lambda j: (0, 0)),
        ],
        out_specs=pl.BlockSpec((ROWS, Y_COLS), lambda j: (0, 0)),
        out_shape=jax.ShapeDtypeStruct((ROWS, Y_COLS), BF),
        scratch_shapes=[pltpu.VMEM((ROWS, SEG), BF)],
        name="back",
    )(grad, gate_mat, up_mat, tail)


def slices_kernel(own_ref, grad_ref, *out_refs):
    own = own_ref[0]
    for t in range(N_DP):
        piece = jnp.concatenate(
            [grad_ref[0, :, t * HS : (t + 1) * HS], grad_ref[1, :, t * HS : (t + 1) * HS]],
            axis=1,
        )
        for d in range(N_DP):

            @pl.when((own + d) % N_DP == t)
            def _(piece=piece, d=d):
                out_refs[d][...] = piece


def slices(own, grad):
    shape = jax.ShapeDtypeStruct((ALL, 2 * HS), BF)
    vmem = pl.BlockSpec(memory_space=pltpu.VMEM)
    return pl.pallas_call(
        slices_kernel,
        in_specs=[pl.BlockSpec(memory_space=pltpu.SMEM), vmem],
        out_specs=[vmem] * N_DP,
        out_shape=[shape] * N_DP,
        name="slices",
    )(own, grad)


def down_kernel(own_ref, act_ref, scaled_ref, *out_refs):
    own = own_ref[0]
    hidden = act_ref[...].astype(BF)
    for t in range(N_DP):
        term = dot_tn(hidden[:, t * HS : (t + 1) * HS], scaled_ref[...]).astype(BF)
        for d in range(N_DP):

            @pl.when((own + d) % N_DP == t)
            def _(term=term, d=d):
                out_refs[d][...] = term


def down_terms(own, act, scaled):
    shape = jax.ShapeDtypeStruct((HS, D), BF)
    vmem = pl.BlockSpec(memory_space=pltpu.VMEM)
    return pl.pallas_call(
        down_kernel,
        in_specs=[pl.BlockSpec(memory_space=pltpu.SMEM), vmem, vmem],
        out_specs=[vmem] * N_DP,
        out_shape=[shape] * N_DP,
        name="down_terms",
    )(own, act, scaled)


def gate_up_kernel(*refs):
    x_refs, spare_refs, g_refs = refs[:N_DP], refs[N_DP : 2 * N_DP], refs[2 * N_DP : 3 * N_DP]
    gate_ref, up_ref, turned_ref = refs[3 * N_DP :]
    step = pl.program_id(0)

    @pl.when(step == 0)
    def _():
        for g in range(N_DP):
            turned = g_refs[g][...].astype(F32).T.astype(BF)
            turned_ref[:, g * ROWS : (g + 1) * ROWS] = turned[:, :ROWS]
            turned_ref[:, N_DP * ROWS + g * EXP : N_DP * ROWS + (g + 1) * EXP] = turned[:, ROWS:]

    pick = one(iota((EXP, ROWS), 1) == iota((EXP, ROWS), 0) * MAIN + step).astype(BF)
    spare = jnp.concatenate(
        [dot(pick, spare_refs[g][...]).astype(BF) for g in range(N_DP)], axis=0
    )
    total = dot(turned_ref[:, N_DP * ROWS :], spare)
    for g in range(N_DP):
        total = total + dot(turned_ref[:, g * ROWS : (g + 1) * ROWS], x_refs[g][...])
    total = total.T
    gate_ref[...] = total[:, :HS].astype(BF)
    up_ref[...] = total[:, HS:].astype(BF)


def gate_up_terms(xs, gs):
    main = pl.BlockSpec((ROWS, SEG), lambda j: (0, j))
    spare = pl.BlockSpec((ROWS, SEG), lambda j: (0, MAIN))
    grad = pl.BlockSpec((ALL, 2 * HS), lambda j: (0, 0))
    out = pl.BlockSpec((SEG, HS), lambda j: (j, 0))
    shape = jax.ShapeDtypeStruct((D, HS), BF)
    return pl.pallas_call(
        gate_up_kernel,
        grid=(MAIN,),
        in_specs=[main] * N_DP + [spare] * N_DP + [grad] * N_DP,
        out_specs=[out, out],
        out_shape=[shape, shape],
        scratch_shapes=[pltpu.VMEM((2 * HS, N_DP * ALL), BF)],
        name="gate_up_terms",
    )(*xs, *xs, *gs)


def combine_kernel(ids_ref, recv_ref, rows_ref, probs_ref):
    picks, _, rank_rows = slot_masks(ids_ref[...])
    main = one(main_mask(rank_rows))
    total = dot_tn(main.astype(BF), recv_ref[:, :D])
    spare = jnp.concatenate(spare_masks(rank_rows), axis=1)
    extra = dot_tn(spare, recv_ref[:, D : D + SEG])
    for j in range(MAIN):
        rows_ref[:, j * SEG : (j + 1) * SEG] = (
            total[:, j * SEG : (j + 1) * SEG] + extra[j * TOK : (j + 1) * TOK, :]
        ).astype(BF)
    tail = recv_ref[:, D + SEG :].astype(F32)
    v_main = tail[:, 0:1] + tail[:, 1:2]
    v_ninth = tail[:, 2:3] + tail[:, 3:4]
    ninth = one((rank_rows == float(MAIN)) & ((iota((ROWS, TOK), 0) & (MAIN - 1)) == 0))
    values = main * v_main + ninth * v_ninth
    owner = iota((ROWS, TOK), 0) >> 3
    for k in range(TOP):
        hit = ids_ref[k : k + 1, :] == owner
        probs_ref[k : k + 1, :] = jnp.sum(jnp.where(hit, values, 0.0), axis=0, keepdims=True)


def combine(ids, recv):
    return pl.pallas_call(
        combine_kernel,
        out_shape=[
            jax.ShapeDtypeStruct((TOK, D), BF),
            jax.ShapeDtypeStruct((TOP, TOK), F32),
        ],
        name="combine",
    )(ids, recv)


def exchange(flat):
    out = lax.all_to_all(
        flat.reshape(EXP, MAIN, flat.shape[1]), "expert", split_axis=0, concat_axis=0, tiled=True
    )
    return out.reshape(flat.shape)


def shift(value, by):
    return lax.ppermute(value, "dp", [(i, (i + by) % N_DP) for i in range(N_DP)])


def per_device(tokens, out_grad, gate_probs, expert_ids, w_gate, w_up, w_down):
    own = lax.axis_index("dp").astype(jnp.int32).reshape(1)
    ids = expert_ids.T
    probs = gate_probs.T.astype(F32)
    gate_mat, up_mat, down_mat = w_gate[0], w_up[0], w_down[0]
    recv_x = exchange(pack(ids, tokens, probs, False))
    recv_dy = exchange(pack(ids, out_grad, probs, True))
    xs = [recv_x] + [shift(recv_x, d) for d in range(1, N_DP)]
    slope, silu, act = forward(recv_x, gate_mat, up_mat)
    grad, scaled, tail = grads(recv_dy, down_mat, slope, silu, act)
    pieces = slices(own, grad)
    gs = [pieces[0]] + [shift(pieces[d], d) for d in range(1, N_DP)]
    back_rows = exchange(back(grad, gate_mat, up_mat, tail))
    terms = down_terms(own, act, scaled)
    downs = [terms[0]] + [shift(terms[d], d) for d in range(1, N_DP)]
    down_grad = downs[0].astype(F32)
    for d in range(1, N_DP):
        down_grad = down_grad + downs[d].astype(F32)
    gate_grad, up_grad = gate_up_terms(xs, gs)
    tokens_grad, probs_grad = combine(ids, back_rows)
    return (
        tokens_grad,
        probs_grad.T,
        gate_grad[None],
        up_grad[None],
        down_grad.astype(BF)[None],
    )


def solution(mesh):
    rows = P(("dp", "expert"), None)
    weights = P("expert", None, None)
    return jax.shard_map(
        per_device,
        mesh=mesh,
        in_specs=(rows, rows, rows, rows, weights, weights, weights),
        out_specs=(rows, rows, P("expert", None, "dp"), P("expert", None, "dp"), P("expert", "dp", None)),
        check_vma=False,
    )
```

time: 545 us -> 373 us (0.68)
  waiting for transfers between devices: 345 us -> 261 us
  local copies, waits for them, and re-layouts: 78.7 us -> 5.68 us
  Pallas kernels: 0 us -> 62.6 us
  matrix products: 43.1 us -> 0 us
  between operations: 14 us -> 0.7 us
  other arithmetic: 16 us -> 3.77 us
  starting transfers between devices: 46.7 us -> 38.4 us
    all_to_all x5 -> x3, waiting for transfers between devices: 345 us -> 103 us  [exchange(): lax.all_to_all(flat.reshape(EXP, MAIN, flat.shape[1]), 'expert', split_ax...]
    ppermute x0 -> x9, waiting for transfers between devices: none -> 158 us  [shift(): lax.ppermute(value, 'dp', [(i, (i + by) % N_DP) for i in range(N_DP)])]
    pallas_call x0 -> x9, Pallas kernels: none -> 62.6 us  [the longest x1 12.4 us: gate_up_terms(): pl.pallas_call(gate_up_kernel, grid=(MAIN,), in_specs=[main] * N_DP + [sp...]
    dot_general x8 -> x0, matrix products: 43.1 us -> none  [the longest x3 20 us: outer_rows(): lax.dot_general(left, right, (((0,), (0,)), ((), ())), preferred_element_...]
    reshape x10 -> x0, local copies, waits for them, and re-layouts: 36.4 us -> none  [the longest x1 6.23 us: per_device(): row_grad.reshape(n_experts, capacity, model_width)]
    gather x5 -> x0, local copies, waits for them, and re-layouts: 29.9 us -> none  [the longest x1 7.97 us: per_device(): send_x = tokens_pad[token_row].reshape(n_experts, capacity, model_width)]
    all_to_all x5 -> x3, starting transfers between devices: 46.2 us -> 25.4 us  [exchange(): lax.all_to_all(flat.reshape(EXP, MAIN, flat.shape[1]), 'expert', split_ax...]
    ppermute x0 -> x9, starting transfers between devices: none -> 13 us  [shift(): lax.ppermute(value, 'dp', [(i, (i + by) % N_DP) for i in range(N_DP)])]
  transfers between devices with their start and end apart: 8 -> 12, of which waited for: 3 -> 6; matrix products, arithmetic and copies ran while one was open for 20% -> 2% of each run, Pallas kernels for 0% -> 10%
where the time goes in v1:
time: 373 us; the launch traced here: 372 us
  waiting for transfers between devices  261 us (70%)
  Pallas kernels  62.6 us (17%)
  starting transfers between devices  38.4 us (10%)
  local copies, waits for them, and re-layouts  5.68 us (2%)
  other arithmetic  3.77 us (1%)
    ppermute x9, waiting for transfers between devices, shift(): lax.ppermute(value, 'dp', [(i, (i + by) % N_DP) for i in range(N_DP)])  158 us
    all_to_all x3, waiting for transfers between devices, exchange(): lax.all_to_all(flat.reshape(EXP, MAIN, flat.shape[1]), 'expert', split_ax...  103 us
    all_to_all x3, starting transfers between devices, exchange(): lax.all_to_all(flat.reshape(EXP, MAIN, flat.shape[1]), 'expert', split_ax...  25.4 us
    ppermute x9, starting transfers between devices, shift(): lax.ppermute(value, 'dp', [(i, (i + by) % N_DP) for i in range(N_DP)])  13 us
    pallas_call x1, Pallas kernels, gate_up_terms(): pl.pallas_call(gate_up_kernel, grid=(MAIN,), in_specs=[main] * N_DP + [sp...  12.4 us
    pallas_call x1, Pallas kernels, forward(): pl.pallas_call(forward_kernel, grid=(H // 256,), in_specs=[full, weight,...  9.53 us
    pallas_call x1, Pallas kernels, grads(): pl.pallas_call(grads_kernel, grid=(H // 256,), in_specs=[full, pl.BlockSp...  9.36 us
    pallas_call x1, Pallas kernels, back(): pl.pallas_call(back_kernel, grid=(D // 512,), in_specs=[pl.BlockSpec((2,...  8.55 us
  transfers between devices with their start and end apart: 12, of which 6 were waited for; matrix products, arithmetic and copies ran while one was open for 2% of the time, Pallas kernels for 10%

profile of v1, /device:TPU:1, one launch (start us, length us, event | category | flops | bytes accessed | tf_op | source)
XLA Modules:
  0.0 372.2 jit_solution(15470540034399069161)
XLA Ops:
  0.6 1.3 convert_bitcast_fusion.probs_ref
  1.9 3.7 %pack_x.1 = bf16[512,2304]{1,0:T(8,128)(2,1)} custom-call(s32[4,128]{1,0:T(4,128)} %bitcast.34, bf16[128,2048]{1,0:T(8,128)(2,1)} %data_ref.3, f32[4,128]{1,0:T(4,128)} %convert_bitcast_fusion.probs_ref), custom_call_target="tpu_custom_call" | custom-call | tf_op jit(solution)/shard_map/pack_x/pallas_call | solution.py:95
  5.6 13.1 %all-to-all-start.1 = ((bf16[64,8,2304]{2,1,0:T(8,128)(2,1)}), bf16[64,8,2304]{2,1,0:T(8,128)(2,1)S(1)}, u32[]{:S(2)}, u32[]{:S(2)}) async-start(bf16[64,8,2304]{2,1,0:T(8,128)(2,1)} %bitcast.30), calls=%async_computation.1 | async-start | bytes 4718592 | tf_op jit(solution)/shard_map/all_to_all | solution.py:377
  18.8 3.9 %pack_dy.1 = bf16[512,2432]{1,0:T(8,128)(2,1)} custom-call(s32[4,128]{1,0:T(4,128)} %bitcast.35, bf16[128,2048]{1,0:T(8,128)(2,1)} %data_ref.2, f32[4,128]{1,0:T(4,128)} %convert_bitcast_fusion.probs_ref), custom_call_target="tpu_custom_call" | custom-call | tf_op jit(solution)/shard_map/pack_dy/pallas_call | solution.py:95
  22.7 52.7 %all-to-all-done.1 = bf16[64,8,2304]{2,1,0:T(8,128)(2,1)S(1)} async-done(((bf16[64,8,2304]{2,1,0:T(8,128)(2,1)}), bf16[64,8,2304]{2,1,0:T(8,128)(2,1)S(1)}, u32[]{:S(2)}, u32[]{:S(2)}) %all-to-all-start.1) | async-done | bytes 2359328 | tf_op jit(solution)/shard_map/all_to_all | solution.py:377
  75.4 0.0 copy-start
  75.4 1.4 copy-done
  76.8 6.1 %all-to-all-start = ((bf16[64,8,2432]{2,1,0:T(8,128)(2,1)}), bf16[64,8,2432]{2,1,0:T(8,128)(2,1)}, u32[]{:S(2)}, u32[]{:S(2)}) async-start(bf16[64,8,2432]{2,1,0:T(8,128)(2,1)} %bitcast.29), calls=%async_computation | async-start | bytes 4980736 | tf_op jit(solution)/shard_map/all_to_all | solution.py:377
  82.9 9.5 %forward.1 = (f32[576,768]{1,0:T(8,128)}, f32[576,768]{1,0:T(8,128)}, f32[576,768]{1,0:T(8,128)}) custom-call(bf16[512,2304]{1,0:T(8,128)(2,1)} %bitcast.18, bf16[2048,768]{1,0:T(8,128)(2,1)} %bitcast.24, bf16[2048,768]{1,0:T(8,128)(2,1)} %bitcast.26), custom_call_target="tpu_custom_call" | custom-call | tf_op jit(solution)/shard_map/forward/pallas_call | solution.py:140
  92.5 49.8 %all-to-all-done = bf16[64,8,2432]{2,1,0:T(8,128)(2,1)} async-done(((bf16[64,8,2432]{2,1,0:T(8,128)(2,1)}), bf16[64,8,2432]{2,1,0:T(8,128)(2,1)}, u32[]{:S(2)}, u32[]{:S(2)}) %all-to-all-start) | async-done | bytes 2490400 | tf_op jit(solution)/shard_map/all_to_all | solution.py:377
  142.3 9.4 %grads.1 = (bf16[2,576,768]{2,1,0:T(8,128)(2,1)}, bf16[576,2048]{1,0:T(8,128)(2,1)}, bf16[512,128]{1,0:T(8,128)(2,1)}) custom-call(bf16[512,2432]{1,0:T(8,128)(2,1)} %bitcast.3.recv_ref, bf16[768,2048]{1,0:T(8,128)(2,1)} %bitcast.31, f32[576,768]{1,0:T(8,128)} %get-tuple-element.23.slope_ref, f32[576,768]{1,0:T(8,128)} %get-tuple-element.24.silu_ref, ...), custom_call_target="tpu_custom_call" | custom-call | tf_op jit(solution)/shard_map/grads/pallas_call | solution.py:196
  151.7 8.6 %back.1 = bf16[512,2432]{1,0:T(8,128)(2,1)} custom-call(bf16[2,576,768]{2,1,0:T(8,128)(2,1)} %get-tuple-element.26.grad_ref, bf16[2048,768]{1,0:T(8,128)(2,1)} %bitcast.25, bf16[2048,768]{1,0:T(8,128)(2,1)} %bitcast.27, bf16[512,128]{1,0:T(8,128)(2,1)} %get-tuple-element.27.tail_ref), custom_call_target="tpu_custom_call" | custom-call | tf_op jit(solution)/shard_map/back/pallas_call | solution.py:237
  160.2 0.0 copy-start.1
  160.2 6.1 %all-to-all-start.2 = ((bf16[64,8,2432]{2,1,0:T(8,128)(2,1)}), bf16[64,8,2432]{2,1,0:T(8,128)(2,1)}, u32[]{:S(2)}, u32[]{:S(2)}) async-start(bf16[64,8,2432]{2,1,0:T(8,128)(2,1)} %bitcast.28), calls=%async_computation.2 | async-start | bytes 4980736 | tf_op jit(solution)/shard_map/all_to_all | solution.py:377
  166.3 0.0 copy-done.1
  166.3 1.3 collective-permute-start
  167.6 2.4 collective-permute-start.1
  170.1 1.2 collective-permute-start.2
  171.3 8.0 %down_terms.1 = (bf16[192,2048]{1,0:T(8,128)(2,1)}, bf16[192,2048]{1,0:T(8,128)(2,1)}, bf16[192,2048]{1,0:T(8,128)(2,1)}, bf16[192,2048]{1,0:T(8,128)(2,1)}) custom-call(s32[1]{0:T(128)} %bitcast.12.own_ref, f32[576,768]{1,0:T(8,128)} %get-tuple-element.25.act_ref, bf16[576,2048]{1,0:T(8,128)(2,1)} %get-tuple-element.36.scaled_ref), custom_call_target="tpu_custom_call" | custom-call | tf_op jit(solution)/shard_map/down_terms/pallas_call | solution.py:294
  179.3 0.3 collective-permute-start.6
  179.6 3.5 slices.1
  183.1 0.0 collective-permute-start.3
  183.1 113.7 %collective-permute-done.3.refs_9_ = bf16[576,384]{1,0:T(8,128)(2,1)S(1)} collective-permute-done((bf16[576,384]{1,0:T(8,128)(2,1)}, bf16[576,384]{1,0:T(8,128)(2,1)S(1)}, u32[]{:S(2)}, u32[]{:S(2)}) %collective-permute-start.3) | collective-permute-done | bytes 442400 | tf_op jit(solution)/shard_map/ppermute | solution.py:384
  296.8 0.0 copy-start.3
  296.8 1.5 collective-permute-start.7
  298.4 0.0 collective-permute-done.6
  298.4 0.9 collective-permute-start.8
  299.3 17.0 %collective-permute-done.7 = bf16[192,2048]{1,0:T(8,128)(2,1)S(1)} collective-permute-done((bf16[192,2048]{1,0:T(8,128)(2,1)}, bf16[192,2048]{1,0:T(8,128)(2,1)S(1)}, u32[]{:S(2)}, u32[]{:S(2)}) %collective-permute-start.7) | collective-permute-done | bytes 786464 | tf_op jit(solution)/shard_map/ppermute | solution.py:384
  316.3 1.5 collective-permute-start.4
  317.8 16.3 %collective-permute-done.8 = bf16[192,2048]{1,0:T(8,128)(2,1)S(1)} collective-permute-done((bf16[192,2048]{1,0:T(8,128)(2,1)}, bf16[192,2048]{1,0:T(8,128)(2,1)S(1)}, u32[]{:S(2)}, u32[]{:S(2)}) %collective-permute-start.8) | collective-permute-done | bytes 786464 | tf_op jit(solution)/shard_map/ppermute | solution.py:384
  334.1 0.0 copy-done.3
  334.1 3.8 %collective-permute-start.5 = (bf16[576,384]{1,0:T(8,128)(2,1)}, bf16[576,384]{1,0:T(8,128)(2,1)S(1)}, u32[]{:S(2)}, u32[]{:S(2)}) collective-permute-start(bf16[576,384]{1,0:T(8,128)(2,1)} %get-tuple-element.33), channel_id=1, source_target_pairs={{0,192},{64,0},{128,64},{192,128},{1,193},{65,1},{129,65},{193,129... | collective-permute-start | bytes 1327112 | tf_op jit(solution)/shard_map/ppermute | solution.py:384
  337.9 2.5 fusion
  340.4 0.0 collective-permute-done.4.refs_10_
  340.4 0.0 copy-start.4
  340.4 11.5 %collective-permute-done.5.refs_11_ = bf16[576,384]{1,0:T(8,128)(2,1)S(1)} collective-permute-done((bf16[576,384]{1,0:T(8,128)(2,1)}, bf16[576,384]{1,0:T(8,128)(2,1)S(1)}, u32[]{:S(2)}, u32[]{:S(2)}) %collective-permute-start.5) | collective-permute-done | bytes 442400 | tf_op jit(solution)/shard_map/ppermute | solution.py:384
  351.9 0.0 copy-start.5
  351.9 0.0 collective-permute-done.refs_1_.refs_5_
  351.9 0.0 collective-permute-done.1.refs_2_.refs_6_
  351.9 0.0 collective-permute-done.2.refs_3_.refs_7_
  351.9 0.0 copy-done.4
  351.9 0.7 copy-done.5
  352.6 12.4 %gate_up_terms.1 = (bf16[2048,192]{1,0:T(8,128)(2,1)}, bf16[2048,192]{1,0:T(8,128)(2,1)}) custom-call(bf16[512,2304]{1,0:T(8,128)(2,1)} %bitcast.19, bf16[512,2304]{1,0:T(8,128)(2,1)} %collective-permute-done.refs_1_.refs_5_, bf16[512,2304]{1,0:T(8,128)(2,1)} %collective-permute-done.1.refs_2_.refs_6_, ...), custom_call_target="tpu_custom_call" | custom-call | tf_op jit(solution)/shard_map/gate_up_terms/pallas_call | solution.py:333
  365.0 2.3 copy.12
  367.3 0.0 copy-done.2
  367.3 1.2 copy.13
  368.5 0.0 all-to-all-done.2
  368.5 3.6 combine.1
  (1 shorter events, 0.0 us)
Async XLA Ops:
  5.6 69.8 %all-to-all-start.1 = ((bf16[64,8,2304]{2,1,0:T(8,128)(2,1)}), bf16[64,8,2304]{2,1,0:T(8,128)(2,1)S(1)}, u32[]{:S(2)}, u32[]{:S(2)}) async-start(bf16[64,8,2304]{2,1,0:T(8,128)(2,1)} %bitcast.30), calls=%async_computation.1 | async-start | bytes 4718592 | tf_op jit(solution)/shard_map/all_to_all | solution.py:377
  75.4 1.4 copy-start
  76.8 65.5 %all-to-all-start = ((bf16[64,8,2432]{2,1,0:T(8,128)(2,1)}), bf16[64,8,2432]{2,1,0:T(8,128)(2,1)}, u32[]{:S(2)}, u32[]{:S(2)}) async-start(bf16[64,8,2432]{2,1,0:T(8,128)(2,1)} %bitcast.29), calls=%async_computation | async-start | bytes 4980736 | tf_op jit(solution)/shard_map/all_to_all | solution.py:377
  160.2 6.1 %copy-start.1 = (bf16[64,8,2304]{2,1,0:T(8,128)(2,1)S(1)}, bf16[64,8,2304]{2,1,0:T(8,128)(2,1)}, u32[]{:S(2)}) copy-start(bf16[64,8,2304]{2,1,0:T(8,128)(2,1)} %copy-done) | copy-start | bytes 7077892
  160.2 208.3 %all-to-all-start.2 = ((bf16[64,8,2432]{2,1,0:T(8,128)(2,1)}), bf16[64,8,2432]{2,1,0:T(8,128)(2,1)}, u32[]{:S(2)}, u32[]{:S(2)}) async-start(bf16[64,8,2432]{2,1,0:T(8,128)(2,1)} %bitcast.28), calls=%async_computation.2 | async-start | bytes 4980736 | tf_op jit(solution)/shard_map/all_to_all | solution.py:377
  166.3 185.5 %collective-permute-start = (bf16[512,2304]{1,0:T(8,128)(2,1)S(1)}, bf16[512,2304]{1,0:T(8,128)(2,1)}, u32[]{:S(2)}, u32[]{:S(2)}) collective-permute-start(bf16[512,2304]{1,0:T(8,128)(2,1)S(1)} %bitcast.21), channel_id=1, source_target_pairs={{0,64},{64,128},{128,192},{192,0},{1,65},{65,129},{129,193},{193,1... | collective-permute-start | bytes 7077896 | tf_op jit(solution)/shard_map/ppermute | solution.py:384
  167.6 184.2 %collective-permute-start.1 = (bf16[512,2304]{1,0:T(8,128)(2,1)S(1)}, bf16[512,2304]{1,0:T(8,128)(2,1)}, u32[]{:S(2)}, u32[]{:S(2)}) collective-permute-start(bf16[512,2304]{1,0:T(8,128)(2,1)S(1)} %bitcast.22), channel_id=1, source_target_pairs={{0,128},{64,192},{128,0},{192,64},{1,129},{65,193},{129,1},{193,65... | collective-permute-start | bytes 7077896 | tf_op jit(solution)/shard_map/ppermute | solution.py:384
  170.1 181.8 %collective-permute-start.2 = (bf16[512,2304]{1,0:T(8,128)(2,1)S(1)}, bf16[512,2304]{1,0:T(8,128)(2,1)}, u32[]{:S(2)}, u32[]{:S(2)}) collective-permute-start(bf16[512,2304]{1,0:T(8,128)(2,1)S(1)} %bitcast.23), channel_id=1, source_target_pairs={{0,192},{64,0},{128,64},{192,128},{1,193},{65,1},{129,65},{193,129... | collective-permute-start | bytes 7077896 | tf_op jit(solution)/shard_map/ppermute | solution.py:384
  179.3 119.1 %collective-permute-start.6 = (bf16[192,2048]{1,0:T(8,128)(2,1)}, bf16[192,2048]{1,0:T(8,128)(2,1)S(1)}, u32[]{:S(2)}, u32[]{:S(2)}) collective-permute-start(bf16[192,2048]{1,0:T(8,128)(2,1)} %get-tuple-element.38), channel_id=1, source_target_pairs={{0,64},{64,128},{128,192},{192,0},{1,65},{65,129},{129,193},{193,1... | collective-permute-start | bytes 2359304 | tf_op jit(solution)/shard_map/ppermute | solution.py:384
  183.1 113.7 %collective-permute-start.3 = (bf16[576,384]{1,0:T(8,128)(2,1)}, bf16[576,384]{1,0:T(8,128)(2,1)S(1)}, u32[]{:S(2)}, u32[]{:S(2)}) collective-permute-start(bf16[576,384]{1,0:T(8,128)(2,1)} %get-tuple-element.31), channel_id=1, source_target_pairs={{0,64},{64,128},{128,192},{192,0},{1,65},{65,129},{129,193},{193,1... | collective-permute-start | bytes 1327112 | tf_op jit(solution)/shard_map/ppermute | solution.py:384
  296.8 37.3 %copy-start.3 = (bf16[576,384]{1,0:T(8,128)(2,1)}, bf16[576,384]{1,0:T(8,128)(2,1)S(1)}, u32[]{:S(2)}) copy-start(bf16[576,384]{1,0:T(8,128)(2,1)S(1)} %collective-permute-done.3.refs_9_) | copy-start | bytes 1327108
  296.8 19.4 %collective-permute-start.7 = (bf16[192,2048]{1,0:T(8,128)(2,1)}, bf16[192,2048]{1,0:T(8,128)(2,1)S(1)}, u32[]{:S(2)}, u32[]{:S(2)}) collective-permute-start(bf16[192,2048]{1,0:T(8,128)(2,1)} %get-tuple-element.39), channel_id=1, source_target_pairs={{0,128},{64,192},{128,0},{192,64},{1,129},{65,193},{129,1},{193,65... | collective-permute-start | bytes 2359304 | tf_op jit(solution)/shard_map/ppermute | solution.py:384
  298.4 35.7 %collective-permute-start.8 = (bf16[192,2048]{1,0:T(8,128)(2,1)}, bf16[192,2048]{1,0:T(8,128)(2,1)S(1)}, u32[]{:S(2)}, u32[]{:S(2)}) collective-permute-start(bf16[192,2048]{1,0:T(8,128)(2,1)} %get-tuple-element.40), channel_id=1, source_target_pairs={{0,192},{64,0},{128,64},{192,128},{1,193},{65,1},{129,65},{193,129... | collective-permute-start | bytes 2359304 | tf_op jit(solution)/shard_map/ppermute | solution.py:384
  316.3 24.1 %collective-permute-start.4 = (bf16[576,384]{1,0:T(8,128)(2,1)}, bf16[576,384]{1,0:T(8,128)(2,1)S(1)}, u32[]{:S(2)}, u32[]{:S(2)}) collective-permute-start(bf16[576,384]{1,0:T(8,128)(2,1)} %get-tuple-element.32), channel_id=1, source_target_pairs={{0,128},{64,192},{128,0},{192,64},{1,129},{65,193},{129,1},{193,65... | collective-permute-start | bytes 1327112 | tf_op jit(solution)/shard_map/ppermute | solution.py:384
  334.1 17.8 %collective-permute-start.5 = (bf16[576,384]{1,0:T(8,128)(2,1)}, bf16[576,384]{1,0:T(8,128)(2,1)S(1)}, u32[]{:S(2)}, u32[]{:S(2)}) collective-permute-start(bf16[576,384]{1,0:T(8,128)(2,1)} %get-tuple-element.33), channel_id=1, source_target_pairs={{0,192},{64,0},{128,64},{192,128},{1,193},{65,1},{129,65},{193,129... | collective-permute-start | bytes 1327112 | tf_op jit(solution)/shard_map/ppermute | solution.py:384
  340.4 11.5 %copy-start.4 = (bf16[576,384]{1,0:T(8,128)(2,1)}, bf16[576,384]{1,0:T(8,128)(2,1)S(1)}, u32[]{:S(2)}) copy-start(bf16[576,384]{1,0:T(8,128)(2,1)S(1)} %collective-permute-done.4.refs_10_) | copy-start | bytes 1327108
  351.9 0.8 copy-start.5
  365.0 2.3 copy-start.2

commit v2 on v1

v2 whole, which is shorter than its diff:
```python
import jax
import jax.numpy as jnp
from jax import lax
from jax.experimental import pallas as pl
from jax.experimental.pallas import tpu as pltpu
from jax.sharding import PartitionSpec as P


BF = jnp.bfloat16
F32 = jnp.float32
TOP = 4
TOK = 128
EXP = 64
MAIN = 8
ROWS = EXP * MAIN
ALL = ROWS + EXP
D = 2048
H = 768
SEG = D // MAIN
N_DP = 4
HS = H // N_DP
X_COLS = D + SEG
Y_COLS = D + SEG + 128


def dot(a, b):
    return jnp.dot(a, b, preferred_element_type=F32)


def dot_nt(a, b):
    return lax.dot_general(a, b, (((1,), (1,)), ((), ())), preferred_element_type=F32)


def dot_tn(a, b):
    return lax.dot_general(a, b, (((0,), (0,)), ((), ())), preferred_element_type=F32)


def iota(shape, axis):
    return lax.broadcasted_iota(jnp.int32, shape, axis)


def one(mask):
    return jnp.where(mask, 1.0, 0.0)


def slot_masks(ids):
    lane_e = iota((EXP, TOK), 0)
    picks = [ids[k : k + 1, :] == lane_e for k in range(TOP)]
    member = picks[0] | picks[1] | picks[2] | picks[3]
    before = one(iota((TOK, TOK), 0) < iota((TOK, TOK), 1)).astype(BF)
    rank = jnp.where(member, dot(one(member).astype(BF), before), 200.0)
    spread = one((iota((ROWS, EXP), 0) >> 3) == iota((ROWS, EXP), 1)).astype(BF)
    rank_rows = dot(spread, rank.astype(BF))
    return picks, spread, rank_rows


def spare_masks(rank_rows):
    sub = iota((ROWS, TOK), 0) & (MAIN - 1)
    ninth = rank_rows == float(MAIN)
    return [one(ninth & (sub == j)).astype(BF) for j in range(MAIN)]


def main_mask(rank_rows):
    sub = iota((ROWS, TOK), 0) & (MAIN - 1)
    return rank_rows == sub.astype(F32)


def pack_rows(ids_ref, data_ref, out_ref):
    picks, spread, rank_rows = slot_masks(ids_ref[...])
    main = one(main_mask(rank_rows))
    out_ref[:, :D] = dot(main.astype(BF), data_ref[...]).astype(BF)
    spare = jnp.concatenate(spare_masks(rank_rows), axis=1)
    parts = jnp.concatenate([data_ref[:, j * SEG : (j + 1) * SEG] for j in range(MAIN)], axis=0)
    out_ref[:, D : D + SEG] = dot(spare, parts).astype(BF)
    return picks, spread, rank_rows, main


def pack_x_kernel(ids_ref, data_ref, out_ref):
    pack_rows(ids_ref, data_ref, out_ref)


def pack_dy_kernel(ids_ref, data_ref, probs_ref, out_ref):
    picks, spread, rank_rows, main = pack_rows(ids_ref, data_ref, out_ref)
    probs = probs_ref[...].astype(F32)
    chosen = jnp.zeros((EXP, TOK), F32)
    for k in range(TOP):
        chosen = chosen + jnp.where(picks[k], probs[k : k + 1, :], 0.0)
    prob_rows = dot(spread, chosen.astype(BF))
    p_main = jnp.sum(main * prob_rows, axis=1, keepdims=True)
    p_ninth = jnp.sum(jnp.where(rank_rows == float(MAIN), prob_rows, 0.0), axis=1, keepdims=True)
    lane = iota((ROWS, 128), 1)
    out_ref[:, D + SEG :] = jnp.where(
        lane == 0, p_main, jnp.where(lane == 1, p_ninth, 0.0)
    ).astype(BF)


def pack_x(ids, data):
    return pl.pallas_call(
        pack_x_kernel, out_shape=jax.ShapeDtypeStruct((ROWS, X_COLS), BF), name="pack_x"
    )(ids, data)


def pack_dy(ids, data, probs):
    return pl.pallas_call(
        pack_dy_kernel, out_shape=jax.ShapeDtypeStruct((ROWS, Y_COLS), BF), name="pack_dy"
    )(ids, data, probs)


def unfold_mask():
    row = iota((ROWS, ROWS), 0)
    col = iota((ROWS, ROWS), 1)
    return one(col == (row & (EXP - 1)) * MAIN + (row >> 6)).astype(BF)


def fold_mask():
    row = iota((ROWS, ROWS), 0)
    col = iota((ROWS, ROWS), 1)
    return one(col == (row & (MAIN - 1)) * EXP + (row >> 3)).astype(BF)


def fill_rows(recv_ref, rows_ref):
    rows_ref[:ROWS, :] = recv_ref[:, :D]
    spare = dot(unfold_mask(), recv_ref[:, D : D + SEG]).astype(BF)
    for j in range(MAIN):
        rows_ref[ROWS:, j * SEG : (j + 1) * SEG] = spare[j * EXP : (j + 1) * EXP, :]


def forward_kernel(recv_ref, gate_ref, up_ref, slope_ref, silu_ref, act_ref, rows_ref):
    @pl.when(pl.program_id(0) == 0)
    def _():
        fill_rows(recv_ref, rows_ref)

    gate_pre = dot(rows_ref[...], gate_ref[...])
    up_pre = dot(rows_ref[...], up_ref[...])
    sig = jax.nn.sigmoid(gate_pre)
    silu = gate_pre * sig
    silu_ref[...] = silu
    act_ref[...] = silu * up_pre
    slope_ref[...] = up_pre * sig * (1.0 + gate_pre * (1.0 - sig))


def forward(recv_x, gate_mat, up_mat):
    full = pl.BlockSpec((ROWS, X_COLS), lambda j: (0, 0))
    weight = pl.BlockSpec((D, 256), lambda j: (0, j))
    out = pl.BlockSpec((ALL, 256), lambda j: (0, j))
    shape = jax.ShapeDtypeStruct((ALL, H), F32)
    return pl.pallas_call(
        forward_kernel,
        grid=(H // 256,),
        in_specs=[full, weight, weight],
        out_specs=[out, out, out],
        out_shape=[shape, shape, shape],
        scratch_shapes=[pltpu.VMEM((ALL, D), BF)],
        name="forward",
    )(recv_x, gate_mat, up_mat)


H_STEPS = H // 256
D_STEPS = D // 512


def rows_kernel(
    recv_ref, down_ref, slope_ref, silu_ref, act_ref, gate_ref, up_ref,
    grad_ref, prob_out_ref, back_ref, rows_ref, prob_ref, sum_ref, spare_ref,
):
    step = pl.program_id(0)

    @pl.when(step == 0)
    def _():
        fill_rows(recv_ref, rows_ref)
        tail = recv_ref[:, D + SEG :]
        pick = one(iota((EXP, ROWS), 1) == iota((EXP, ROWS), 0) * MAIN).astype(BF)
        prob_ref[:ROWS, :] = tail[:, 0:1].astype(F32)
        prob_ref[ROWS:, :] = dot(pick, tail)[:, 1:2]
        sum_ref[...] = jnp.zeros_like(sum_ref)

    for h in range(H_STEPS):

        @pl.when(step == h)
        def _(h=h):
            grad_hidden = dot_nt(rows_ref[...], down_ref[...])
            sum_ref[...] += jnp.sum(act_ref[...] * grad_hidden, axis=1, keepdims=True)
            scaled = prob_ref[...] * grad_hidden
            grad_ref[0, :, h * 256 : (h + 1) * 256] = (scaled * slope_ref[...]).astype(BF)
            grad_ref[1, :, h * 256 : (h + 1) * 256] = (scaled * silu_ref[...]).astype(BF)

    for q in range(D_STEPS):

        @pl.when(step == H_STEPS + q)
        def _(q=q):
            row = dot_nt(grad_ref[0], gate_ref[...]) + dot_nt(grad_ref[1], up_ref[...])
            row = row.astype(BF)
            back_ref[:, q * 512 : (q + 1) * 512] = row[:ROWS]
            for h in range(2):
                spare_ref[(2 * q + h) * EXP : (2 * q + h + 1) * EXP, :] = row[
                    ROWS:, h * SEG : (h + 1) * SEG
                ]

    @pl.when(step == H_STEPS + D_STEPS - 1)
    def _():
        back_ref[:, D : D + SEG] = dot(fold_mask(), spare_ref[...]).astype(BF)
        total = sum_ref[...]
        high = total.astype(BF)
        low = (total - high.astype(F32)).astype(BF)
        lane = iota((EXP, 128), 1)
        ninth = jnp.where(
            lane == 2,
            high[ROWS:].astype(F32),
            jnp.where(lane == 3, low[ROWS:].astype(F32), 0.0),
        ).astype(BF)
        spread = one((iota((ROWS, EXP), 0) >> 3) == iota((ROWS, EXP), 1)).astype(BF)
        lane_rows = iota((ROWS, 128), 1)
        back_ref[:, D + SEG :] = jnp.where(
            lane_rows == 0,
            high[:ROWS].astype(F32),
            jnp.where(lane_rows == 1, low[:ROWS].astype(F32), dot(spread, ninth)),
        ).astype(BF)
        prob_out_ref[...] = jnp.broadcast_to(prob_ref[...], (ALL, 128))


def rows_pass(recv_dy, down_mat, slope, silu, act, gate_mat, up_mat):
    last_h = H_STEPS - 1
    full = pl.BlockSpec((ROWS, Y_COLS), lambda j: (0, 0))
    block = pl.BlockSpec((ALL, 256), lambda j: (0, jnp.minimum(j, last_h)))
    weight = pl.BlockSpec((512, H), lambda j: (jnp.maximum(j - H_STEPS, 0), 0))
    return pl.pallas_call(
        rows_kernel,
        grid=(H_STEPS + D_STEPS,),
        in_specs=[
            full,
            pl.BlockSpec((256, D), lambda j: (jnp.minimum(j, last_h), 0)),
            block, block, block, weight, weight,
        ],
        out_specs=[
            pl.BlockSpec((2, ALL, H), lambda j: (0, 0, 0)),
            pl.BlockSpec((ALL, 128), lambda j: (0, 0)),
            full,
        ],
        out_shape=[
            jax.ShapeDtypeStruct((2, ALL, H), BF),
            jax.ShapeDtypeStruct((ALL, 128), F32),
            jax.ShapeDtypeStruct((ROWS, Y_COLS), BF),
        ],
        scratch_shapes=[
            pltpu.VMEM((ALL, D), BF),
            pltpu.VMEM((ALL, 1), F32),
            pltpu.VMEM((ALL, 1), F32),
            pltpu.VMEM((ROWS, SEG), BF),
        ],
        name="rows_pass",
    )(recv_dy, down_mat, slope, silu, act, gate_mat, up_mat)


def slices_kernel(own_ref, grad_ref, *out_refs):
    own = own_ref[0]
    for t in range(N_DP):
        piece = jnp.concatenate(
            [grad_ref[0, :, t * HS : (t + 1) * HS], grad_ref[1, :, t * HS : (t + 1) * HS]],
            axis=1,
        )
        for d in range(N_DP):

            @pl.when((own + d) % N_DP == t)
            def _(piece=piece, d=d):
                out_refs[d][...] = piece


def slices(own, grad):
    shape = jax.ShapeDtypeStruct((ALL, 2 * HS), BF)
    vmem = pl.BlockSpec(memory_space=pltpu.VMEM)
    return pl.pallas_call(
        slices_kernel,
        in_specs=[pl.BlockSpec(memory_space=pltpu.SMEM), vmem],
        out_specs=[vmem] * N_DP,
        out_shape=[shape] * N_DP,
        name="slices",
    )(own, grad)


def down_kernel(own_ref, act_ref, recv_ref, prob_ref, *refs):
    out_refs, rows_ref = refs[:N_DP], refs[N_DP]
    own = own_ref[0]
    fill_rows(recv_ref, rows_ref)
    scaled = (prob_ref[:, 0:1] * rows_ref[...].astype(F32)).astype(BF)
    hidden = act_ref[...].astype(BF)
    for t in range(N_DP):
        term = dot_tn(hidden[:, t * HS : (t + 1) * HS], scaled).astype(BF)
        for d in range(N_DP):

            @pl.when((own + d) % N_DP == t)
            def _(term=term, d=d):
                out_refs[d][...] = term


def down_terms(own, act, recv_dy, prob):
    shape = jax.ShapeDtypeStruct((HS, D), BF)
    vmem = pl.BlockSpec(memory_space=pltpu.VMEM)
    return pl.pallas_call(
        down_kernel,
        in_specs=[pl.BlockSpec(memory_space=pltpu.SMEM), vmem, vmem, vmem],
        out_specs=[vmem] * N_DP,
        out_shape=[shape] * N_DP,
        scratch_shapes=[pltpu.VMEM((ALL, D), BF)],
        name="down_terms",
    )(own, act, recv_dy, prob)


HALF = ROWS // 2
X_PARTS = (1, 2, 2, 2)


def gate_up_kernel(*refs):
    n_x = sum(X_PARTS)
    x_refs, spare_refs, g_refs = refs[:n_x], refs[n_x : 2 * n_x], refs[2 * n_x : 2 * n_x + N_DP]
    gate_ref, up_ref, turned_ref = refs[2 * n_x + N_DP :]
    step = pl.program_id(0)

    @pl.when(step == 0)
    def _():
        for g in range(N_DP):
            turned = g_refs[g][...].astype(F32).T.astype(BF)
            turned_ref[:, g * ROWS : (g + 1) * ROWS] = turned[:, :ROWS]
            turned_ref[:, N_DP * ROWS + g * EXP : N_DP * ROWS + (g + 1) * EXP] = turned[:, ROWS:]

    spares = []
    total = jnp.zeros((2 * HS, SEG), F32)
    at = 0
    for x_ref, spare_ref in zip(x_refs, spare_refs):
        n = x_ref.shape[0]
        pick = one(iota((n // MAIN, n), 1) == iota((n // MAIN, n), 0) * MAIN + step).astype(BF)
        spares.append(dot(pick, spare_ref[...]).astype(BF))
        total = total + dot(turned_ref[:, at : at + n], x_ref[...])
        at += n
    total = total + dot(turned_ref[:, at:], jnp.concatenate(spares, axis=0))
    gate_ref[...] = total[:HS].astype(BF)
    up_ref[...] = total[HS:].astype(BF)


def gate_up_terms(xs, gs):
    mains = [pl.BlockSpec((x.shape[0], SEG), lambda j: (0, j)) for x in xs]
    spares = [pl.BlockSpec((x.shape[0], SEG), lambda j: (0, MAIN)) for x in xs]
    grad = pl.BlockSpec((ALL, 2 * HS), lambda j: (0, 0))
    out = pl.BlockSpec((HS, SEG), lambda j: (0, j))
    shape = jax.ShapeDtypeStruct((HS, D), BF)
    return pl.pallas_call(
        gate_up_kernel,
        grid=(MAIN,),
        in_specs=mains + spares + [grad] * N_DP,
        out_specs=[out, out],
        out_shape=[shape, shape],
        scratch_shapes=[pltpu.VMEM((2 * HS, N_DP * ALL), BF)],
        name="gate_up_terms",
    )(*xs, *xs, *gs)


def combine_kernel(ids_ref, recv_ref, rows_ref, probs_ref):
    _, _, rank_rows = slot_masks(ids_ref[...])
    main = one(main_mask(rank_rows))
    total = dot_tn(main.astype(BF), recv_ref[:, :D])
    spare = jnp.concatenate(spare_masks(rank_rows), axis=1)
    extra = dot_tn(spare, recv_ref[:, D : D + SEG])
    for j in range(MAIN):
        rows_ref[:, j * SEG : (j + 1) * SEG] = (
            total[:, j * SEG : (j + 1) * SEG] + extra[j * TOK : (j + 1) * TOK, :]
        ).astype(BF)
    tail = recv_ref[:, D + SEG :].astype(F32)
    v_main = tail[:, 0:1] + tail[:, 1:2]
    v_ninth = tail[:, 2:3] + tail[:, 3:4]
    ninth = one((rank_rows == float(MAIN)) & ((iota((ROWS, TOK), 0) & (MAIN - 1)) == 0))
    values = main * v_main + ninth * v_ninth
    owner = iota((ROWS, TOK), 0) >> 3
    for k in range(TOP):
        hit = ids_ref[k : k + 1, :] == owner
        probs_ref[k : k + 1, :] = jnp.sum(jnp.where(hit, values, 0.0), axis=0, keepdims=True)


def combine(ids, recv):
    return pl.pallas_call(
        combine_kernel,
        out_shape=[
            jax.ShapeDtypeStruct((TOK, D), BF),
            jax.ShapeDtypeStruct((TOP, TOK), F32),
        ],
        name="combine",
    )(ids, recv)


def exchange(flat):
    out = lax.all_to_all(
        flat.reshape(EXP, MAIN, flat.shape[1]), "expert", split_axis=0, concat_axis=0, tiled=True
    )
    return out.reshape(flat.shape)


def shift(value, by):
    return lax.ppermute(value, "dp", [(i, (i + by) % N_DP) for i in range(N_DP)])


def gather_rows(recv):
    top, low = recv[:HALF], recv[HALF:]
    prev_top = shift(top, 1)
    next_low = shift(low, 3)
    prev_low = shift(low, 1)
    next_top = shift(top, 3)
    far_top = shift(prev_top, 1)
    far_low = shift(next_low, 3)
    return [recv, prev_top, prev_low, far_top, far_low, next_top, next_low]


def per_device(tokens, out_grad, gate_probs, expert_ids, w_gate, w_up, w_down):
    own = lax.axis_index("dp").astype(jnp.int32).reshape(1)
    ids = expert_ids.T
    gate_mat, up_mat, down_mat = w_gate[0], w_up[0], w_down[0]
    recv_x = exchange(pack_x(ids, tokens))
    recv_dy = exchange(pack_dy(ids, out_grad, gate_probs.T))
    xs = gather_rows(recv_x)
    slope, silu, act = forward(recv_x, gate_mat, up_mat)
    grad, prob, back = rows_pass(recv_dy, down_mat, slope, silu, act, gate_mat, up_mat)
    back_rows = exchange(back)
    pieces = slices(own, grad)
    gs = [pieces[0]] + [shift(pieces[d], d) for d in range(1, N_DP)]
    terms = down_terms(own, act, recv_dy, prob)
    downs = [terms[0]] + [shift(terms[d], d) for d in range(1, N_DP)]
    gate_grad, up_grad = gate_up_terms(xs, gs)
    down_grad = downs[0].astype(F32)
    for d in range(1, N_DP):
        down_grad = down_grad + downs[d].astype(F32)
    tokens_grad, probs_grad = combine(ids, back_rows)
    return (
        tokens_grad,
        probs_grad.T,
        gate_grad.T[None],
        up_grad.T[None],
        down_grad.astype(BF)[None],
    )


def solution(mesh):
    rows = P(("dp", "expert"), None)
    weights = P("expert", None, None)
    return jax.shard_map(
        per_device,
        mesh=mesh,
        in_specs=(rows, rows, rows, rows, weights, weights, weights),
        out_specs=(rows, rows, P("expert", None, "dp"), P("expert", None, "dp"), P("expert", "dp", None)),
        check_vma=False,
    )
```

time: 373 us -> 325 us (0.87)
  waiting for transfers between devices: 261 us -> 207 us
  starting transfers between devices: 38.4 us -> 47.8 us
    ppermute x9 -> x12, waiting for transfers between devices: 158 us -> 104 us  [shift(): lax.ppermute(value, 'dp', [(i, (i + by) % N_DP) for i in range(N_DP)])]
    ppermute x9 -> x12, starting transfers between devices: 13 us -> 22.4 us  [shift(): lax.ppermute(value, 'dp', [(i, (i + by) % N_DP) for i in range(N_DP)])]
    pallas_call x5 -> x4, Pallas kernels: 37.9 us -> 35.3 us  [the longest x1 15 us: rows_pass(): pl.pallas_call(rows_kernel, grid=(H_STEPS + D_STEPS,), in_specs=[full, pl...]
  transfers between devices with their start and end apart: 12 -> 15, of which waited for: 6 -> 7; matrix products, arithmetic and copies ran while one was open for 2% -> 1% of each run, Pallas kernels for 10% -> 12%
where the time goes in v2:
time: 325 us; the launch traced here: 323 us
  waiting for transfers between devices  207 us (64%)
  Pallas kernels  60.1 us (18%)
  starting transfers between devices  47.8 us (15%)
  local copies, waits for them, and re-layouts  5.11 us (2%)
    ppermute x12, waiting for transfers between devices, shift(): lax.ppermute(value, 'dp', [(i, (i + by) % N_DP) for i in range(N_DP)])  104 us
    all_to_all x3, waiting for transfers between devices, exchange(): lax.all_to_all(flat.reshape(EXP, MAIN, flat.shape[1]), 'expert', split_ax...  103 us
    all_to_all x3, starting transfers between devices, exchange(): lax.all_to_all(flat.reshape(EXP, MAIN, flat.shape[1]), 'expert', split_ax...  25.4 us
    ppermute x12, starting transfers between devices, shift(): lax.ppermute(value, 'dp', [(i, (i + by) % N_DP) for i in range(N_DP)])  22.4 us
    pallas_call x1, Pallas kernels, rows_pass(): pl.pallas_call(rows_kernel, grid=(H_STEPS + D_STEPS,), in_specs=[full, pl...  15 us
    pallas_call x1, Pallas kernels, gate_up_terms(): pl.pallas_call(gate_up_kernel, grid=(MAIN,), in_specs=mains + spares + [g...  12.6 us
    pallas_call x1, Pallas kernels, forward(): pl.pallas_call(forward_kernel, grid=(H // 256,), in_specs=[full, weight,...  9.52 us
    pallas_call x1, Pallas kernels, down_terms(): pl.pallas_call(down_kernel, in_specs=[pl.BlockSpec(memory_space=pltpu.SME...  8.22 us
  transfers between devices with their start and end apart: 15, of which 7 were waited for; matrix products, arithmetic and copies ran while one was open for 1% of the time, Pallas kernels for 12%

profile of v2, /device:TPU:1, one launch (start us, length us, event | category | flops | bytes accessed | tf_op | source)
XLA Modules:
  0.0 322.9 jit_solution(17018374671185143713)
XLA Ops:
  0.6 3.7 %pack_x.1 = bf16[512,2304]{1,0:T(8,128)(2,1)} custom-call(s32[4,128]{1,0:T(4,128)} %bitcast.36, bf16[128,2048]{1,0:T(8,128)(2,1)} %data_ref.3), custom_call_target="tpu_custom_call" | custom-call | tf_op jit(solution)/shard_map/pack_x/pallas_call | solution.py:98
  4.4 13.1 %all-to-all-start.1 = ((bf16[64,8,2304]{2,1,0:T(8,128)(2,1)}), bf16[64,8,2304]{2,1,0:T(8,128)(2,1)S(1)}, u32[]{:S(2)}, u32[]{:S(2)}) async-start(bf16[64,8,2304]{2,1,0:T(8,128)(2,1)} %bitcast.33), calls=%async_computation.1 | async-start | bytes 4718592 | tf_op jit(solution)/shard_map/all_to_all | solution.py:389
  17.5 3.9 %pack_dy.1 = bf16[512,2432]{1,0:T(8,128)(2,1)} custom-call(s32[4,128]{1,0:T(4,128)} %bitcast.37, bf16[128,2048]{1,0:T(8,128)(2,1)} %data_ref.2, bf16[4,128]{1,0:T(4,128)(2,1)} %bitcast.39), custom_call_target="tpu_custom_call" | custom-call | tf_op jit(solution)/shard_map/pack_dy/pallas_call | solution.py:104
  21.4 52.7 %all-to-all-done.1 = bf16[64,8,2304]{2,1,0:T(8,128)(2,1)S(1)} async-done(((bf16[64,8,2304]{2,1,0:T(8,128)(2,1)}), bf16[64,8,2304]{2,1,0:T(8,128)(2,1)S(1)}, u32[]{:S(2)}, u32[]{:S(2)}) %all-to-all-start.1) | async-done | bytes 2359328 | tf_op jit(solution)/shard_map/all_to_all | solution.py:389
  74.1 1.5 copy-done
  75.6 6.1 %all-to-all-start = ((bf16[64,8,2432]{2,1,0:T(8,128)(2,1)}), bf16[64,8,2432]{2,1,0:T(8,128)(2,1)}, u32[]{:S(2)}, u32[]{:S(2)}) async-start(bf16[64,8,2432]{2,1,0:T(8,128)(2,1)} %bitcast.32), calls=%async_computation | async-start | bytes 4980736 | tf_op jit(solution)/shard_map/all_to_all | solution.py:389
  81.7 9.5 %forward.1 = (f32[576,768]{1,0:T(8,128)}, f32[576,768]{1,0:T(8,128)}, f32[576,768]{1,0:T(8,128)}) custom-call(bf16[512,2304]{1,0:T(8,128)(2,1)} %bitcast.25, bf16[2048,768]{1,0:T(8,128)(2,1)} %bitcast.28, bf16[2048,768]{1,0:T(8,128)(2,1)} %bitcast.30), custom_call_target="tpu_custom_call" | custom-call | tf_op jit(solution)/shard_map/forward/pallas_call | solution.py:147
  91.2 49.8 %all-to-all-done = bf16[64,8,2432]{2,1,0:T(8,128)(2,1)} async-done(((bf16[64,8,2432]{2,1,0:T(8,128)(2,1)}), bf16[64,8,2432]{2,1,0:T(8,128)(2,1)}, u32[]{:S(2)}, u32[]{:S(2)}) %all-to-all-start) | async-done | bytes 2490400 | tf_op jit(solution)/shard_map/all_to_all | solution.py:389
  141.1 15.0 %rows_pass.1 = (bf16[2,576,768]{2,1,0:T(8,128)(2,1)}, f32[576,128]{1,0:T(8,128)}, bf16[512,2432]{1,0:T(8,128)(2,1)}) custom-call(bf16[512,2432]{1,0:T(8,128)(2,1)} %bitcast.3.recv_ref, bf16[768,2048]{1,0:T(8,128)(2,1)} %bitcast.34, f32[576,768]{1,0:T(8,128)} %get-tuple-element.23.slope_ref, f32[576,768]{1,0:T(8,128)} %get-tuple-element.24.silu_ref, ...), custom_call_target="tpu_custom_call" | custom-call | tf_op jit(solution)/shard_map/rows_pass/pallas_call | solution.py:226
  156.1 6.1 %all-to-all-start.2 = ((bf16[64,8,2432]{2,1,0:T(8,128)(2,1)}), bf16[64,8,2432]{2,1,0:T(8,128)(2,1)}, u32[]{:S(2)}, u32[]{:S(2)}) async-start(bf16[64,8,2432]{2,1,0:T(8,128)(2,1)} %bitcast.35), calls=%async_computation.2 | async-start | bytes 4980736 | tf_op jit(solution)/shard_map/all_to_all | solution.py:389
  162.2 0.0 copy-done.1
  162.2 1.5 slice_bitcast_fusion
  163.8 1.2 collective-permute-start
  165.0 1.5 collective-permute-start.3
  166.5 3.4 %slices.1 = (bf16[576,384]{1,0:T(8,128)(2,1)}, bf16[576,384]{1,0:T(8,128)(2,1)}, bf16[576,384]{1,0:T(8,128)(2,1)}, bf16[576,384]{1,0:T(8,128)(2,1)}) custom-call(s32[1]{0:T(128)} %bitcast.14.own_ref, bf16[2,576,768]{2,1,0:T(8,128)(2,1)} %get-tuple-element.29.grad_ref), custom_call_target="tpu_custom_call" | custom-call | tf_op jit(solution)/shard_map/slices/pallas_call | solution.py:271
  169.9 0.0 collective-permute-start.6
  169.9 8.2 %down_terms.1 = (bf16[192,2048]{1,0:T(8,128)(2,1)}, bf16[192,2048]{1,0:T(8,128)(2,1)}, bf16[192,2048]{1,0:T(8,128)(2,1)}, bf16[192,2048]{1,0:T(8,128)(2,1)}) custom-call(s32[1]{0:T(128)} %bitcast.14.own_ref, f32[576,768]{1,0:T(8,128)} %get-tuple-element.25.act_ref, bf16[512,2432]{1,0:T(8,128)(2,1)} %bitcast.3.recv_ref, f32[576,128]{1,0:T(8,128)} %get-tuple-element.36.prob_ref), custom_call_target="tpu_custom_call" | custom-call | tf_op jit(solution)/shard_map/down_terms/pallas_call | solution.py:298
  178.1 2.4 collective-permute-start.10
  180.6 1.1 collective-permute-start.11
  181.7 20.1 %collective-permute-done.6.refs_15_ = bf16[576,384]{1,0:T(8,128)(2,1)S(1)} collective-permute-done((bf16[576,384]{1,0:T(8,128)(2,1)}, bf16[576,384]{1,0:T(8,128)(2,1)S(1)}, u32[]{:S(2)}, u32[]{:S(2)}) %collective-permute-start.6) | collective-permute-done | bytes 442400 | tf_op jit(solution)/shard_map/ppermute | solution.py:396
  201.8 1.5 collective-permute-start.7
  203.3 25.7 %collective-permute-done.7.refs_16_ = bf16[576,384]{1,0:T(8,128)(2,1)S(1)} collective-permute-done((bf16[576,384]{1,0:T(8,128)(2,1)}, bf16[576,384]{1,0:T(8,128)(2,1)S(1)}, u32[]{:S(2)}, u32[]{:S(2)}) %collective-permute-start.7) | collective-permute-done | bytes 442400 | tf_op jit(solution)/shard_map/ppermute | solution.py:396
  229.0 8.0 %collective-permute-start.9 = (bf16[192,2048]{1,0:T(8,128)(2,1)}, bf16[192,2048]{1,0:T(8,128)(2,1)S(1)}, u32[]{:S(2)}, u32[]{:S(2)}) collective-permute-start(bf16[192,2048]{1,0:T(8,128)(2,1)} %get-tuple-element.38), channel_id=1, source_target_pairs={{0,64},{64,128},{128,192},{192,0},{1,65},{65,129},{129,193},{193,1... | collective-permute-start | bytes 2359304 | tf_op jit(solution)/shard_map/ppermute | solution.py:396
  237.0 0.0 copy-done.8
  237.0 0.0 copy-done.9
  237.0 0.0 collective-permute-done.10
  237.0 0.8 collective-permute-start.1
  237.8 0.0 collective-permute-done.11
  237.8 2.0 collective-permute-start.5
  239.8 0.0 collective-permute-done.refs_1_.refs_8_
  239.8 0.0 collective-permute-start.2
  239.8 0.0 collective-permute-done.3.refs_6_.refs_13_
  239.8 0.0 copy-start.3
  239.8 2.7 collective-permute-start.4
  242.5 11.5 %collective-permute-done.9 = bf16[192,2048]{1,0:T(8,128)(2,1)S(1)} collective-permute-done((bf16[192,2048]{1,0:T(8,128)(2,1)}, bf16[192,2048]{1,0:T(8,128)(2,1)S(1)}, u32[]{:S(2)}, u32[]{:S(2)}) %collective-permute-start.9) | collective-permute-done | bytes 786464 | tf_op jit(solution)/shard_map/ppermute | solution.py:396
  254.0 1.2 collective-permute-start.8
  255.2 2.5 fusion
  257.7 40.6 %collective-permute-done.8.refs_17_ = bf16[576,384]{1,0:T(8,128)(2,1)S(1)} collective-permute-done((bf16[576,384]{1,0:T(8,128)(2,1)}, bf16[576,384]{1,0:T(8,128)(2,1)S(1)}, u32[]{:S(2)}, u32[]{:S(2)}) %collective-permute-start.8) | collective-permute-done | bytes 442400 | tf_op jit(solution)/shard_map/ppermute | solution.py:396
  298.3 0.0 collective-permute-done.1.refs_2_.refs_9_
  298.3 0.0 collective-permute-done.5.refs_5_.refs_12_
  298.4 0.0 copy-start.5
  298.4 6.2 %collective-permute-done.2.refs_3_.refs_10_ = bf16[256,2304]{1,0:T(8,128)(2,1)S(1)} collective-permute-done((bf16[256,2304]{1,0:T(8,128)(2,1)S(1)}, bf16[256,2304]{1,0:T(8,128)(2,1)S(1)}, u32[]{:S(2)}, u32[]{:S(2)}) %collective-permute-start.2) | collective-permute-done | bytes 1179680 | tf_op jit(solution)/shard_map/ppermute | solution.py:396
  304.6 0.0 collective-permute-done.4.refs_4_.refs_11_
  304.6 1.0 copy-done.6
  305.6 1.1 copy-done.7
  306.7 12.6 %gate_up_terms.1 = (bf16[192,2048]{1,0:T(8,128)(2,1)}, bf16[192,2048]{1,0:T(8,128)(2,1)}) custom-call(bf16[512,2304]{1,0:T(8,128)(2,1)} %bitcast.26, bf16[256,2304]{1,0:T(8,128)(2,1)} %copy-done.2, bf16[256,2304]{1,0:T(8,128)(2,1)} %copy-done.4, bf16[256,2304]{1,0:T(8,128)(2,1)} %copy-done.6, bf16[256,2304]{1,0:T(8,128)(2,1)} %copy-done.7, ...), custom_call_target="tpu_custom_call" | custom-call | tf_op jit(solution)/shard_map/gate_up_terms/pallas_call | solution.py:345
  319.3 0.0 all-to-all-done.2
  319.3 3.6 %combine.1 = (bf16[128,2048]{1,0:T(8,128)(2,1)}, f32[4,128]{1,0:T(4,128)}) custom-call(s32[4,128]{1,0:T(4,128)} %bitcast.38, bf16[512,2432]{1,0:T(8,128)(2,1)} %bitcast.10.recv_ref), custom_call_target="tpu_custom_call" | custom-call | tf_op jit(solution)/shard_map/combine/pallas_call | solution.py:378
  (14 shorter events, 0.0 us)
Async XLA Ops:
  4.4 69.8 %all-to-all-start.1 = ((bf16[64,8,2304]{2,1,0:T(8,128)(2,1)}), bf16[64,8,2304]{2,1,0:T(8,128)(2,1)S(1)}, u32[]{:S(2)}, u32[]{:S(2)}) async-start(bf16[64,8,2304]{2,1,0:T(8,128)(2,1)} %bitcast.33), calls=%async_computation.1 | async-start | bytes 4718592 | tf_op jit(solution)/shard_map/all_to_all | solution.py:389
  74.1 1.5 copy-start
  75.6 65.5 %all-to-all-start = ((bf16[64,8,2432]{2,1,0:T(8,128)(2,1)}), bf16[64,8,2432]{2,1,0:T(8,128)(2,1)}, u32[]{:S(2)}, u32[]{:S(2)}) async-start(bf16[64,8,2432]{2,1,0:T(8,128)(2,1)} %bitcast.32), calls=%async_computation | async-start | bytes 4980736 | tf_op jit(solution)/shard_map/all_to_all | solution.py:389
  156.1 6.1 %copy-start.1 = (bf16[64,8,2304]{2,1,0:T(8,128)(2,1)S(1)}, bf16[64,8,2304]{2,1,0:T(8,128)(2,1)}, u32[]{:S(2)}) copy-start(bf16[64,8,2304]{2,1,0:T(8,128)(2,1)} %copy-done) | copy-start | bytes 7077892
  156.1 163.2 %all-to-all-start.2 = ((bf16[64,8,2432]{2,1,0:T(8,128)(2,1)}), bf16[64,8,2432]{2,1,0:T(8,128)(2,1)}, u32[]{:S(2)}, u32[]{:S(2)}) async-start(bf16[64,8,2432]{2,1,0:T(8,128)(2,1)} %bitcast.35), calls=%async_computation.2 | async-start | bytes 4980736 | tf_op jit(solution)/shard_map/all_to_all | solution.py:389
  163.8 76.0 %collective-permute-start = (bf16[256,2304]{1,0:T(8,128)(2,1)}, bf16[256,2304]{1,0:T(8,128)(2,1)S(1)}, u32[]{:S(2)}, u32[]{:S(2)}) collective-permute-start(bf16[256,2304]{1,0:T(8,128)(2,1)} %get-tuple-element.42), channel_id=1, source_target_pairs={{0,64},{64,128},{128,192},{192,0},{1,65},{65,129},{129,193},{193,1... | collective-permute-start | bytes 3538952 | tf_op jit(solution)/shard_map/ppermute | solution.py:396
  165.0 74.8 %collective-permute-start.3 = (bf16[256,2304]{1,0:T(8,128)(2,1)}, bf16[256,2304]{1,0:T(8,128)(2,1)S(1)}, u32[]{:S(2)}, u32[]{:S(2)}) collective-permute-start(bf16[256,2304]{1,0:T(8,128)(2,1)} %get-tuple-element.41), channel_id=1, source_target_pairs={{0,192},{64,0},{128,64},{192,128},{1,193},{65,1},{129,65},{193,129... | collective-permute-start | bytes 3538952 | tf_op jit(solution)/shard_map/ppermute | solution.py:396
  169.9 31.9 %collective-permute-start.6 = (bf16[576,384]{1,0:T(8,128)(2,1)}, bf16[576,384]{1,0:T(8,128)(2,1)S(1)}, u32[]{:S(2)}, u32[]{:S(2)}) collective-permute-start(bf16[576,384]{1,0:T(8,128)(2,1)} %get-tuple-element.31), channel_id=1, source_target_pairs={{0,64},{64,128},{128,192},{192,0},{1,65},{65,129},{129,193},{193,1... | collective-permute-start | bytes 1327112 | tf_op jit(solution)/shard_map/ppermute | solution.py:396
  178.1 58.9 %collective-permute-start.10 = (bf16[192,2048]{1,0:T(8,128)(2,1)}, bf16[192,2048]{1,0:T(8,128)(2,1)S(1)}, u32[]{:S(2)}, u32[]{:S(2)}) collective-permute-start(bf16[192,2048]{1,0:T(8,128)(2,1)} %get-tuple-element.39), channel_id=1, source_target_pairs={{0,128},{64,192},{128,0},{192,64},{1,129},{65,193},{129,1},{193,65... | collective-permute-start | bytes 2359304 | tf_op jit(solution)/shard_map/ppermute | solution.py:396
  180.6 57.2 %collective-permute-start.11 = (bf16[192,2048]{1,0:T(8,128)(2,1)}, bf16[192,2048]{1,0:T(8,128)(2,1)S(1)}, u32[]{:S(2)}, u32[]{:S(2)}) collective-permute-start(bf16[192,2048]{1,0:T(8,128)(2,1)} %get-tuple-element.40), channel_id=1, source_target_pairs={{0,192},{64,0},{128,64},{192,128},{1,193},{65,1},{129,65},{193,129... | collective-permute-start | bytes 2359304 | tf_op jit(solution)/shard_map/ppermute | solution.py:396
  201.8 35.2 %copy-start.8 = (bf16[576,384]{1,0:T(8,128)(2,1)}, bf16[576,384]{1,0:T(8,128)(2,1)S(1)}, u32[]{:S(2)}) copy-start(bf16[576,384]{1,0:T(8,128)(2,1)S(1)} %collective-permute-done.6.refs_15_) | copy-start | bytes 1327108
  201.8 27.2 %collective-permute-start.7 = (bf16[576,384]{1,0:T(8,128)(2,1)}, bf16[576,384]{1,0:T(8,128)(2,1)S(1)}, u32[]{:S(2)}, u32[]{:S(2)}) collective-permute-start(bf16[576,384]{1,0:T(8,128)(2,1)} %get-tuple-element.32), channel_id=1, source_target_pairs={{0,128},{64,192},{128,0},{192,64},{1,129},{65,193},{129,1},{193,65... | collective-permute-start | bytes 1327112 | tf_op jit(solution)/shard_map/ppermute | solution.py:396
  229.0 8.0 %copy-start.9 = (bf16[576,384]{1,0:T(8,128)(2,1)}, bf16[576,384]{1,0:T(8,128)(2,1)S(1)}, u32[]{:S(2)}) copy-start(bf16[576,384]{1,0:T(8,128)(2,1)S(1)} %collective-permute-done.7.refs_16_) | copy-start | bytes 1327108
  229.0 25.0 %collective-permute-start.9 = (bf16[192,2048]{1,0:T(8,128)(2,1)}, bf16[192,2048]{1,0:T(8,128)(2,1)S(1)}, u32[]{:S(2)}, u32[]{:S(2)}) collective-permute-start(bf16[192,2048]{1,0:T(8,128)(2,1)} %get-tuple-element.38), channel_id=1, source_target_pairs={{0,64},{64,128},{128,192},{192,0},{1,65},{65,129},{129,193},{193,1... | collective-permute-start | bytes 2359304 | tf_op jit(solution)/shard_map/ppermute | solution.py:396
  237.0 61.3 %collective-permute-start.1 = (bf16[256,2304]{1,0:T(8,128)(2,1)}, bf16[256,2304]{1,0:T(8,128)(2,1)S(1)}, u32[]{:S(2)}, u32[]{:S(2)}) collective-permute-start(bf16[256,2304]{1,0:T(8,128)(2,1)} %get-tuple-element.41), channel_id=1, source_target_pairs={{0,64},{64,128},{128,192},{192,0},{1,65},{65,129},{129,193},{193,1... | collective-permute-start | bytes 3538952 | tf_op jit(solution)/shard_map/ppermute | solution.py:396
  237.8 60.6 %collective-permute-start.5 = (bf16[256,2304]{1,0:T(8,128)(2,1)}, bf16[256,2304]{1,0:T(8,128)(2,1)S(1)}, u32[]{:S(2)}, u32[]{:S(2)}) collective-permute-start(bf16[256,2304]{1,0:T(8,128)(2,1)} %get-tuple-element.42), channel_id=1, source_target_pairs={{0,192},{64,0},{128,64},{192,128},{1,193},{65,1},{129,65},{193,129... | collective-permute-start | bytes 3538952 | tf_op jit(solution)/shard_map/ppermute | solution.py:396
  239.8 17.9 %copy-start.2 = (bf16[256,2304]{1,0:T(8,128)(2,1)}, bf16[256,2304]{1,0:T(8,128)(2,1)S(1)}, u32[]{:S(2)}) copy-start(bf16[256,2304]{1,0:T(8,128)(2,1)S(1)} %collective-permute-done.refs_1_.refs_8_) | copy-start | bytes 3538948
  239.8 64.8 %collective-permute-start.2 = (bf16[256,2304]{1,0:T(8,128)(2,1)S(1)}, bf16[256,2304]{1,0:T(8,128)(2,1)S(1)}, u32[]{:S(2)}, u32[]{:S(2)}) collective-permute-start(bf16[256,2304]{1,0:T(8,128)(2,1)S(1)} %collective-permute-done.refs_1_.refs_8_), channel_id=1, source_target_pairs={{0,64},{64,128},{128,192},{192,0},{1,65},{65,129},{129,193},{193,1... | collective-permute-start | bytes 3538952 | tf_op jit(solution)/shard_map/ppermute | solution.py:396
  239.8 17.9 %copy-start.3 = (bf16[256,2304]{1,0:T(8,128)(2,1)}, bf16[256,2304]{1,0:T(8,128)(2,1)S(1)}, u32[]{:S(2)}) copy-start(bf16[256,2304]{1,0:T(8,128)(2,1)S(1)} %collective-permute-done.3.refs_6_.refs_13_) | copy-start | bytes 3538948
  239.8 64.8 %collective-permute-start.4 = (bf16[256,2304]{1,0:T(8,128)(2,1)S(1)}, bf16[256,2304]{1,0:T(8,128)(2,1)S(1)}, u32[]{:S(2)}, u32[]{:S(2)}) collective-permute-start(bf16[256,2304]{1,0:T(8,128)(2,1)S(1)} %collective-permute-done.3.refs_6_.refs_13_), channel_id=1, source_target_pairs={{0,192},{64,0},{128,64},{192,128},{1,193},{65,1},{129,65},{193,129... | collective-permute-start | bytes 3538952 | tf_op jit(solution)/shard_map/ppermute | solution.py:396
  254.0 44.3 %collective-permute-start.8 = (bf16[576,384]{1,0:T(8,128)(2,1)}, bf16[576,384]{1,0:T(8,128)(2,1)S(1)}, u32[]{:S(2)}, u32[]{:S(2)}) collective-permute-start(bf16[576,384]{1,0:T(8,128)(2,1)} %get-tuple-element.33), channel_id=1, source_target_pairs={{0,192},{64,0},{128,64},{192,128},{1,193},{65,1},{129,65},{193,129... | collective-permute-start | bytes 1327112 | tf_op jit(solution)/shard_map/ppermute | solution.py:396
  298.3 6.2 %copy-start.10 = (bf16[576,384]{1,0:T(8,128)(2,1)}, bf16[576,384]{1,0:T(8,128)(2,1)S(1)}, u32[]{:S(2)}) copy-start(bf16[576,384]{1,0:T(8,128)(2,1)S(1)} %collective-permute-done.8.refs_17_) | copy-start | bytes 1327108
  298.3 8.3 %copy-start.4 = (bf16[256,2304]{1,0:T(8,128)(2,1)}, bf16[256,2304]{1,0:T(8,128)(2,1)S(1)}, u32[]{:S(2)}) copy-start(bf16[256,2304]{1,0:T(8,128)(2,1)S(1)} %collective-permute-done.1.refs_2_.refs_9_) | copy-start | bytes 3538948
  298.4 6.2 %copy-start.5 = (bf16[256,2304]{1,0:T(8,128)(2,1)}, bf16[256,2304]{1,0:T(8,128)(2,1)S(1)}, u32[]{:S(2)}) copy-start(bf16[256,2304]{1,0:T(8,128)(2,1)S(1)} %collective-permute-done.5.refs_5_.refs_12_) | copy-start | bytes 3538948
  304.6 1.0 copy-start.6
  305.6 1.1 copy-start.7

commit v3 on v2

v3 whole, which is shorter than its diff:
```python
import jax
import jax.numpy as jnp
from jax import lax
from jax.experimental import pallas as pl
from jax.experimental.pallas import tpu as pltpu
from jax.sharding import PartitionSpec as P


BF = jnp.bfloat16
F32 = jnp.float32
TOP = 4
TOK = 128
EXP = 64
MAIN = 8
ROWS = EXP * MAIN
ALL = ROWS + EXP
D = 2048
H = 768
SEG = D // MAIN
N_DP = 4
HS = H // N_DP
X_COLS = D + SEG
Y_COLS = D + SEG + 128


def dot(a, b):
    return jnp.dot(a, b, preferred_element_type=F32)


def dot_nt(a, b):
    return lax.dot_general(a, b, (((1,), (1,)), ((), ())), preferred_element_type=F32)


def iota(shape, axis):
    return lax.broadcasted_iota(jnp.int32, shape, axis)


def one(mask):
    return jnp.where(mask, 1.0, 0.0)


PACK_STEPS = 2
PACK = ROWS // PACK_STEPS


def pack_rows(ids_ref, data_ref, out_ref, rank_ref, probs_ref=None, chosen_ref=None):
    step = pl.program_id(0)

    @pl.when(step == 0)
    def _():
        ids = ids_ref[...]
        lane_e = iota((EXP, TOK), 0)
        picks = [ids[k : k + 1, :] == lane_e for k in range(TOP)]
        member = picks[0] | picks[1] | picks[2] | picks[3]
        before = one(iota((TOK, TOK), 0) < iota((TOK, TOK), 1)).astype(BF)
        rank_ref[...] = jnp.where(member, dot(one(member).astype(BF), before), 200.0).astype(BF)
        if probs_ref is not None:
            probs = probs_ref[...].astype(F32)
            chosen = jnp.zeros((EXP, TOK), F32)
            for k in range(TOP):
                chosen = chosen + jnp.where(picks[k], probs[k : k + 1, :], 0.0)
            chosen_ref[...] = chosen.astype(BF)

    expert = (iota((PACK, EXP), 0) >> 3) + step * (PACK // MAIN)
    spread = one(expert == iota((PACK, EXP), 1)).astype(BF)
    rank_rows = dot(spread, rank_ref[...])
    sub = iota((PACK, TOK), 0) & (MAIN - 1)
    main = rank_rows == sub.astype(F32)
    ninth = rank_rows == float(MAIN)
    spare = jnp.concatenate([one(ninth & (sub == j)).astype(BF) for j in range(MAIN)], axis=1)
    parts = jnp.concatenate([data_ref[:, j * SEG : (j + 1) * SEG] for j in range(MAIN)], axis=0)
    rows = dot(one(main).astype(BF), data_ref[...])
    extra = dot(spare, parts)
    if probs_ref is not None:
        prob_rows = dot(spread, chosen_ref[...])
        rows = rows * jnp.sum(jnp.where(main, prob_rows, 0.0), axis=1, keepdims=True)
        extra = extra * jnp.sum(jnp.where(ninth, prob_rows, 0.0), axis=1, keepdims=True)
    out_ref[:, :D] = rows.astype(BF)
    out_ref[:, D:] = extra.astype(BF)


def pack_x_kernel(ids_ref, data_ref, out_ref, rank_ref):
    pack_rows(ids_ref, data_ref, out_ref, rank_ref)


def pack_dy_kernel(ids_ref, data_ref, probs_ref, out_ref, rank_ref, chosen_ref):
    pack_rows(ids_ref, data_ref, out_ref, rank_ref, probs_ref, chosen_ref)


def pack(kernel, *args):
    return pl.pallas_call(
        kernel,
        grid=(PACK_STEPS,),
        in_specs=[pl.BlockSpec(x.shape, lambda j: (0, 0)) for x in args],
        out_specs=pl.BlockSpec((PACK, X_COLS), lambda j: (j, 0)),
        out_shape=jax.ShapeDtypeStruct((ROWS, X_COLS), BF),
        scratch_shapes=[pltpu.VMEM((EXP, TOK), BF)] * (len(args) - 1),
    )(*args)


def unfold_mask():
    row = iota((ROWS, ROWS), 0)
    col = iota((ROWS, ROWS), 1)
    return one(col == (row & (EXP - 1)) * MAIN + (row >> 6)).astype(BF)


def fold_mask():
    row = iota((ROWS, ROWS), 0)
    col = iota((ROWS, ROWS), 1)
    return one(col == (row & (MAIN - 1)) * EXP + (row >> 3)).astype(BF)


def fill_rows(recv_ref, rows_ref):
    rows_ref[:ROWS, :] = recv_ref[:, :D]
    spare = dot(unfold_mask(), recv_ref[:, D : D + SEG]).astype(BF)
    for j in range(MAIN):
        rows_ref[ROWS:, j * SEG : (j + 1) * SEG] = spare[j * EXP : (j + 1) * EXP, :]


def forward_kernel(
    recv_ref, gate_ref, up_ref, slope_ref, silu_ref, act_ref, turned_ref, rows_ref
):
    @pl.when(pl.program_id(0) == 0)
    def _():
        fill_rows(recv_ref, rows_ref)

    gate_pre = dot(rows_ref[...], gate_ref[...])
    up_pre = dot(rows_ref[...], up_ref[...])
    sig = jax.nn.sigmoid(gate_pre)
    silu = gate_pre * sig
    silu_ref[...] = silu
    act = silu * up_pre
    act_ref[...] = act
    turned_ref[...] = act.T.astype(BF)
    slope_ref[...] = up_pre * sig * (1.0 + gate_pre * (1.0 - sig))


def forward(recv_x, gate_mat, up_mat):
    full = pl.BlockSpec((ROWS, X_COLS), lambda j: (0, 0))
    weight = pl.BlockSpec((D, 256), lambda j: (0, j))
    out = pl.BlockSpec((ALL, 256), lambda j: (0, j))
    shape = jax.ShapeDtypeStruct((ALL, H), F32)
    return pl.pallas_call(
        forward_kernel,
        grid=(H // 256,),
        in_specs=[full, weight, weight],
        out_specs=[out, out, out, pl.BlockSpec((256, ALL), lambda j: (j, 0))],
        out_shape=[shape, shape, shape, jax.ShapeDtypeStruct((H, ALL), BF)],
        scratch_shapes=[pltpu.VMEM((ALL, D), BF)],
        name="forward",
    )(recv_x, gate_mat, up_mat)


def fill_spare(rows_ref, spare_ref):
    spare = dot(unfold_mask(), spare_ref[...]).astype(BF)
    for j in range(MAIN):
        rows_ref[ROWS:, j * SEG : (j + 1) * SEG] = spare[j * EXP : (j + 1) * EXP, :]


def start(source, target, sem):
    copy = pltpu.make_async_copy(source, target, sem)
    copy.start()
    return copy


def cols(ref, first, count):
    return ref.at[:, pl.ds(first, count)]


def rows_kernel(
    own_ref, recv_ref, down_ref, slope_ref, silu_ref, act_ref, gate_ref, up_ref,
    back_ref, piece0_ref, piece1_ref, piece2_ref, piece3_ref,
    rows_v, extra_v, down_v, slope_v, silu_v, act_v, weight_v, grad_v, piece_v, back_v, spare_v,
    sem_in, sem_out,
):
    pieces = [piece0_ref, piece1_ref, piece2_ref, piece3_ref]
    first = [
        start(cols(recv_ref, 0, D), rows_v.at[pl.ds(0, ROWS)], sem_in.at[0]),
        start(cols(recv_ref, D, SEG), extra_v, sem_in.at[1]),
    ]
    down_in = start(down_ref, down_v, sem_in.at[2])
    terms_in = [
        start(act_ref, act_v, sem_in.at[3]),
        start(slope_ref, slope_v, sem_in.at[4]),
        start(silu_ref, silu_v, sem_in.at[5]),
    ]
    for copy in first:
        copy.wait()
    weights_in = [
        start(gate_ref, cols(weight_v, 0, H), sem_in.at[6]),
        start(up_ref, cols(weight_v, H, H), sem_in.at[7]),
    ]
    fill_spare(rows_v, extra_v)
    down_in.wait()
    grad_hidden = dot_nt(rows_v[...], down_v[...])
    for copy in terms_in:
        copy.wait()
    total = jnp.sum(act_v[...] * grad_hidden, axis=1, keepdims=True)
    grad_v[:, :H] = (grad_hidden * slope_v[...]).astype(BF)
    grad_v[:, H:] = (grad_hidden * silu_v[...]).astype(BF)
    for copy in weights_in:
        copy.wait()
    outs = []
    own = own_ref[0]
    for q in range(2):
        n = D // 2
        row = dot_nt(grad_v[...], weight_v[q * n : (q + 1) * n, :]).astype(BF)
        back_v[:, q * n : (q + 1) * n] = row[:ROWS]
        for j in range(MAIN // 2):
            at = (q * (MAIN // 2) + j) * EXP
            spare_v[at : at + EXP, :] = row[ROWS:, j * SEG : (j + 1) * SEG]
        outs.append(start(cols(back_v, q * n, n), cols(back_ref, q * n, n), sem_out.at[q]))
        if q == 0:
            for t in range(N_DP):
                piece_v[t, :, :HS] = grad_v[:, t * HS : (t + 1) * HS]
                piece_v[t, :, HS:] = grad_v[:, H + t * HS : H + (t + 1) * HS]
            for d in range(N_DP):
                t = lax.rem(own + d, N_DP)
                outs.append(start(piece_v.at[t], pieces[d], sem_out.at[2 + d]))
    back_v[:, D : D + SEG] = dot(fold_mask(), spare_v[...]).astype(BF)
    high = total.astype(BF)
    low = (total - high.astype(F32)).astype(BF)
    lane = iota((EXP, 128), 1)
    ninth = jnp.where(
        lane == 2,
        high[ROWS:].astype(F32),
        jnp.where(lane == 3, low[ROWS:].astype(F32), 0.0),
    ).astype(BF)
    spread = one((iota((ROWS, EXP), 0) >> 3) == iota((ROWS, EXP), 1)).astype(BF)
    lane_rows = iota((ROWS, 128), 1)
    back_v[:, D + SEG :] = jnp.where(
        lane_rows == 0,
        high[:ROWS].astype(F32),
        jnp.where(lane_rows == 1, low[:ROWS].astype(F32), dot(spread, ninth)),
    ).astype(BF)
    outs.append(start(cols(back_v, D, SEG + 128), cols(back_ref, D, SEG + 128), sem_out.at[6]))
    for copy in outs:
        copy.wait()


def rows_pass(own, recv_dy, down_mat, slope, silu, act, gate_mat, up_mat):
    hbm = pl.BlockSpec(memory_space=pltpu.HBM)
    piece = jax.ShapeDtypeStruct((ALL, 2 * HS), BF)
    return pl.pallas_call(
        rows_kernel,
        in_specs=[pl.BlockSpec(memory_space=pltpu.SMEM)] + [hbm] * 7,
        out_specs=[hbm] * (1 + N_DP),
        out_shape=[jax.ShapeDtypeStruct((ROWS, Y_COLS), BF)] + [piece] * N_DP,
        scratch_shapes=[
            pltpu.VMEM((ALL, D), BF),
            pltpu.VMEM((ROWS, SEG), BF),
            pltpu.VMEM((H, D), BF),
            pltpu.VMEM((ALL, H), F32),
            pltpu.VMEM((ALL, H), F32),
            pltpu.VMEM((ALL, H), F32),
            pltpu.VMEM((D, 2 * H), BF),
            pltpu.VMEM((ALL, 2 * H), BF),
            pltpu.VMEM((N_DP, ALL, 2 * HS), BF),
            pltpu.VMEM((ROWS, Y_COLS), BF),
            pltpu.VMEM((ROWS, SEG), BF),
            pltpu.SemaphoreType.DMA((8,)),
            pltpu.SemaphoreType.DMA((7,)),
        ],
        name="rows_pass",
    )(own, recv_dy, down_mat, slope, silu, act, gate_mat, up_mat)


def down_kernel(
    own_ref, turned_ref, recv_ref, out0_ref, out1_ref, out2_ref, out3_ref,
    rows_v, extra_v, turned_v, out_v, sem_in, sem_out,
):
    outs_ref = [out0_ref, out1_ref, out2_ref, out3_ref]
    ins = [
        start(cols(recv_ref, D, SEG), extra_v, sem_in.at[1]),
        start(cols(recv_ref, 0, D), rows_v.at[pl.ds(0, ROWS)], sem_in.at[0]),
        start(turned_ref, turned_v, sem_in.at[2]),
    ]
    ins[0].wait()
    fill_spare(rows_v, extra_v)
    ins[1].wait()
    ins[2].wait()
    outs = []
    for n in range(N_DP):
        d = (n + 1) % N_DP
        at = pl.multiple_of(lax.rem(own_ref[0] + d, N_DP) * HS, HS)
        out_v[d] = dot(turned_v[pl.ds(at, HS), :], rows_v[...]).astype(BF)
        outs.append(start(out_v.at[d], outs_ref[d], sem_out.at[d]))
    for copy in outs:
        copy.wait()


def down_terms(own, turned, recv_dy):
    hbm = pl.BlockSpec(memory_space=pltpu.HBM)
    return pl.pallas_call(
        down_kernel,
        in_specs=[pl.BlockSpec(memory_space=pltpu.SMEM), hbm, hbm],
        out_specs=[hbm] * N_DP,
        out_shape=[jax.ShapeDtypeStruct((HS, D), BF)] * N_DP,
        scratch_shapes=[
            pltpu.VMEM((ALL, D), BF),
            pltpu.VMEM((ROWS, SEG), BF),
            pltpu.VMEM((H, ALL), BF),
            pltpu.VMEM((N_DP, HS, D), BF),
            pltpu.SemaphoreType.DMA((3,)),
            pltpu.SemaphoreType.DMA((N_DP,)),
        ],
        name="down_terms",
    )(own, turned, recv_dy)


HALF = ROWS // 2
X_PARTS = (1, 2, 2, 2)


def gate_up_kernel(*refs):
    n_x = sum(X_PARTS)
    x_refs, spare_refs, g_refs = refs[:n_x], refs[n_x : 2 * n_x], refs[2 * n_x : 2 * n_x + N_DP]
    gate_ref, up_ref, turned_ref = refs[2 * n_x + N_DP :]
    step = pl.program_id(0)

    @pl.when(step == 0)
    def _():
        for g in range(N_DP):
            turned = g_refs[g][...].astype(F32).T.astype(BF)
            turned_ref[:, g * ROWS : (g + 1) * ROWS] = turned[:, :ROWS]
            turned_ref[:, N_DP * ROWS + g * EXP : N_DP * ROWS + (g + 1) * EXP] = turned[:, ROWS:]

    spares = []
    total = jnp.zeros((2 * HS, SEG), F32)
    at = 0
    for x_ref, spare_ref in zip(x_refs, spare_refs):
        n = x_ref.shape[0]
        pick = one(iota((n // MAIN, n), 1) == iota((n // MAIN, n), 0) * MAIN + step).astype(BF)
        spares.append(dot(pick, spare_ref[...]).astype(BF))
        total = total + dot(turned_ref[:, at : at + n], x_ref[...])
        at += n
    total = total + dot(turned_ref[:, at:], jnp.concatenate(spares, axis=0))
    gate_ref[...] = total[:HS].astype(BF)
    up_ref[...] = total[HS:].astype(BF)


def gate_up_terms(xs, gs):
    mains = [pl.BlockSpec((x.shape[0], SEG), lambda j: (0, j)) for x in xs]
    spares = [pl.BlockSpec((x.shape[0], SEG), lambda j: (0, MAIN)) for x in xs]
    grad = pl.BlockSpec((ALL, 2 * HS), lambda j: (0, 0))
    out = pl.BlockSpec((HS, SEG), lambda j: (0, j))
    shape = jax.ShapeDtypeStruct((HS, D), BF)
    return pl.pallas_call(
        gate_up_kernel,
        grid=(MAIN,),
        in_specs=mains + spares + [grad] * N_DP,
        out_specs=[out, out],
        out_shape=[shape, shape],
        scratch_shapes=[pltpu.VMEM((2 * HS, N_DP * ALL), BF)],
        name="gate_up_terms",
    )(*xs, *xs, *gs)


def combine_kernel(ids_ref, probs_ref, recv_ref, rows_ref, probs_grad_ref, recv_v, sem):
    halves = [
        start(recv_ref.at[pl.ds(h * HALF, HALF)], recv_v.at[pl.ds(h * HALF, HALF)], sem.at[h])
        for h in range(2)
    ]
    ids = jnp.concatenate(
        [ids_ref[...].astype(F32), jnp.zeros((8 - TOP, TOK), F32)], axis=0
    ).T.astype(jnp.int32)
    lane_e = iota((TOK, EXP), 1)
    member = ids[:, 0:1] == lane_e
    for k in range(1, TOP):
        member = member | (ids[:, k : k + 1] == lane_e)
    before = one(iota((TOK, TOK), 1) < iota((TOK, TOK), 0)).astype(BF)
    rank = jnp.where(member, dot(before, one(member).astype(BF)), 200.0)
    slot = iota((TOK, ROWS), 1)
    spread = one(iota((EXP, ROWS), 0) == (iota((EXP, ROWS), 1) >> 3)).astype(BF)
    rank_slots = dot(rank.astype(BF), spread)
    sub = slot & (MAIN - 1)
    main = rank_slots == sub.astype(F32)
    ninth = rank_slots == float(MAIN)
    main_bf = one(main).astype(BF)
    spare = jnp.concatenate([one(ninth & (sub == j)).astype(BF) for j in range(MAIN)], axis=0)
    for copy in halves:
        copy.wait()
    extra = dot(spare, recv_v[:, D : D + SEG])
    for j in range(MAIN):
        at = slice(j * SEG, (j + 1) * SEG)
        part = dot(main_bf, recv_v[:, at])
        rows_ref[:, at] = (part + extra[j * TOK : (j + 1) * TOK, :]).astype(BF)
    lanes = one(iota((8, 128), 0) == iota((8, 128), 1)).astype(BF)
    values = dot_nt(lanes, recv_v[:, D + SEG :])
    per_slot = jnp.where(main, values[0:1] + values[1:2], 0.0)
    per_slot = per_slot + jnp.where(ninth & (sub == 0), values[2:3] + values[3:4], 0.0)
    lane_k = iota((TOK, 8), 1)
    found = jnp.zeros((TOK, 8), F32)
    for k in range(TOP):
        hit = ids[:, k : k + 1] == (slot >> 3)
        value = jnp.sum(jnp.where(hit, per_slot, 0.0), axis=1, keepdims=True)
        found = jnp.where(lane_k == k, value, found)
    probs_grad_ref[...] = found.T[:TOP] / probs_ref[...].astype(F32)


def combine(ids, probs, recv):
    vmem = pl.BlockSpec(memory_space=pltpu.VMEM)
    return pl.pallas_call(
        combine_kernel,
        in_specs=[vmem, vmem, pl.BlockSpec(memory_space=pltpu.HBM)],
        out_specs=[vmem, vmem],
        out_shape=[
            jax.ShapeDtypeStruct((TOK, D), BF),
            jax.ShapeDtypeStruct((TOP, TOK), F32),
        ],
        scratch_shapes=[pltpu.VMEM((ROWS, Y_COLS), BF), pltpu.SemaphoreType.DMA((2,))],
        name="combine",
    )(ids, probs, recv)


def exchange(flat):
    out = lax.all_to_all(
        flat.reshape(EXP, MAIN, flat.shape[1]), "expert", split_axis=0, concat_axis=0, tiled=True
    )
    return out.reshape(flat.shape)


def shift(value, by):
    return lax.ppermute(value, "dp", [(i, (i + by) % N_DP) for i in range(N_DP)])


def gather_rows(recv):
    top, low = recv[:HALF], recv[HALF:]
    prev_top = shift(top, 1)
    next_low = shift(low, 3)
    prev_low = shift(low, 1)
    next_top = shift(top, 3)
    far_top = shift(prev_top, 1)
    far_low = shift(next_low, 3)
    return [recv, prev_top, prev_low, far_top, far_low, next_top, next_low]


def per_device(tokens, out_grad, gate_probs, expert_ids, w_gate, w_up, w_down):
    own = lax.axis_index("dp").astype(jnp.int32).reshape(1)
    ids = expert_ids.T
    gate_mat, up_mat, down_mat = w_gate[0], w_up[0], w_down[0]
    recv_x = exchange(pack(pack_x_kernel, ids, tokens))
    probs = gate_probs.T
    recv_dy = exchange(pack(pack_dy_kernel, ids, out_grad, probs))
    xs = gather_rows(recv_x)
    slope, silu, act, turned = forward(recv_x, gate_mat, up_mat)
    back, *pieces = rows_pass(own, recv_dy, down_mat, slope, silu, act, gate_mat, up_mat)
    back_rows = exchange(back)
    gs = [pieces[0]] + [shift(pieces[d], d) for d in range(1, N_DP)]
    terms = down_terms(own, turned, recv_dy)
    downs = [terms[0]] + [shift(terms[d], d) for d in range(1, N_DP)]
    gate_grad, up_grad = gate_up_terms(xs, gs)
    down_grad = downs[0].astype(F32)
    for d in range(1, N_DP):
        down_grad = down_grad + downs[d].astype(F32)
    tokens_grad, probs_grad = combine(ids, probs, back_rows)
    return (
        tokens_grad,
        probs_grad.T,
        gate_grad.T[None],
        up_grad.T[None],
        down_grad.astype(BF)[None],
    )


def solution(mesh):
    rows = P(("dp", "expert"), None)
    weights = P("expert", None, None)
    return jax.shard_map(
        per_device,
        mesh=mesh,
        in_specs=(rows, rows, rows, rows, weights, weights, weights),
        out_specs=(rows, rows, P("expert", None, "dp"), P("expert", None, "dp"), P("expert", "dp", None)),
        check_vma=False,
    )
```

time: 325 us -> 320 us (0.985)
  Pallas kernels: 60.1 us -> 52 us
  waiting for transfers between devices: 207 us -> 211 us
    ppermute x12, waiting for transfers between devices: 104 us -> 111 us  [shift(): lax.ppermute(value, 'dp', [(i, (i + by) % N_DP) for i in range(N_DP)])]
    pallas_call x5 -> x4, Pallas kernels: 29.7 us -> 24.3 us  [the longest x1 12.8 us: rows_pass(): pl.pallas_call(rows_kernel, in_specs=[pl.BlockSpec(memory_space=pltpu.SME...]
  transfers between devices with their start and end apart: 15 -> 15, of which waited for: 7 -> 7; matrix products, arithmetic and copies ran while one was open for 1% -> 1% of each run, Pallas kernels for 12% -> 10%
where the time goes in v3:
time: 320 us; the launch traced here: 318 us
  waiting for transfers between devices  211 us (66%)
  Pallas kernels  52 us (16%)
  starting transfers between devices  47.3 us (15%)
  local copies, waits for them, and re-layouts  5.04 us (2%)
    ppermute x12, waiting for transfers between devices, shift(): lax.ppermute(value, 'dp', [(i, (i + by) % N_DP) for i in range(N_DP)])  111 us
    all_to_all x3, waiting for transfers between devices, exchange(): lax.all_to_all(flat.reshape(EXP, MAIN, flat.shape[1]), 'expert', split_ax...  99.8 us
    all_to_all x3, starting transfers between devices, exchange(): lax.all_to_all(flat.reshape(EXP, MAIN, flat.shape[1]), 'expert', split_ax...  25.5 us
    ppermute x12, starting transfers between devices, shift(): lax.ppermute(value, 'dp', [(i, (i + by) % N_DP) for i in range(N_DP)])  21.8 us
    pallas_call x1, Pallas kernels, rows_pass(): pl.pallas_call(rows_kernel, in_specs=[pl.BlockSpec(memory_space=pltpu.SME...  12.8 us
    pallas_call x1, Pallas kernels, gate_up_terms(): pl.pallas_call(gate_up_kernel, grid=(MAIN,), in_specs=mains + spares + [g...  12.6 us
    pallas_call x1, Pallas kernels, forward(): pl.pallas_call(forward_kernel, grid=(H // 256,), in_specs=[full, weight,...  9.39 us
    pallas_call x2, Pallas kernels, pack(): pl.pallas_call(kernel, grid=(PACK_STEPS,), in_specs=[pl.BlockSpec(x.shape...  7.54 us
  transfers between devices with their start and end apart: 15, of which 7 were waited for; matrix products, arithmetic and copies ran while one was open for 1% of the time, Pallas kernels for 10%

profile of v3, /device:TPU:1, one launch (start us, length us, event | category | flops | bytes accessed | tf_op | source)
XLA Modules:
  0.0 318.4 jit_solution(2877859924163729550)
XLA Ops:
  0.6 3.6 %shard_map.111 = bf16[512,2304]{1,0:T(8,128)(2,1)} custom-call(s32[4,128]{1,0:T(4,128)} %bitcast.36, bf16[128,2048]{1,0:T(8,128)(2,1)} %data_ref.3), custom_call_target="tpu_custom_call" | custom-call | tf_op jit(solution)/shard_map/pallas_call | solution.py:91
  4.2 13.1 %all-to-all-start.1 = ((bf16[64,8,2304]{2,1,0:T(8,128)(2,1)}), bf16[64,8,2304]{2,1,0:T(8,128)(2,1)S(1)}, u32[]{:S(2)}, u32[]{:S(2)}) async-start(bf16[64,8,2304]{2,1,0:T(8,128)(2,1)} %bitcast.33), calls=%async_computation.1 | async-start | bytes 4718592 | tf_op jit(solution)/shard_map/all_to_all | solution.py:417
  17.4 3.9 %shard_map.110 = bf16[512,2304]{1,0:T(8,128)(2,1)} custom-call(s32[4,128]{1,0:T(4,128)} %bitcast.37, bf16[128,2048]{1,0:T(8,128)(2,1)} %data_ref.2, bf16[4,128]{1,0:T(4,128)(2,1)} %bitcast.39), custom_call_target="tpu_custom_call" | custom-call | tf_op jit(solution)/shard_map/pallas_call | solution.py:91
  21.3 52.7 %all-to-all-done.1 = bf16[64,8,2304]{2,1,0:T(8,128)(2,1)S(1)} async-done(((bf16[64,8,2304]{2,1,0:T(8,128)(2,1)}), bf16[64,8,2304]{2,1,0:T(8,128)(2,1)S(1)}, u32[]{:S(2)}, u32[]{:S(2)}) %all-to-all-start.1) | async-done | bytes 2359328 | tf_op jit(solution)/shard_map/all_to_all | solution.py:417
  74.0 1.4 copy-done
  75.4 6.1 %all-to-all-start = ((bf16[64,8,2304]{2,1,0:T(8,128)(2,1)}), bf16[64,8,2304]{2,1,0:T(8,128)(2,1)}, u32[]{:S(2)}, u32[]{:S(2)}) async-start(bf16[64,8,2304]{2,1,0:T(8,128)(2,1)} %bitcast.32), calls=%async_computation | async-start | bytes 4718592 | tf_op jit(solution)/shard_map/all_to_all | solution.py:417
  81.5 9.4 %forward.1 = (f32[576,768]{1,0:T(8,128)}, f32[576,768]{1,0:T(8,128)}, f32[576,768]{1,0:T(8,128)}, bf16[768,576]{1,0:T(8,128)(2,1)}) custom-call(bf16[512,2304]{1,0:T(8,128)(2,1)} %bitcast.25, bf16[2048,768]{1,0:T(8,128)(2,1)} %bitcast.28, bf16[2048,768]{1,0:T(8,128)(2,1)} %bitcast.30), custom_call_target="tpu_custom_call" | custom-call | tf_op jit(solution)/shard_map/forward/pallas_call | solution.py:143
  90.9 47.2 %all-to-all-done = bf16[64,8,2304]{2,1,0:T(8,128)(2,1)} async-done(((bf16[64,8,2304]{2,1,0:T(8,128)(2,1)}), bf16[64,8,2304]{2,1,0:T(8,128)(2,1)}, u32[]{:S(2)}, u32[]{:S(2)}) %all-to-all-start) | async-done | bytes 2359328 | tf_op jit(solution)/shard_map/all_to_all | solution.py:417
  138.1 12.8 %rows_pass.1 = (bf16[512,2432]{1,0:T(8,128)(2,1)}, bf16[576,384]{1,0:T(8,128)(2,1)}, bf16[576,384]{1,0:T(8,128)(2,1)}, bf16[576,384]{1,0:T(8,128)(2,1)}, bf16[576,384]{1,0:T(8,128)(2,1)}) custom-call(s32[1]{0:T(128)} %bitcast.2.own_ref, bf16[512,2304]{1,0:T(8,128)(2,1)} %bitcast.4.recv_ref, bf16[768,2048]{1,0:T(8,128)(2,1)} %bitcast.34, ...), custom_call_target="tpu_custom_call" | custom-call | tf_op jit(solution)/shard_map/rows_pass/pallas_call | solution.py:244
  150.9 0.0 copy-start.1
  150.9 6.3 %all-to-all-start.2 = ((bf16[64,8,2432]{2,1,0:T(8,128)(2,1)}), bf16[64,8,2432]{2,1,0:T(8,128)(2,1)}, u32[]{:S(2)}, u32[]{:S(2)}) async-start(bf16[64,8,2432]{2,1,0:T(8,128)(2,1)} %bitcast.35), calls=%async_computation.2 | async-start | bytes 4980736 | tf_op jit(solution)/shard_map/all_to_all | solution.py:417
  157.2 0.0 copy-done.1
  157.2 1.5 slice_bitcast_fusion
  158.7 1.2 collective-permute-start
  159.9 1.5 collective-permute-start.3
  161.4 0.0 collective-permute-start.6
  161.4 5.7 %down_terms.1 = (bf16[192,2048]{1,0:T(8,128)(2,1)}, bf16[192,2048]{1,0:T(8,128)(2,1)}, bf16[192,2048]{1,0:T(8,128)(2,1)}, bf16[192,2048]{1,0:T(8,128)(2,1)}) custom-call(s32[1]{0:T(128)} %bitcast.2.own_ref, bf16[768,576]{1,0:T(8,128)(2,1)} %get-tuple-element.34.turned_ref, bf16[512,2304]{1,0:T(8,128)(2,1)} %bitcast.4.recv_ref), custom_call_target="tpu_custom_call" | custom-call | tf_op jit(solution)/shard_map/down_terms/pallas_call | solution.py:294
  167.1 2.7 collective-permute-start.11
  169.8 0.3 collective-permute-start.10
  170.2 26.6 %collective-permute-done.6.refs_15_ = bf16[576,384]{1,0:T(8,128)(2,1)S(1)} collective-permute-done((bf16[576,384]{1,0:T(8,128)(2,1)}, bf16[576,384]{1,0:T(8,128)(2,1)S(1)}, u32[]{:S(2)}, u32[]{:S(2)}) %collective-permute-start.6) | collective-permute-done | bytes 442400 | tf_op jit(solution)/shard_map/ppermute | solution.py:424
  196.7 0.0 copy-done.11
  196.7 1.5 collective-permute-start.7
  198.3 25.7 %collective-permute-done.7.refs_16_ = bf16[576,384]{1,0:T(8,128)(2,1)S(1)} collective-permute-done((bf16[576,384]{1,0:T(8,128)(2,1)S(1)}, bf16[576,384]{1,0:T(8,128)(2,1)S(1)}, u32[]{:S(2)}, u32[]{:S(2)}) %collective-permute-start.7) | collective-permute-done | bytes 442400 | tf_op jit(solution)/shard_map/ppermute | solution.py:424
  224.0 8.0 %collective-permute-start.9 = (bf16[192,2048]{1,0:T(8,128)(2,1)}, bf16[192,2048]{1,0:T(8,128)(2,1)S(1)}, u32[]{:S(2)}, u32[]{:S(2)}) collective-permute-start(bf16[192,2048]{1,0:T(8,128)(2,1)} %get-tuple-element.36), channel_id=1, source_target_pairs={{0,64},{64,128},{128,192},{192,0},{1,65},{65,129},{129,193},{193,1... | collective-permute-start | bytes 2359304 | tf_op jit(solution)/shard_map/ppermute | solution.py:424
  231.9 0.0 copy-done.8
  231.9 0.0 collective-permute-done.11
  231.9 0.1 collective-permute-start.1
  232.0 0.0 collective-permute-done.10
  232.0 2.6 collective-permute-start.5
  234.6 0.0 collective-permute-done.refs_1_.refs_8_
  234.6 0.0 collective-permute-start.2
  234.6 0.0 collective-permute-done.3.refs_6_.refs_13_
  234.6 0.0 copy-start.3
  234.6 2.7 collective-permute-start.4
  237.3 11.6 %collective-permute-done.9 = bf16[192,2048]{1,0:T(8,128)(2,1)S(1)} collective-permute-done((bf16[192,2048]{1,0:T(8,128)(2,1)}, bf16[192,2048]{1,0:T(8,128)(2,1)S(1)}, u32[]{:S(2)}, u32[]{:S(2)}) %collective-permute-start.9) | collective-permute-done | bytes 786464 | tf_op jit(solution)/shard_map/ppermute | solution.py:424
  248.9 1.2 collective-permute-start.8
  250.1 2.5 fusion
  252.6 0.0 copy-done.2
  252.6 40.2 %collective-permute-done.8.refs_17_ = bf16[576,384]{1,0:T(8,128)(2,1)S(1)} collective-permute-done((bf16[576,384]{1,0:T(8,128)(2,1)}, bf16[576,384]{1,0:T(8,128)(2,1)S(1)}, u32[]{:S(2)}, u32[]{:S(2)}) %collective-permute-start.8) | collective-permute-done | bytes 442400 | tf_op jit(solution)/shard_map/ppermute | solution.py:424
  292.8 0.0 collective-permute-done.1.refs_2_.refs_9_
  292.8 0.0 collective-permute-done.5.refs_5_.refs_12_
  292.8 6.7 %collective-permute-done.2.refs_3_.refs_10_ = bf16[256,2304]{1,0:T(8,128)(2,1)S(1)} collective-permute-done((bf16[256,2304]{1,0:T(8,128)(2,1)S(1)}, bf16[256,2304]{1,0:T(8,128)(2,1)S(1)}, u32[]{:S(2)}, u32[]{:S(2)}) %collective-permute-start.2) | collective-permute-done | bytes 1179680 | tf_op jit(solution)/shard_map/ppermute | solution.py:424
  299.5 0.0 collective-permute-done.4.refs_4_.refs_11_
  299.5 1.0 copy-done.6
  300.5 1.1 copy-done.7
  301.6 12.6 %gate_up_terms.1 = (bf16[192,2048]{1,0:T(8,128)(2,1)}, bf16[192,2048]{1,0:T(8,128)(2,1)}) custom-call(bf16[512,2304]{1,0:T(8,128)(2,1)} %bitcast.26, bf16[256,2304]{1,0:T(8,128)(2,1)} %copy-done.2, bf16[256,2304]{1,0:T(8,128)(2,1)} %copy-done.4, bf16[256,2304]{1,0:T(8,128)(2,1)} %copy-done.6, bf16[256,2304]{1,0:T(8,128)(2,1)} %copy-done.7, ...), custom_call_target="tpu_custom_call" | custom-call | tf_op jit(solution)/shard_map/gate_up_terms/pallas_call | solution.py:348
  314.2 0.0 all-to-all-done.2
  314.2 4.0 %combine.1 = (bf16[128,2048]{1,0:T(8,128)(2,1)}, f32[4,128]{1,0:T(4,128)}) custom-call(s32[4,128]{1,0:T(4,128)} %bitcast.38, bf16[4,128]{1,0:T(4,128)(2,1)} %bitcast.40, bf16[512,2432]{1,0:T(8,128)(2,1)} %bitcast.11.recv_ref), custom_call_target="tpu_custom_call" | custom-call | tf_op jit(solution)/shard_map/combine/pallas_call | solution.py:403
  (15 shorter events, 0.0 us)
Async XLA Ops:
  4.2 69.8 %all-to-all-start.1 = ((bf16[64,8,2304]{2,1,0:T(8,128)(2,1)}), bf16[64,8,2304]{2,1,0:T(8,128)(2,1)S(1)}, u32[]{:S(2)}, u32[]{:S(2)}) async-start(bf16[64,8,2304]{2,1,0:T(8,128)(2,1)} %bitcast.33), calls=%async_computation.1 | async-start | bytes 4718592 | tf_op jit(solution)/shard_map/all_to_all | solution.py:417
  74.0 1.4 copy-start
  75.4 62.7 %all-to-all-start = ((bf16[64,8,2304]{2,1,0:T(8,128)(2,1)}), bf16[64,8,2304]{2,1,0:T(8,128)(2,1)}, u32[]{:S(2)}, u32[]{:S(2)}) async-start(bf16[64,8,2304]{2,1,0:T(8,128)(2,1)} %bitcast.32), calls=%async_computation | async-start | bytes 4718592 | tf_op jit(solution)/shard_map/all_to_all | solution.py:417
  150.9 6.3 %copy-start.1 = (bf16[64,8,2304]{2,1,0:T(8,128)(2,1)S(1)}, bf16[64,8,2304]{2,1,0:T(8,128)(2,1)}, u32[]{:S(2)}) copy-start(bf16[64,8,2304]{2,1,0:T(8,128)(2,1)} %copy-done) | copy-start | bytes 7077892
  150.9 163.3 %all-to-all-start.2 = ((bf16[64,8,2432]{2,1,0:T(8,128)(2,1)}), bf16[64,8,2432]{2,1,0:T(8,128)(2,1)}, u32[]{:S(2)}, u32[]{:S(2)}) async-start(bf16[64,8,2432]{2,1,0:T(8,128)(2,1)} %bitcast.35), calls=%async_computation.2 | async-start | bytes 4980736 | tf_op jit(solution)/shard_map/all_to_all | solution.py:417
  158.7 75.9 %collective-permute-start = (bf16[256,2304]{1,0:T(8,128)(2,1)}, bf16[256,2304]{1,0:T(8,128)(2,1)S(1)}, u32[]{:S(2)}, u32[]{:S(2)}) collective-permute-start(bf16[256,2304]{1,0:T(8,128)(2,1)} %get-tuple-element.40), channel_id=1, source_target_pairs={{0,64},{64,128},{128,192},{192,0},{1,65},{65,129},{129,193},{193,1... | collective-permute-start | bytes 3538952 | tf_op jit(solution)/shard_map/ppermute | solution.py:424
  159.9 74.7 %collective-permute-start.3 = (bf16[256,2304]{1,0:T(8,128)(2,1)}, bf16[256,2304]{1,0:T(8,128)(2,1)S(1)}, u32[]{:S(2)}, u32[]{:S(2)}) collective-permute-start(bf16[256,2304]{1,0:T(8,128)(2,1)} %get-tuple-element.39), channel_id=1, source_target_pairs={{0,192},{64,0},{128,64},{192,128},{1,193},{65,1},{129,65},{193,129... | collective-permute-start | bytes 3538952 | tf_op jit(solution)/shard_map/ppermute | solution.py:424
  161.4 35.3 %collective-permute-start.6 = (bf16[576,384]{1,0:T(8,128)(2,1)}, bf16[576,384]{1,0:T(8,128)(2,1)S(1)}, u32[]{:S(2)}, u32[]{:S(2)}) collective-permute-start(bf16[576,384]{1,0:T(8,128)(2,1)} %get-tuple-element.29), channel_id=1, source_target_pairs={{0,64},{64,128},{128,192},{192,0},{1,65},{65,129},{129,193},{193,1... | collective-permute-start | bytes 1327112 | tf_op jit(solution)/shard_map/ppermute | solution.py:424
  161.4 35.3 %copy-start.11 = (bf16[576,384]{1,0:T(8,128)(2,1)S(1)}, bf16[576,384]{1,0:T(8,128)(2,1)}, u32[]{:S(2)}) copy-start(bf16[576,384]{1,0:T(8,128)(2,1)} %get-tuple-element.30) | copy-start | bytes 1327108
  167.1 64.8 %collective-permute-start.11 = (bf16[192,2048]{1,0:T(8,128)(2,1)}, bf16[192,2048]{1,0:T(8,128)(2,1)S(1)}, u32[]{:S(2)}, u32[]{:S(2)}) collective-permute-start(bf16[192,2048]{1,0:T(8,128)(2,1)} %get-tuple-element.38), channel_id=1, source_target_pairs={{0,192},{64,0},{128,64},{192,128},{1,193},{65,1},{129,65},{193,129... | collective-permute-start | bytes 2359304 | tf_op jit(solution)/shard_map/ppermute | solution.py:424
  169.8 62.2 %collective-permute-start.10 = (bf16[192,2048]{1,0:T(8,128)(2,1)}, bf16[192,2048]{1,0:T(8,128)(2,1)S(1)}, u32[]{:S(2)}, u32[]{:S(2)}) collective-permute-start(bf16[192,2048]{1,0:T(8,128)(2,1)} %get-tuple-element.37), channel_id=1, source_target_pairs={{0,128},{64,192},{128,0},{192,64},{1,129},{65,193},{129,1},{193,65... | collective-permute-start | bytes 2359304 | tf_op jit(solution)/shard_map/ppermute | solution.py:424
  196.7 35.2 %copy-start.8 = (bf16[576,384]{1,0:T(8,128)(2,1)}, bf16[576,384]{1,0:T(8,128)(2,1)S(1)}, u32[]{:S(2)}) copy-start(bf16[576,384]{1,0:T(8,128)(2,1)S(1)} %collective-permute-done.6.refs_15_) | copy-start | bytes 1327108
  196.7 27.2 %collective-permute-start.7 = (bf16[576,384]{1,0:T(8,128)(2,1)S(1)}, bf16[576,384]{1,0:T(8,128)(2,1)S(1)}, u32[]{:S(2)}, u32[]{:S(2)}) collective-permute-start(bf16[576,384]{1,0:T(8,128)(2,1)S(1)} %copy-done.11), channel_id=1, source_target_pairs={{0,128},{64,192},{128,0},{192,64},{1,129},{65,193},{129,1},{193,65... | collective-permute-start | bytes 1327112 | tf_op jit(solution)/shard_map/ppermute | solution.py:424
  224.0 25.0 %copy-start.9 = (bf16[576,384]{1,0:T(8,128)(2,1)}, bf16[576,384]{1,0:T(8,128)(2,1)S(1)}, u32[]{:S(2)}) copy-start(bf16[576,384]{1,0:T(8,128)(2,1)S(1)} %collective-permute-done.7.refs_16_) | copy-start | bytes 1327108
  224.0 25.0 %collective-permute-start.9 = (bf16[192,2048]{1,0:T(8,128)(2,1)}, bf16[192,2048]{1,0:T(8,128)(2,1)S(1)}, u32[]{:S(2)}, u32[]{:S(2)}) collective-permute-start(bf16[192,2048]{1,0:T(8,128)(2,1)} %get-tuple-element.36), channel_id=1, source_target_pairs={{0,64},{64,128},{128,192},{192,0},{1,65},{65,129},{129,193},{193,1... | collective-permute-start | bytes 2359304 | tf_op jit(solution)/shard_map/ppermute | solution.py:424
  231.9 60.9 %collective-permute-start.1 = (bf16[256,2304]{1,0:T(8,128)(2,1)}, bf16[256,2304]{1,0:T(8,128)(2,1)S(1)}, u32[]{:S(2)}, u32[]{:S(2)}) collective-permute-start(bf16[256,2304]{1,0:T(8,128)(2,1)} %get-tuple-element.39), channel_id=1, source_target_pairs={{0,64},{64,128},{128,192},{192,0},{1,65},{65,129},{129,193},{193,1... | collective-permute-start | bytes 3538952 | tf_op jit(solution)/shard_map/ppermute | solution.py:424
  232.0 60.8 %collective-permute-start.5 = (bf16[256,2304]{1,0:T(8,128)(2,1)}, bf16[256,2304]{1,0:T(8,128)(2,1)S(1)}, u32[]{:S(2)}, u32[]{:S(2)}) collective-permute-start(bf16[256,2304]{1,0:T(8,128)(2,1)} %get-tuple-element.40), channel_id=1, source_target_pairs={{0,192},{64,0},{128,64},{192,128},{1,193},{65,1},{129,65},{193,129... | collective-permute-start | bytes 3538952 | tf_op jit(solution)/shard_map/ppermute | solution.py:424
  234.6 18.0 %copy-start.2 = (bf16[256,2304]{1,0:T(8,128)(2,1)}, bf16[256,2304]{1,0:T(8,128)(2,1)S(1)}, u32[]{:S(2)}) copy-start(bf16[256,2304]{1,0:T(8,128)(2,1)S(1)} %collective-permute-done.refs_1_.refs_8_) | copy-start | bytes 3538948
  234.6 64.9 %collective-permute-start.2 = (bf16[256,2304]{1,0:T(8,128)(2,1)S(1)}, bf16[256,2304]{1,0:T(8,128)(2,1)S(1)}, u32[]{:S(2)}, u32[]{:S(2)}) collective-permute-start(bf16[256,2304]{1,0:T(8,128)(2,1)S(1)} %collective-permute-done.refs_1_.refs_8_), channel_id=1, source_target_pairs={{0,64},{64,128},{128,192},{192,0},{1,65},{65,129},{129,193},{193,1... | collective-permute-start | bytes 3538952 | tf_op jit(solution)/shard_map/ppermute | solution.py:424
  234.6 18.0 %copy-start.3 = (bf16[256,2304]{1,0:T(8,128)(2,1)}, bf16[256,2304]{1,0:T(8,128)(2,1)S(1)}, u32[]{:S(2)}) copy-start(bf16[256,2304]{1,0:T(8,128)(2,1)S(1)} %collective-permute-done.3.refs_6_.refs_13_) | copy-start | bytes 3538948
  234.6 64.9 %collective-permute-start.4 = (bf16[256,2304]{1,0:T(8,128)(2,1)S(1)}, bf16[256,2304]{1,0:T(8,128)(2,1)S(1)}, u32[]{:S(2)}, u32[]{:S(2)}) collective-permute-start(bf16[256,2304]{1,0:T(8,128)(2,1)S(1)} %collective-permute-done.3.refs_6_.refs_13_), channel_id=1, source_target_pairs={{0,192},{64,0},{128,64},{192,128},{1,193},{65,1},{129,65},{193,129... | collective-permute-start | bytes 3538952 | tf_op jit(solution)/shard_map/ppermute | solution.py:424
  248.9 43.9 %collective-permute-start.8 = (bf16[576,384]{1,0:T(8,128)(2,1)}, bf16[576,384]{1,0:T(8,128)(2,1)S(1)}, u32[]{:S(2)}, u32[]{:S(2)}) collective-permute-start(bf16[576,384]{1,0:T(8,128)(2,1)} %get-tuple-element.31), channel_id=1, source_target_pairs={{0,192},{64,0},{128,64},{192,128},{1,193},{65,1},{129,65},{193,129... | collective-permute-start | bytes 1327112 | tf_op jit(solution)/shard_map/ppermute | solution.py:424
  292.8 6.7 %copy-start.10 = (bf16[576,384]{1,0:T(8,128)(2,1)}, bf16[576,384]{1,0:T(8,128)(2,1)S(1)}, u32[]{:S(2)}) copy-start(bf16[576,384]{1,0:T(8,128)(2,1)S(1)} %collective-permute-done.8.refs_17_) | copy-start | bytes 1327108
  292.8 8.8 %copy-start.4 = (bf16[256,2304]{1,0:T(8,128)(2,1)}, bf16[256,2304]{1,0:T(8,128)(2,1)S(1)}, u32[]{:S(2)}) copy-start(bf16[256,2304]{1,0:T(8,128)(2,1)S(1)} %collective-permute-done.1.refs_2_.refs_9_) | copy-start | bytes 3538948
  292.8 6.7 %copy-start.5 = (bf16[256,2304]{1,0:T(8,128)(2,1)}, bf16[256,2304]{1,0:T(8,128)(2,1)S(1)}, u32[]{:S(2)}) copy-start(bf16[256,2304]{1,0:T(8,128)(2,1)S(1)} %collective-permute-done.5.refs_5_.refs_12_) | copy-start | bytes 3538948
  299.5 1.0 copy-start.6
  300.5 1.1 copy-start.7

commit v4 on v3

--- a/solution.py
+++ b/solution.py
@@ -202,12 +202,12 @@
         copy.wait()
     outs = []
     own = own_ref[0]
-    for q in range(2):
-        n = D // 2
+    for q in range(4):
+        n = D // 4
         row = dot_nt(grad_v[...], weight_v[q * n : (q + 1) * n, :]).astype(BF)
         back_v[:, q * n : (q + 1) * n] = row[:ROWS]
-        for j in range(MAIN // 2):
-            at = (q * (MAIN // 2) + j) * EXP
+        for j in range(MAIN // 4):
+            at = (q * (MAIN // 4) + j) * EXP
             spare_v[at : at + EXP, :] = row[ROWS:, j * SEG : (j + 1) * SEG]
         outs.append(start(cols(back_v, q * n, n), cols(back_ref, q * n, n), sem_out.at[q]))
         if q == 0:
@@ -216,7 +216,7 @@
                 piece_v[t, :, HS:] = grad_v[:, H + t * HS : H + (t + 1) * HS]
             for d in range(N_DP):
                 t = lax.rem(own + d, N_DP)
-                outs.append(start(piece_v.at[t], pieces[d], sem_out.at[2 + d]))
+                outs.append(start(piece_v.at[t], pieces[d], sem_out.at[4 + d]))
     back_v[:, D : D + SEG] = dot(fold_mask(), spare_v[...]).astype(BF)
     high = total.astype(BF)
     low = (total - high.astype(F32)).astype(BF)
@@ -233,7 +233,7 @@
         high[:ROWS].astype(F32),
         jnp.where(lane_rows == 1, low[:ROWS].astype(F32), dot(spread, ninth)),
     ).astype(BF)
-    outs.append(start(cols(back_v, D, SEG + 128), cols(back_ref, D, SEG + 128), sem_out.at[6]))
+    outs.append(start(cols(back_v, D, SEG + 128), cols(back_ref, D, SEG + 128), sem_out.at[8]))
     for copy in outs:
         copy.wait()
 
@@ -259,17 +259,19 @@
             pltpu.VMEM((ROWS, Y_COLS), BF),
             pltpu.VMEM((ROWS, SEG), BF),
             pltpu.SemaphoreType.DMA((8,)),
-            pltpu.SemaphoreType.DMA((7,)),
+            pltpu.SemaphoreType.DMA((9,)),
         ],
         name="rows_pass",
     )(own, recv_dy, down_mat, slope, silu, act, gate_mat, up_mat)
 
 
+HALF_H = HS // 2
+
+
 def down_kernel(
-    own_ref, turned_ref, recv_ref, out0_ref, out1_ref, out2_ref, out3_ref,
+    own_ref, turned_ref, recv_ref, same_ref, next_ref, far_top_ref, far_low_ref, prev_ref,
     rows_v, extra_v, turned_v, out_v, sem_in, sem_out,
 ):
-    outs_ref = [out0_ref, out1_ref, out2_ref, out3_ref]
     ins = [
         start(cols(recv_ref, D, SEG), extra_v, sem_in.at[1]),
         start(cols(recv_ref, 0, D), rows_v.at[pl.ds(0, ROWS)], sem_in.at[0]),
@@ -280,32 +282,52 @@
     ins[1].wait()
     ins[2].wait()
     outs = []
-    for n in range(N_DP):
-        d = (n + 1) % N_DP
+    for d in (2, 1, 3, 0):
         at = pl.multiple_of(lax.rem(own_ref[0] + d, N_DP) * HS, HS)
         out_v[d] = dot(turned_v[pl.ds(at, HS), :], rows_v[...]).astype(BF)
-        outs.append(start(out_v.at[d], outs_ref[d], sem_out.at[d]))
+        if d == 2:
+            top, low = out_v.at[d, pl.ds(0, HALF_H)], out_v.at[d, pl.ds(HALF_H, HALF_H)]
+            outs.append(start(top, far_top_ref, sem_out.at[d]))
+            outs.append(start(low, far_low_ref, sem_out.at[N_DP]))
+        else:
+            target = {0: same_ref, 1: next_ref, 3: prev_ref}[d]
+            outs.append(start(out_v.at[d], target, sem_out.at[d]))
     for copy in outs:
         copy.wait()
 
 
 def down_terms(own, turned, recv_dy):
     hbm = pl.BlockSpec(memory_space=pltpu.HBM)
+    rows = [HS, HS, HALF_H, HALF_H, HS]
     return pl.pallas_call(
         down_kernel,
         in_specs=[pl.BlockSpec(memory_space=pltpu.SMEM), hbm, hbm],
-        out_specs=[hbm] * N_DP,
-        out_shape=[jax.ShapeDtypeStruct((HS, D), BF)] * N_DP,
+        out_specs=[hbm] * len(rows),
+        out_shape=[jax.ShapeDtypeStruct((n, D), BF) for n in rows],
         scratch_shapes=[
             pltpu.VMEM((ALL, D), BF),
             pltpu.VMEM((ROWS, SEG), BF),
             pltpu.VMEM((H, ALL), BF),
             pltpu.VMEM((N_DP, HS, D), BF),
             pltpu.SemaphoreType.DMA((3,)),
-            pltpu.SemaphoreType.DMA((N_DP,)),
+            pltpu.SemaphoreType.DMA((N_DP + 1,)),
         ],
         name="down_terms",
     )(own, turned, recv_dy)
+
+
+def merge_kernel(next_ref, prev_ref, from_prev_ref, from_next_ref, next_out_ref, prev_out_ref):
+    top = next_ref[:HALF_H].astype(F32) + from_prev_ref[...].astype(F32)
+    next_out_ref[:HALF_H] = top.astype(BF)
+    next_out_ref[HALF_H:] = next_ref[HALF_H:]
+    low = prev_ref[HALF_H:].astype(F32) + from_next_ref[...].astype(F32)
+    prev_out_ref[:HALF_H] = prev_ref[:HALF_H]
+    prev_out_ref[HALF_H:] = low.astype(BF)
+
+
+def merge(*args):
+    shape = jax.ShapeDtypeStruct((HS, D), BF)
+    return pl.pallas_call(merge_kernel, out_shape=[shape, shape], name="merge")(*args)
 
 
 HALF = ROWS // 2
@@ -352,6 +374,7 @@
         out_specs=[out, out],
         out_shape=[shape, shape],
         scratch_shapes=[pltpu.VMEM((2 * HS, N_DP * ALL), BF)],
+        compiler_params=pltpu.CompilerParams(vmem_limit_bytes=65 * 1024 * 1000),
         name="gate_up_terms",
     )(*xs, *xs, *gs)
 
@@ -448,11 +471,15 @@
     back_rows = exchange(back)
     gs = [pieces[0]] + [shift(pieces[d], d) for d in range(1, N_DP)]
     terms = down_terms(own, turned, recv_dy)
-    downs = [terms[0]] + [shift(terms[d], d) for d in range(1, N_DP)]
+    own_term, next_term, far_top, far_low, prev_term = terms
+    from_prev = shift(far_top, 1)
+    from_next = shift(far_low, 3)
+    next_term, prev_term = merge(next_term, prev_term, from_prev, from_next)
+    downs = [own_term, shift(next_term, 1), shift(prev_term, 3)]
     gate_grad, up_grad = gate_up_terms(xs, gs)
     down_grad = downs[0].astype(F32)
-    for d in range(1, N_DP):
-        down_grad = down_grad + downs[d].astype(F32)
+    for term in downs[1:]:
+        down_grad = down_grad + term.astype(F32)
     tokens_grad, probs_grad = combine(ids, probs, back_rows)
     return (
         tokens_grad,

time: 320 us -> 329 us (1.028)
  the two profiles are of different devices: /device:TPU:1 before, /device:TPU:30 now
where the time goes in v4:
time: 329 us; the launch traced here: 328 us
  waiting for transfers between devices  219 us (67%)
  Pallas kernels  54.5 us (17%)
  starting transfers between devices  45.4 us (14%)
  local copies, waits for them, and re-layouts  5.55 us (2%)
    ppermute x13, waiting for transfers between devices, shift(): lax.ppermute(value, 'dp', [(i, (i + by) % N_DP) for i in range(N_DP)])  124 us
    all_to_all x3, waiting for transfers between devices, exchange(): lax.all_to_all(flat.reshape(EXP, MAIN, flat.shape[1]), 'expert', split_ax...  95 us
    all_to_all x3, starting transfers between devices, exchange(): lax.all_to_all(flat.reshape(EXP, MAIN, flat.shape[1]), 'expert', split_ax...  29.1 us
    ppermute x13, starting transfers between devices, shift(): lax.ppermute(value, 'dp', [(i, (i + by) % N_DP) for i in range(N_DP)])  16.3 us
    pallas_call x1, Pallas kernels, gate_up_terms(): pl.pallas_call(gate_up_kernel, grid=(MAIN,), in_specs=mains + spares + [g...  12.6 us
    pallas_call x1, Pallas kernels, rows_pass(): pl.pallas_call(rows_kernel, in_specs=[pl.BlockSpec(memory_space=pltpu.SME...  12.2 us
    pallas_call x1, Pallas kernels, forward(): pl.pallas_call(forward_kernel, grid=(H // 256,), in_specs=[full, weight,...  9.47 us
    pallas_call x2, Pallas kernels, pack(): pl.pallas_call(kernel, grid=(PACK_STEPS,), in_specs=[pl.BlockSpec(x.shape...  7.55 us
  transfers between devices with their start and end apart: 16, of which 6 were waited for; matrix products, arithmetic and copies ran while one was open for 1% of the time, Pallas kernels for 11%

profile of v4, /device:TPU:30, one launch (start us, length us, event | category | flops | bytes accessed | tf_op | source)
XLA Modules:
  0.0 327.8 jit_solution(2598069027928655726)
XLA Ops:
  0.6 3.6 %shard_map.111 = bf16[512,2304]{1,0:T(8,128)(2,1)} custom-call(s32[4,128]{1,0:T(4,128)} %bitcast.36, bf16[128,2048]{1,0:T(8,128)(2,1)} %data_ref.3), custom_call_target="tpu_custom_call" | custom-call | tf_op jit(solution)/shard_map/pallas_call | solution.py:91
  4.2 12.1 %all-to-all-start.1 = ((bf16[64,8,2304]{2,1,0:T(8,128)(2,1)}), bf16[64,8,2304]{2,1,0:T(8,128)(2,1)S(1)}, u32[]{:S(2)}, u32[]{:S(2)}) async-start(bf16[64,8,2304]{2,1,0:T(8,128)(2,1)} %bitcast.33), calls=%async_computation.1 | async-start | bytes 4718592 | tf_op jit(solution)/shard_map/all_to_all | solution.py:440
  16.3 3.9 %shard_map.110 = bf16[512,2304]{1,0:T(8,128)(2,1)} custom-call(s32[4,128]{1,0:T(4,128)} %bitcast.37, bf16[128,2048]{1,0:T(8,128)(2,1)} %data_ref.2, bf16[4,128]{1,0:T(4,128)(2,1)} %bitcast.39), custom_call_target="tpu_custom_call" | custom-call | tf_op jit(solution)/shard_map/pallas_call | solution.py:91
  20.3 50.3 %all-to-all-done.1 = bf16[64,8,2304]{2,1,0:T(8,128)(2,1)S(1)} async-done(((bf16[64,8,2304]{2,1,0:T(8,128)(2,1)}), bf16[64,8,2304]{2,1,0:T(8,128)(2,1)S(1)}, u32[]{:S(2)}, u32[]{:S(2)}) %all-to-all-start.1) | async-done | bytes 2359328 | tf_op jit(solution)/shard_map/all_to_all | solution.py:440
  70.6 1.4 copy-done
  72.0 8.5 %all-to-all-start = ((bf16[64,8,2304]{2,1,0:T(8,128)(2,1)}), bf16[64,8,2304]{2,1,0:T(8,128)(2,1)}, u32[]{:S(2)}, u32[]{:S(2)}) async-start(bf16[64,8,2304]{2,1,0:T(8,128)(2,1)} %bitcast.32), calls=%async_computation | async-start | bytes 4718592 | tf_op jit(solution)/shard_map/all_to_all | solution.py:440
  80.5 9.5 %forward.1 = (f32[576,768]{1,0:T(8,128)}, f32[576,768]{1,0:T(8,128)}, f32[576,768]{1,0:T(8,128)}, bf16[768,576]{1,0:T(8,128)(2,1)}) custom-call(bf16[512,2304]{1,0:T(8,128)(2,1)} %bitcast.25, bf16[2048,768]{1,0:T(8,128)(2,1)} %bitcast.28, bf16[2048,768]{1,0:T(8,128)(2,1)} %bitcast.30), custom_call_target="tpu_custom_call" | custom-call | tf_op jit(solution)/shard_map/forward/pallas_call | solution.py:143
  90.0 44.7 %all-to-all-done = bf16[64,8,2304]{2,1,0:T(8,128)(2,1)} async-done(((bf16[64,8,2304]{2,1,0:T(8,128)(2,1)}), bf16[64,8,2304]{2,1,0:T(8,128)(2,1)}, u32[]{:S(2)}, u32[]{:S(2)}) %all-to-all-start) | async-done | bytes 2359328 | tf_op jit(solution)/shard_map/all_to_all | solution.py:440
  134.7 12.2 %rows_pass.1 = (bf16[512,2432]{1,0:T(8,128)(2,1)}, bf16[576,384]{1,0:T(8,128)(2,1)}, bf16[576,384]{1,0:T(8,128)(2,1)}, bf16[576,384]{1,0:T(8,128)(2,1)}, bf16[576,384]{1,0:T(8,128)(2,1)}) custom-call(s32[1]{0:T(128)} %bitcast.2.own_ref, bf16[512,2304]{1,0:T(8,128)(2,1)} %bitcast.4.recv_ref, bf16[768,2048]{1,0:T(8,128)(2,1)} %bitcast.34, ...), custom_call_target="tpu_custom_call" | custom-call | tf_op jit(solution)/shard_map/rows_pass/pallas_call | solution.py:244
  146.9 8.5 %all-to-all-start.2 = ((bf16[64,8,2432]{2,1,0:T(8,128)(2,1)}), bf16[64,8,2432]{2,1,0:T(8,128)(2,1)}, u32[]{:S(2)}, u32[]{:S(2)}) async-start(bf16[64,8,2432]{2,1,0:T(8,128)(2,1)} %bitcast.35), calls=%async_computation.2 | async-start | bytes 4980736 | tf_op jit(solution)/shard_map/all_to_all | solution.py:440
  155.5 5.8 %down_terms.1 = (bf16[192,2048]{1,0:T(8,128)(2,1)}, bf16[192,2048]{1,0:T(8,128)(2,1)}, bf16[96,2048]{1,0:T(8,128)(2,1)}, bf16[96,2048]{1,0:T(8,128)(2,1)}, bf16[192,2048]{1,0:T(8,128)(2,1)}) custom-call(s32[1]{0:T(128)} %bitcast.2.own_ref, bf16[768,576]{1,0:T(8,128)(2,1)} %get-tuple-element.37.turned_ref, bf16[512,2304]{1,0:T(8,128)(2,1)} %bitcast.4.recv_ref), custom_call_target="tpu_custom_call" | custom-call | tf_op jit(solution)/shard_map/down_terms/pallas_call | solution.py:302
  161.3 0.9 collective-permute-start.10
  162.2 2.4 collective-permute-start.9
  164.6 1.2 slice_bitcast_fusion
  165.7 0.0 collective-permute-start
  165.7 2.0 collective-permute-start.3
  167.8 7.1 %collective-permute-done.10.from_next_ref = bf16[96,2048]{1,0:T(8,128)(2,1)} collective-permute-done((bf16[96,2048]{1,0:T(8,128)(2,1)}, bf16[96,2048]{1,0:T(8,128)(2,1)}, u32[]{:S(2)}, u32[]{:S(2)}) %collective-permute-start.10) | collective-permute-done | bytes 393248 | tf_op jit(solution)/shard_map/ppermute | solution.py:447
  174.8 0.0 collective-permute-done.9.from_prev_ref
  174.8 2.9 merge.1
  177.8 3.2 collective-permute-start.11
  181.0 0.0 collective-permute-start.6
  181.0 0.8 collective-permute-start.7
  181.8 52.5 %collective-permute-done.6.refs_15_ = bf16[576,384]{1,0:T(8,128)(2,1)S(1)} collective-permute-done((bf16[576,384]{1,0:T(8,128)(2,1)}, bf16[576,384]{1,0:T(8,128)(2,1)S(1)}, u32[]{:S(2)}, u32[]{:S(2)}) %collective-permute-start.6) | collective-permute-done | bytes 442400 | tf_op jit(solution)/shard_map/ppermute | solution.py:447
  234.4 0.0 collective-permute-start.12
  234.4 0.0 collective-permute-done.7.refs_16_
  234.4 3.6 %collective-permute-start.1 = (bf16[256,2304]{1,0:T(8,128)(2,1)}, bf16[256,2304]{1,0:T(8,128)(2,1)S(1)}, u32[]{:S(2)}, u32[]{:S(2)}) collective-permute-start(bf16[256,2304]{1,0:T(8,128)(2,1)} %get-tuple-element.45), channel_id=1, source_target_pairs={{0,64},{64,128},{128,192},{192,0},{1,65},{65,129},{129,193},{193,1... | collective-permute-start | bytes 3538952 | tf_op jit(solution)/shard_map/ppermute | solution.py:447
  238.0 0.0 collective-permute-done.11
  238.0 0.0 collective-permute-start.5
  238.0 0.0 collective-permute-done.refs_1_.refs_8_
  238.1 3.2 collective-permute-start.2
  241.3 0.0 collective-permute-done.3.refs_6_.refs_13_
  241.3 0.0 collective-permute-start.4
  241.3 15.2 %collective-permute-done.12 = bf16[192,2048]{1,0:T(8,128)(2,1)S(1)} collective-permute-done((bf16[192,2048]{1,0:T(8,128)(2,1)}, bf16[192,2048]{1,0:T(8,128)(2,1)S(1)}, u32[]{:S(2)}, u32[]{:S(2)}) %collective-permute-start.12) | collective-permute-done | bytes 786464 | tf_op jit(solution)/shard_map/ppermute | solution.py:447
  256.6 0.0 collective-permute-start.8
  256.6 2.4 fusion
  259.0 49.0 %collective-permute-done.8.refs_17_ = bf16[576,384]{1,0:T(8,128)(2,1)S(1)} collective-permute-done((bf16[576,384]{1,0:T(8,128)(2,1)}, bf16[576,384]{1,0:T(8,128)(2,1)S(1)}, u32[]{:S(2)}, u32[]{:S(2)}) %collective-permute-start.8) | collective-permute-done | bytes 442400 | tf_op jit(solution)/shard_map/ppermute | solution.py:447
  308.0 0.0 collective-permute-done.1.refs_2_.refs_9_
  308.0 0.0 collective-permute-done.5.refs_5_.refs_12_
  308.1 0.0 collective-permute-done.2.refs_3_.refs_10_
  308.1 0.0 collective-permute-done.4.refs_4_.refs_11_
  308.1 0.7 copy-done.10
  308.8 0.4 copy-done.4
  309.2 0.4 copy-done.5
  309.6 0.4 copy-done.6
  310.0 1.0 copy-done.7
  311.0 12.6 %gate_up_terms.1 = (bf16[192,2048]{1,0:T(8,128)(2,1)}, bf16[192,2048]{1,0:T(8,128)(2,1)}) custom-call(bf16[512,2304]{1,0:T(8,128)(2,1)} %bitcast.26, bf16[256,2304]{1,0:T(8,128)(2,1)} %copy-done.2, bf16[256,2304]{1,0:T(8,128)(2,1)} %copy-done.4, bf16[256,2304]{1,0:T(8,128)(2,1)} %copy-done.6, bf16[256,2304]{1,0:T(8,128)(2,1)} %copy-done.7, ...), custom_call_target="tpu_custom_call" | custom-call | tf_op jit(solution)/shard_map/gate_up_terms/pallas_call | solution.py:370
  323.6 0.0 all-to-all-done.2
  323.6 4.0 %combine.1 = (bf16[128,2048]{1,0:T(8,128)(2,1)}, f32[4,128]{1,0:T(4,128)}) custom-call(s32[4,128]{1,0:T(4,128)} %bitcast.38, bf16[4,128]{1,0:T(4,128)(2,1)} %bitcast.40, bf16[512,2432]{1,0:T(8,128)(2,1)} %bitcast.11.recv_ref), custom_call_target="tpu_custom_call" | custom-call | tf_op jit(solution)/shard_map/combine/pallas_call | solution.py:426
  (16 shorter events, 0.0 us)
Async XLA Ops:
  4.2 66.3 %all-to-all-start.1 = ((bf16[64,8,2304]{2,1,0:T(8,128)(2,1)}), bf16[64,8,2304]{2,1,0:T(8,128)(2,1)S(1)}, u32[]{:S(2)}, u32[]{:S(2)}) async-start(bf16[64,8,2304]{2,1,0:T(8,128)(2,1)} %bitcast.33), calls=%async_computation.1 | async-start | bytes 4718592 | tf_op jit(solution)/shard_map/all_to_all | solution.py:440
  70.6 1.4 copy-start
  72.0 62.7 %all-to-all-start = ((bf16[64,8,2304]{2,1,0:T(8,128)(2,1)}), bf16[64,8,2304]{2,1,0:T(8,128)(2,1)}, u32[]{:S(2)}, u32[]{:S(2)}) async-start(bf16[64,8,2304]{2,1,0:T(8,128)(2,1)} %bitcast.32), calls=%async_computation | async-start | bytes 4718592 | tf_op jit(solution)/shard_map/all_to_all | solution.py:440
  146.9 176.7 %all-to-all-start.2 = ((bf16[64,8,2432]{2,1,0:T(8,128)(2,1)}), bf16[64,8,2432]{2,1,0:T(8,128)(2,1)}, u32[]{:S(2)}, u32[]{:S(2)}) async-start(bf16[64,8,2432]{2,1,0:T(8,128)(2,1)} %bitcast.35), calls=%async_computation.2 | async-start | bytes 4980736 | tf_op jit(solution)/shard_map/all_to_all | solution.py:440
  155.5 9.1 %copy-start.1 = (bf16[64,8,2304]{2,1,0:T(8,128)(2,1)S(1)}, bf16[64,8,2304]{2,1,0:T(8,128)(2,1)}, u32[]{:S(2)}) copy-start(bf16[64,8,2304]{2,1,0:T(8,128)(2,1)} %copy-done) | copy-start | bytes 7077892
  161.3 13.6 %collective-permute-start.10 = (bf16[96,2048]{1,0:T(8,128)(2,1)}, bf16[96,2048]{1,0:T(8,128)(2,1)}, u32[]{:S(2)}, u32[]{:S(2)}) collective-permute-start(bf16[96,2048]{1,0:T(8,128)(2,1)} %get-tuple-element.42), channel_id=1, source_target_pairs={{0,192},{64,0},{128,64},{192,128},{1,193},{65,1},{129,65},{193,129... | collective-permute-start | bytes 1179656 | tf_op jit(solution)/shard_map/ppermute | solution.py:447
  162.2 12.7 %collective-permute-start.9 = (bf16[96,2048]{1,0:T(8,128)(2,1)}, bf16[96,2048]{1,0:T(8,128)(2,1)}, u32[]{:S(2)}, u32[]{:S(2)}) collective-permute-start(bf16[96,2048]{1,0:T(8,128)(2,1)} %get-tuple-element.41), channel_id=1, source_target_pairs={{0,64},{64,128},{128,192},{192,0},{1,65},{65,129},{129,193},{193,1... | collective-permute-start | bytes 1179656 | tf_op jit(solution)/shard_map/ppermute | solution.py:447
  165.7 72.3 %collective-permute-start = (bf16[256,2304]{1,0:T(8,128)(2,1)S(1)}, bf16[256,2304]{1,0:T(8,128)(2,1)S(1)}, u32[]{:S(2)}, u32[]{:S(2)}) collective-permute-start(bf16[256,2304]{1,0:T(8,128)(2,1)S(1)} %get-tuple-element.46), channel_id=1, source_target_pairs={{0,64},{64,128},{128,192},{192,0},{1,65},{65,129},{129,193},{193,1... | collective-permute-start | bytes 3538952 | tf_op jit(solution)/shard_map/ppermute | solution.py:447
  165.7 75.6 %collective-permute-start.3 = (bf16[256,2304]{1,0:T(8,128)(2,1)}, bf16[256,2304]{1,0:T(8,128)(2,1)S(1)}, u32[]{:S(2)}, u32[]{:S(2)}) collective-permute-start(bf16[256,2304]{1,0:T(8,128)(2,1)} %get-tuple-element.45), channel_id=1, source_target_pairs={{0,192},{64,0},{128,64},{192,128},{1,193},{65,1},{129,65},{193,129... | collective-permute-start | bytes 3538952 | tf_op jit(solution)/shard_map/ppermute | solution.py:447
  177.8 60.3 %collective-permute-start.11 = (bf16[192,2048]{1,0:T(8,128)(2,1)}, bf16[192,2048]{1,0:T(8,128)(2,1)S(1)}, u32[]{:S(2)}, u32[]{:S(2)}) collective-permute-start(bf16[192,2048]{1,0:T(8,128)(2,1)} %get-tuple-element.43), channel_id=1, source_target_pairs={{0,64},{64,128},{128,192},{192,0},{1,65},{65,129},{129,193},{193,1... | collective-permute-start | bytes 2359304 | tf_op jit(solution)/shard_map/ppermute | solution.py:447
  181.0 53.4 %collective-permute-start.6 = (bf16[576,384]{1,0:T(8,128)(2,1)}, bf16[576,384]{1,0:T(8,128)(2,1)S(1)}, u32[]{:S(2)}, u32[]{:S(2)}) collective-permute-start(bf16[576,384]{1,0:T(8,128)(2,1)} %get-tuple-element.32), channel_id=1, source_target_pairs={{0,64},{64,128},{128,192},{192,0},{1,65},{65,129},{129,193},{193,1... | collective-permute-start | bytes 1327112 | tf_op jit(solution)/shard_map/ppermute | solution.py:447
  181.0 53.4 %collective-permute-start.7 = (bf16[576,384]{1,0:T(8,128)(2,1)}, bf16[576,384]{1,0:T(8,128)(2,1)S(1)}, u32[]{:S(2)}, u32[]{:S(2)}) collective-permute-start(bf16[576,384]{1,0:T(8,128)(2,1)} %get-tuple-element.33), channel_id=1, source_target_pairs={{0,128},{64,192},{128,0},{192,64},{1,129},{65,193},{129,1},{193,65... | collective-permute-start | bytes 1327112 | tf_op jit(solution)/shard_map/ppermute | solution.py:447
  234.4 22.2 %copy-start.8 = (bf16[576,384]{1,0:T(8,128)(2,1)}, bf16[576,384]{1,0:T(8,128)(2,1)S(1)}, u32[]{:S(2)}) copy-start(bf16[576,384]{1,0:T(8,128)(2,1)S(1)} %collective-permute-done.6.refs_15_) | copy-start | bytes 1327108
  234.4 22.2 %collective-permute-start.12 = (bf16[192,2048]{1,0:T(8,128)(2,1)}, bf16[192,2048]{1,0:T(8,128)(2,1)S(1)}, u32[]{:S(2)}, u32[]{:S(2)}) collective-permute-start(bf16[192,2048]{1,0:T(8,128)(2,1)} %get-tuple-element.44), channel_id=1, source_target_pairs={{0,192},{64,0},{128,64},{192,128},{1,193},{65,1},{129,65},{193,129... | collective-permute-start | bytes 2359304 | tf_op jit(solution)/shard_map/ppermute | solution.py:447
  234.4 22.2 %copy-start.9 = (bf16[576,384]{1,0:T(8,128)(2,1)}, bf16[576,384]{1,0:T(8,128)(2,1)S(1)}, u32[]{:S(2)}) copy-start(bf16[576,384]{1,0:T(8,128)(2,1)S(1)} %collective-permute-done.7.refs_16_) | copy-start | bytes 1327108
  234.4 73.6 %collective-permute-start.1 = (bf16[256,2304]{1,0:T(8,128)(2,1)}, bf16[256,2304]{1,0:T(8,128)(2,1)S(1)}, u32[]{:S(2)}, u32[]{:S(2)}) collective-permute-start(bf16[256,2304]{1,0:T(8,128)(2,1)} %get-tuple-element.45), channel_id=1, source_target_pairs={{0,64},{64,128},{128,192},{192,0},{1,65},{65,129},{129,193},{193,1... | collective-permute-start | bytes 3538952 | tf_op jit(solution)/shard_map/ppermute | solution.py:447
  238.0 70.0 %collective-permute-start.5 = (bf16[256,2304]{1,0:T(8,128)(2,1)S(1)}, bf16[256,2304]{1,0:T(8,128)(2,1)S(1)}, u32[]{:S(2)}, u32[]{:S(2)}) collective-permute-start(bf16[256,2304]{1,0:T(8,128)(2,1)S(1)} %get-tuple-element.46), channel_id=1, source_target_pairs={{0,192},{64,0},{128,64},{192,128},{1,193},{65,1},{129,65},{193,129... | collective-permute-start | bytes 3538952 | tf_op jit(solution)/shard_map/ppermute | solution.py:447
  238.1 20.9 %copy-start.2 = (bf16[256,2304]{1,0:T(8,128)(2,1)}, bf16[256,2304]{1,0:T(8,128)(2,1)S(1)}, u32[]{:S(2)}) copy-start(bf16[256,2304]{1,0:T(8,128)(2,1)S(1)} %collective-permute-done.refs_1_.refs_8_) | copy-start | bytes 3538948
  238.1 70.0 %collective-permute-start.2 = (bf16[256,2304]{1,0:T(8,128)(2,1)S(1)}, bf16[256,2304]{1,0:T(8,128)(2,1)S(1)}, u32[]{:S(2)}, u32[]{:S(2)}) collective-permute-start(bf16[256,2304]{1,0:T(8,128)(2,1)S(1)} %collective-permute-done.refs_1_.refs_8_), channel_id=1, source_target_pairs={{0,64},{64,128},{128,192},{192,0},{1,65},{65,129},{129,193},{193,1... | collective-permute-start | bytes 3538952 | tf_op jit(solution)/shard_map/ppermute | solution.py:447
  241.3 17.7 %copy-start.3 = (bf16[256,2304]{1,0:T(8,128)(2,1)}, bf16[256,2304]{1,0:T(8,128)(2,1)S(1)}, u32[]{:S(2)}) copy-start(bf16[256,2304]{1,0:T(8,128)(2,1)S(1)} %collective-permute-done.3.refs_6_.refs_13_) | copy-start | bytes 3538948
  241.3 66.8 %collective-permute-start.4 = (bf16[256,2304]{1,0:T(8,128)(2,1)S(1)}, bf16[256,2304]{1,0:T(8,128)(2,1)S(1)}, u32[]{:S(2)}, u32[]{:S(2)}) collective-permute-start(bf16[256,2304]{1,0:T(8,128)(2,1)S(1)} %collective-permute-done.3.refs_6_.refs_13_), channel_id=1, source_target_pairs={{0,192},{64,0},{128,64},{192,128},{1,193},{65,1},{129,65},{193,129... | collective-permute-start | bytes 3538952 | tf_op jit(solution)/shard_map/ppermute | solution.py:447
  256.6 51.5 %collective-permute-start.8 = (bf16[576,384]{1,0:T(8,128)(2,1)}, bf16[576,384]{1,0:T(8,128)(2,1)S(1)}, u32[]{:S(2)}, u32[]{:S(2)}) collective-permute-start(bf16[576,384]{1,0:T(8,128)(2,1)} %get-tuple-element.34), channel_id=1, source_target_pairs={{0,192},{64,0},{128,64},{192,128},{1,193},{65,1},{129,65},{193,129... | collective-permute-start | bytes 1327112 | tf_op jit(solution)/shard_map/ppermute | solution.py:447
  308.0 0.8 copy-start.10
  308.0 1.1 copy-start.4
  308.0 1.6 copy-start.5
  308.1 1.9 copy-start.6
  310.0 1.0 copy-start.7

commit v5 on v4

--- a/solution.py
+++ b/solution.py
@@ -380,10 +380,8 @@
 
 
 def combine_kernel(ids_ref, probs_ref, recv_ref, rows_ref, probs_grad_ref, recv_v, sem):
-    halves = [
-        start(recv_ref.at[pl.ds(h * HALF, HALF)], recv_v.at[pl.ds(h * HALF, HALF)], sem.at[h])
-        for h in range(2)
-    ]
+    tail_in = start(cols(recv_ref, D, SEG + 128), cols(recv_v, D, SEG + 128), sem.at[0])
+    main_in = start(cols(recv_ref, 0, D), cols(recv_v, 0, D), sem.at[1])
     ids = jnp.concatenate(
         [ids_ref[...].astype(F32), jnp.zeros((8 - TOP, TOK), F32)], axis=0
     ).T.astype(jnp.int32)
@@ -401,13 +399,8 @@
     ninth = rank_slots == float(MAIN)
     main_bf = one(main).astype(BF)
     spare = jnp.concatenate([one(ninth & (sub == j)).astype(BF) for j in range(MAIN)], axis=0)
-    for copy in halves:
-        copy.wait()
+    tail_in.wait()
     extra = dot(spare, recv_v[:, D : D + SEG])
-    for j in range(MAIN):
-        at = slice(j * SEG, (j + 1) * SEG)
-        part = dot(main_bf, recv_v[:, at])
-        rows_ref[:, at] = (part + extra[j * TOK : (j + 1) * TOK, :]).astype(BF)
     lanes = one(iota((8, 128), 0) == iota((8, 128), 1)).astype(BF)
     values = dot_nt(lanes, recv_v[:, D + SEG :])
     per_slot = jnp.where(main, values[0:1] + values[1:2], 0.0)
@@ -419,6 +412,11 @@
         value = jnp.sum(jnp.where(hit, per_slot, 0.0), axis=1, keepdims=True)
         found = jnp.where(lane_k == k, value, found)
     probs_grad_ref[...] = found.T[:TOP] / probs_ref[...].astype(F32)
+    main_in.wait()
+    for j in range(MAIN):
+        at = slice(j * SEG, (j + 1) * SEG)
+        part = dot(main_bf, recv_v[:, at])
+        rows_ref[:, at] = (part + extra[j * TOK : (j + 1) * TOK, :]).astype(BF)
 
 
 def combine(ids, probs, recv):

time: 329 us -> 329 us (level)
  no operation moved by 1% of the time
where the time goes in v5:
time: 329 us; the launch traced here: 328 us
  waiting for transfers between devices  219 us (67%)
  Pallas kernels  54.7 us (17%)
  starting transfers between devices  45.4 us (14%)
  local copies, waits for them, and re-layouts  5.55 us (2%)
    ppermute x13, waiting for transfers between devices, shift(): lax.ppermute(value, 'dp', [(i, (i + by) % N_DP) for i in range(N_DP)])  124 us
    all_to_all x3, waiting for transfers between devices, exchange(): lax.all_to_all(flat.reshape(EXP, MAIN, flat.shape[1]), 'expert', split_ax...  95 us
    all_to_all x3, starting transfers between devices, exchange(): lax.all_to_all(flat.reshape(EXP, MAIN, flat.shape[1]), 'expert', split_ax...  29.1 us
    ppermute x13, starting transfers between devices, shift(): lax.ppermute(value, 'dp', [(i, (i + by) % N_DP) for i in range(N_DP)])  16.3 us
    pallas_call x1, Pallas kernels, gate_up_terms(): pl.pallas_call(gate_up_kernel, grid=(MAIN,), in_specs=mains + spares + [g...  12.6 us
    pallas_call x1, Pallas kernels, rows_pass(): pl.pallas_call(rows_kernel, in_specs=[pl.BlockSpec(memory_space=pltpu.SME...  12.2 us
    pallas_call x1, Pallas kernels, forward(): pl.pallas_call(forward_kernel, grid=(H // 256,), in_specs=[full, weight,...  9.47 us
    pallas_call x2, Pallas kernels, pack(): pl.pallas_call(kernel, grid=(PACK_STEPS,), in_specs=[pl.BlockSpec(x.shape...  7.55 us
  transfers between devices with their start and end apart: 16, of which 6 were waited for; matrix products, arithmetic and copies ran while one was open for 1% of the time, Pallas kernels for 11%

profile of v5, /device:TPU:30, one launch (start us, length us, event | category | flops | bytes accessed | tf_op | source)
XLA Modules:
  0.0 327.9 jit_solution(14509952096569516551)
XLA Ops:
  0.6 3.6 %shard_map.111 = bf16[512,2304]{1,0:T(8,128)(2,1)} custom-call(s32[4,128]{1,0:T(4,128)} %bitcast.36, bf16[128,2048]{1,0:T(8,128)(2,1)} %data_ref.3), custom_call_target="tpu_custom_call" | custom-call | tf_op jit(solution)/shard_map/pallas_call | solution.py:91
  4.2 12.1 %all-to-all-start.1 = ((bf16[64,8,2304]{2,1,0:T(8,128)(2,1)}), bf16[64,8,2304]{2,1,0:T(8,128)(2,1)S(1)}, u32[]{:S(2)}, u32[]{:S(2)}) async-start(bf16[64,8,2304]{2,1,0:T(8,128)(2,1)} %bitcast.33), calls=%async_computation.1 | async-start | bytes 4718592 | tf_op jit(solution)/shard_map/all_to_all | solution.py:438
  16.3 3.9 %shard_map.110 = bf16[512,2304]{1,0:T(8,128)(2,1)} custom-call(s32[4,128]{1,0:T(4,128)} %bitcast.37, bf16[128,2048]{1,0:T(8,128)(2,1)} %data_ref.2, bf16[4,128]{1,0:T(4,128)(2,1)} %bitcast.39), custom_call_target="tpu_custom_call" | custom-call | tf_op jit(solution)/shard_map/pallas_call | solution.py:91
  20.3 50.3 %all-to-all-done.1 = bf16[64,8,2304]{2,1,0:T(8,128)(2,1)S(1)} async-done(((bf16[64,8,2304]{2,1,0:T(8,128)(2,1)}), bf16[64,8,2304]{2,1,0:T(8,128)(2,1)S(1)}, u32[]{:S(2)}, u32[]{:S(2)}) %all-to-all-start.1) | async-done | bytes 2359328 | tf_op jit(solution)/shard_map/all_to_all | solution.py:438
  70.6 1.4 copy-done
  72.0 8.5 %all-to-all-start = ((bf16[64,8,2304]{2,1,0:T(8,128)(2,1)}), bf16[64,8,2304]{2,1,0:T(8,128)(2,1)}, u32[]{:S(2)}, u32[]{:S(2)}) async-start(bf16[64,8,2304]{2,1,0:T(8,128)(2,1)} %bitcast.32), calls=%async_computation | async-start | bytes 4718592 | tf_op jit(solution)/shard_map/all_to_all | solution.py:438
  80.5 9.5 %forward.1 = (f32[576,768]{1,0:T(8,128)}, f32[576,768]{1,0:T(8,128)}, f32[576,768]{1,0:T(8,128)}, bf16[768,576]{1,0:T(8,128)(2,1)}) custom-call(bf16[512,2304]{1,0:T(8,128)(2,1)} %bitcast.25, bf16[2048,768]{1,0:T(8,128)(2,1)} %bitcast.28, bf16[2048,768]{1,0:T(8,128)(2,1)} %bitcast.30), custom_call_target="tpu_custom_call" | custom-call | tf_op jit(solution)/shard_map/forward/pallas_call | solution.py:143
  90.0 44.7 %all-to-all-done = bf16[64,8,2304]{2,1,0:T(8,128)(2,1)} async-done(((bf16[64,8,2304]{2,1,0:T(8,128)(2,1)}), bf16[64,8,2304]{2,1,0:T(8,128)(2,1)}, u32[]{:S(2)}, u32[]{:S(2)}) %all-to-all-start) | async-done | bytes 2359328 | tf_op jit(solution)/shard_map/all_to_all | solution.py:438
  134.7 12.2 %rows_pass.1 = (bf16[512,2432]{1,0:T(8,128)(2,1)}, bf16[576,384]{1,0:T(8,128)(2,1)}, bf16[576,384]{1,0:T(8,128)(2,1)}, bf16[576,384]{1,0:T(8,128)(2,1)}, bf16[576,384]{1,0:T(8,128)(2,1)}) custom-call(s32[1]{0:T(128)} %bitcast.2.own_ref, bf16[512,2304]{1,0:T(8,128)(2,1)} %bitcast.4.recv_ref, bf16[768,2048]{1,0:T(8,128)(2,1)} %bitcast.34, ...), custom_call_target="tpu_custom_call" | custom-call | tf_op jit(solution)/shard_map/rows_pass/pallas_call | solution.py:244
  146.9 8.5 %all-to-all-start.2 = ((bf16[64,8,2432]{2,1,0:T(8,128)(2,1)}), bf16[64,8,2432]{2,1,0:T(8,128)(2,1)}, u32[]{:S(2)}, u32[]{:S(2)}) async-start(bf16[64,8,2432]{2,1,0:T(8,128)(2,1)} %bitcast.35), calls=%async_computation.2 | async-start | bytes 4980736 | tf_op jit(solution)/shard_map/all_to_all | solution.py:438
  155.5 5.8 %down_terms.1 = (bf16[192,2048]{1,0:T(8,128)(2,1)}, bf16[192,2048]{1,0:T(8,128)(2,1)}, bf16[96,2048]{1,0:T(8,128)(2,1)}, bf16[96,2048]{1,0:T(8,128)(2,1)}, bf16[192,2048]{1,0:T(8,128)(2,1)}) custom-call(s32[1]{0:T(128)} %bitcast.2.own_ref, bf16[768,576]{1,0:T(8,128)(2,1)} %get-tuple-element.37.turned_ref, bf16[512,2304]{1,0:T(8,128)(2,1)} %bitcast.4.recv_ref), custom_call_target="tpu_custom_call" | custom-call | tf_op jit(solution)/shard_map/down_terms/pallas_call | solution.py:302
  161.3 0.9 collective-permute-start.10
  162.2 2.4 collective-permute-start.9
  164.6 1.2 slice_bitcast_fusion
  165.7 0.0 collective-permute-start
  165.7 2.0 collective-permute-start.3
  167.8 7.1 %collective-permute-done.10.from_next_ref = bf16[96,2048]{1,0:T(8,128)(2,1)} collective-permute-done((bf16[96,2048]{1,0:T(8,128)(2,1)}, bf16[96,2048]{1,0:T(8,128)(2,1)}, u32[]{:S(2)}, u32[]{:S(2)}) %collective-permute-start.10) | collective-permute-done | bytes 393248 | tf_op jit(solution)/shard_map/ppermute | solution.py:445
  174.8 0.0 collective-permute-done.9.from_prev_ref
  174.8 2.9 merge.1
  177.8 3.2 collective-permute-start.11
  181.0 0.0 collective-permute-start.6
  181.0 0.8 collective-permute-start.7
  181.8 52.5 %collective-permute-done.6.refs_15_ = bf16[576,384]{1,0:T(8,128)(2,1)S(1)} collective-permute-done((bf16[576,384]{1,0:T(8,128)(2,1)}, bf16[576,384]{1,0:T(8,128)(2,1)S(1)}, u32[]{:S(2)}, u32[]{:S(2)}) %collective-permute-start.6) | collective-permute-done | bytes 442400 | tf_op jit(solution)/shard_map/ppermute | solution.py:445
  234.4 0.0 collective-permute-start.12
  234.4 0.0 collective-permute-done.7.refs_16_
  234.4 3.6 %collective-permute-start.1 = (bf16[256,2304]{1,0:T(8,128)(2,1)}, bf16[256,2304]{1,0:T(8,128)(2,1)S(1)}, u32[]{:S(2)}, u32[]{:S(2)}) collective-permute-start(bf16[256,2304]{1,0:T(8,128)(2,1)} %get-tuple-element.45), channel_id=1, source_target_pairs={{0,64},{64,128},{128,192},{192,0},{1,65},{65,129},{129,193},{193,1... | collective-permute-start | bytes 3538952 | tf_op jit(solution)/shard_map/ppermute | solution.py:445
  238.0 0.0 collective-permute-done.11
  238.0 0.0 collective-permute-start.5
  238.0 0.0 collective-permute-done.refs_1_.refs_8_
  238.1 3.2 collective-permute-start.2
  241.3 0.0 collective-permute-done.3.refs_6_.refs_13_
  241.3 0.0 collective-permute-start.4
  241.3 15.2 %collective-permute-done.12 = bf16[192,2048]{1,0:T(8,128)(2,1)S(1)} collective-permute-done((bf16[192,2048]{1,0:T(8,128)(2,1)}, bf16[192,2048]{1,0:T(8,128)(2,1)S(1)}, u32[]{:S(2)}, u32[]{:S(2)}) %collective-permute-start.12) | collective-permute-done | bytes 786464 | tf_op jit(solution)/shard_map/ppermute | solution.py:445
  256.6 0.0 collective-permute-start.8
  256.6 2.4 fusion
  259.0 49.0 %collective-permute-done.8.refs_17_ = bf16[576,384]{1,0:T(8,128)(2,1)S(1)} collective-permute-done((bf16[576,384]{1,0:T(8,128)(2,1)}, bf16[576,384]{1,0:T(8,128)(2,1)S(1)}, u32[]{:S(2)}, u32[]{:S(2)}) %collective-permute-start.8) | collective-permute-done | bytes 442400 | tf_op jit(solution)/shard_map/ppermute | solution.py:445
  308.0 0.0 collective-permute-done.1.refs_2_.refs_9_
  308.0 0.0 collective-permute-done.5.refs_5_.refs_12_
  308.1 0.0 collective-permute-done.2.refs_3_.refs_10_
  308.1 0.0 collective-permute-done.4.refs_4_.refs_11_
  308.1 0.7 copy-done.10
  308.8 0.4 copy-done.4
  309.2 0.4 copy-done.5
  309.6 0.4 copy-done.6
  310.0 1.0 copy-done.7
  311.0 12.6 %gate_up_terms.1 = (bf16[192,2048]{1,0:T(8,128)(2,1)}, bf16[192,2048]{1,0:T(8,128)(2,1)}) custom-call(bf16[512,2304]{1,0:T(8,128)(2,1)} %bitcast.26, bf16[256,2304]{1,0:T(8,128)(2,1)} %copy-done.2, bf16[256,2304]{1,0:T(8,128)(2,1)} %copy-done.4, bf16[256,2304]{1,0:T(8,128)(2,1)} %copy-done.6, bf16[256,2304]{1,0:T(8,128)(2,1)} %copy-done.7, ...), custom_call_target="tpu_custom_call" | custom-call | tf_op jit(solution)/shard_map/gate_up_terms/pallas_call | solution.py:370
  323.6 0.0 all-to-all-done.2
  323.6 4.1 %combine.1 = (bf16[128,2048]{1,0:T(8,128)(2,1)}, f32[4,128]{1,0:T(4,128)}) custom-call(s32[4,128]{1,0:T(4,128)} %bitcast.38, bf16[4,128]{1,0:T(4,128)(2,1)} %bitcast.40, bf16[512,2432]{1,0:T(8,128)(2,1)} %bitcast.11.recv_ref), custom_call_target="tpu_custom_call" | custom-call | tf_op jit(solution)/shard_map/combine/pallas_call | solution.py:424
  (16 shorter events, 0.0 us)
Async XLA Ops:
  4.2 66.3 %all-to-all-start.1 = ((bf16[64,8,2304]{2,1,0:T(8,128)(2,1)}), bf16[64,8,2304]{2,1,0:T(8,128)(2,1)S(1)}, u32[]{:S(2)}, u32[]{:S(2)}) async-start(bf16[64,8,2304]{2,1,0:T(8,128)(2,1)} %bitcast.33), calls=%async_computation.1 | async-start | bytes 4718592 | tf_op jit(solution)/shard_map/all_to_all | solution.py:438
  70.6 1.4 copy-start
  72.0 62.7 %all-to-all-start = ((bf16[64,8,2304]{2,1,0:T(8,128)(2,1)}), bf16[64,8,2304]{2,1,0:T(8,128)(2,1)}, u32[]{:S(2)}, u32[]{:S(2)}) async-start(bf16[64,8,2304]{2,1,0:T(8,128)(2,1)} %bitcast.32), calls=%async_computation | async-start | bytes 4718592 | tf_op jit(solution)/shard_map/all_to_all | solution.py:438
  146.9 176.7 %all-to-all-start.2 = ((bf16[64,8,2432]{2,1,0:T(8,128)(2,1)}), bf16[64,8,2432]{2,1,0:T(8,128)(2,1)}, u32[]{:S(2)}, u32[]{:S(2)}) async-start(bf16[64,8,2432]{2,1,0:T(8,128)(2,1)} %bitcast.35), calls=%async_computation.2 | async-start | bytes 4980736 | tf_op jit(solution)/shard_map/all_to_all | solution.py:438
  155.5 9.1 %copy-start.1 = (bf16[64,8,2304]{2,1,0:T(8,128)(2,1)S(1)}, bf16[64,8,2304]{2,1,0:T(8,128)(2,1)}, u32[]{:S(2)}) copy-start(bf16[64,8,2304]{2,1,0:T(8,128)(2,1)} %copy-done) | copy-start | bytes 7077892
  161.3 13.6 %collective-permute-start.10 = (bf16[96,2048]{1,0:T(8,128)(2,1)}, bf16[96,2048]{1,0:T(8,128)(2,1)}, u32[]{:S(2)}, u32[]{:S(2)}) collective-permute-start(bf16[96,2048]{1,0:T(8,128)(2,1)} %get-tuple-element.42), channel_id=1, source_target_pairs={{0,192},{64,0},{128,64},{192,128},{1,193},{65,1},{129,65},{193,129... | collective-permute-start | bytes 1179656 | tf_op jit(solution)/shard_map/ppermute | solution.py:445
  162.2 12.7 %collective-permute-start.9 = (bf16[96,2048]{1,0:T(8,128)(2,1)}, bf16[96,2048]{1,0:T(8,128)(2,1)}, u32[]{:S(2)}, u32[]{:S(2)}) collective-permute-start(bf16[96,2048]{1,0:T(8,128)(2,1)} %get-tuple-element.41), channel_id=1, source_target_pairs={{0,64},{64,128},{128,192},{192,0},{1,65},{65,129},{129,193},{193,1... | collective-permute-start | bytes 1179656 | tf_op jit(solution)/shard_map/ppermute | solution.py:445
  165.7 72.3 %collective-permute-start = (bf16[256,2304]{1,0:T(8,128)(2,1)S(1)}, bf16[256,2304]{1,0:T(8,128)(2,1)S(1)}, u32[]{:S(2)}, u32[]{:S(2)}) collective-permute-start(bf16[256,2304]{1,0:T(8,128)(2,1)S(1)} %get-tuple-element.46), channel_id=1, source_target_pairs={{0,64},{64,128},{128,192},{192,0},{1,65},{65,129},{129,193},{193,1... | collective-permute-start | bytes 3538952 | tf_op jit(solution)/shard_map/ppermute | solution.py:445
  165.7 75.6 %collective-permute-start.3 = (bf16[256,2304]{1,0:T(8,128)(2,1)}, bf16[256,2304]{1,0:T(8,128)(2,1)S(1)}, u32[]{:S(2)}, u32[]{:S(2)}) collective-permute-start(bf16[256,2304]{1,0:T(8,128)(2,1)} %get-tuple-element.45), channel_id=1, source_target_pairs={{0,192},{64,0},{128,64},{192,128},{1,193},{65,1},{129,65},{193,129... | collective-permute-start | bytes 3538952 | tf_op jit(solution)/shard_map/ppermute | solution.py:445
  177.8 60.3 %collective-permute-start.11 = (bf16[192,2048]{1,0:T(8,128)(2,1)}, bf16[192,2048]{1,0:T(8,128)(2,1)S(1)}, u32[]{:S(2)}, u32[]{:S(2)}) collective-permute-start(bf16[192,2048]{1,0:T(8,128)(2,1)} %get-tuple-element.43), channel_id=1, source_target_pairs={{0,64},{64,128},{128,192},{192,0},{1,65},{65,129},{129,193},{193,1... | collective-permute-start | bytes 2359304 | tf_op jit(solution)/shard_map/ppermute | solution.py:445
  181.0 53.4 %collective-permute-start.6 = (bf16[576,384]{1,0:T(8,128)(2,1)}, bf16[576,384]{1,0:T(8,128)(2,1)S(1)}, u32[]{:S(2)}, u32[]{:S(2)}) collective-permute-start(bf16[576,384]{1,0:T(8,128)(2,1)} %get-tuple-element.32), channel_id=1, source_target_pairs={{0,64},{64,128},{128,192},{192,0},{1,65},{65,129},{129,193},{193,1... | collective-permute-start | bytes 1327112 | tf_op jit(solution)/shard_map/ppermute | solution.py:445
  181.0 53.4 %collective-permute-start.7 = (bf16[576,384]{1,0:T(8,128)(2,1)}, bf16[576,384]{1,0:T(8,128)(2,1)S(1)}, u32[]{:S(2)}, u32[]{:S(2)}) collective-permute-start(bf16[576,384]{1,0:T(8,128)(2,1)} %get-tuple-element.33), channel_id=1, source_target_pairs={{0,128},{64,192},{128,0},{192,64},{1,129},{65,193},{129,1},{193,65... | collective-permute-start | bytes 1327112 | tf_op jit(solution)/shard_map/ppermute | solution.py:445
  234.4 22.2 %copy-start.8 = (bf16[576,384]{1,0:T(8,128)(2,1)}, bf16[576,384]{1,0:T(8,128)(2,1)S(1)}, u32[]{:S(2)}) copy-start(bf16[576,384]{1,0:T(8,128)(2,1)S(1)} %collective-permute-done.6.refs_15_) | copy-start | bytes 1327108
  234.4 22.2 %collective-permute-start.12 = (bf16[192,2048]{1,0:T(8,128)(2,1)}, bf16[192,2048]{1,0:T(8,128)(2,1)S(1)}, u32[]{:S(2)}, u32[]{:S(2)}) collective-permute-start(bf16[192,2048]{1,0:T(8,128)(2,1)} %get-tuple-element.44), channel_id=1, source_target_pairs={{0,192},{64,0},{128,64},{192,128},{1,193},{65,1},{129,65},{193,129... | collective-permute-start | bytes 2359304 | tf_op jit(solution)/shard_map/ppermute | solution.py:445
  234.4 22.2 %copy-start.9 = (bf16[576,384]{1,0:T(8,128)(2,1)}, bf16[576,384]{1,0:T(8,128)(2,1)S(1)}, u32[]{:S(2)}) copy-start(bf16[576,384]{1,0:T(8,128)(2,1)S(1)} %collective-permute-done.7.refs_16_) | copy-start | bytes 1327108
  234.4 73.6 %collective-permute-start.1 = (bf16[256,2304]{1,0:T(8,128)(2,1)}, bf16[256,2304]{1,0:T(8,128)(2,1)S(1)}, u32[]{:S(2)}, u32[]{:S(2)}) collective-permute-start(bf16[256,2304]{1,0:T(8,128)(2,1)} %get-tuple-element.45), channel_id=1, source_target_pairs={{0,64},{64,128},{128,192},{192,0},{1,65},{65,129},{129,193},{193,1... | collective-permute-start | bytes 3538952 | tf_op jit(solution)/shard_map/ppermute | solution.py:445
  238.0 70.0 %collective-permute-start.5 = (bf16[256,2304]{1,0:T(8,128)(2,1)S(1)}, bf16[256,2304]{1,0:T(8,128)(2,1)S(1)}, u32[]{:S(2)}, u32[]{:S(2)}) collective-permute-start(bf16[256,2304]{1,0:T(8,128)(2,1)S(1)} %get-tuple-element.46), channel_id=1, source_target_pairs={{0,192},{64,0},{128,64},{192,128},{1,193},{65,1},{129,65},{193,129... | collective-permute-start | bytes 3538952 | tf_op jit(solution)/shard_map/ppermute | solution.py:445
  238.1 20.9 %copy-start.2 = (bf16[256,2304]{1,0:T(8,128)(2,1)}, bf16[256,2304]{1,0:T(8,128)(2,1)S(1)}, u32[]{:S(2)}) copy-start(bf16[256,2304]{1,0:T(8,128)(2,1)S(1)} %collective-permute-done.refs_1_.refs_8_) | copy-start | bytes 3538948
  238.1 70.0 %collective-permute-start.2 = (bf16[256,2304]{1,0:T(8,128)(2,1)S(1)}, bf16[256,2304]{1,0:T(8,128)(2,1)S(1)}, u32[]{:S(2)}, u32[]{:S(2)}) collective-permute-start(bf16[256,2304]{1,0:T(8,128)(2,1)S(1)} %collective-permute-done.refs_1_.refs_8_), channel_id=1, source_target_pairs={{0,64},{64,128},{128,192},{192,0},{1,65},{65,129},{129,193},{193,1... | collective-permute-start | bytes 3538952 | tf_op jit(solution)/shard_map/ppermute | solution.py:445
  241.3 17.7 %copy-start.3 = (bf16[256,2304]{1,0:T(8,128)(2,1)}, bf16[256,2304]{1,0:T(8,128)(2,1)S(1)}, u32[]{:S(2)}) copy-start(bf16[256,2304]{1,0:T(8,128)(2,1)S(1)} %collective-permute-done.3.refs_6_.refs_13_) | copy-start | bytes 3538948
  241.3 66.8 %collective-permute-start.4 = (bf16[256,2304]{1,0:T(8,128)(2,1)S(1)}, bf16[256,2304]{1,0:T(8,128)(2,1)S(1)}, u32[]{:S(2)}, u32[]{:S(2)}) collective-permute-start(bf16[256,2304]{1,0:T(8,128)(2,1)S(1)} %collective-permute-done.3.refs_6_.refs_13_), channel_id=1, source_target_pairs={{0,192},{64,0},{128,64},{192,128},{1,193},{65,1},{129,65},{193,129... | collective-permute-start | bytes 3538952 | tf_op jit(solution)/shard_map/ppermute | solution.py:445
  256.6 51.5 %collective-permute-start.8 = (bf16[576,384]{1,0:T(8,128)(2,1)}, bf16[576,384]{1,0:T(8,128)(2,1)S(1)}, u32[]{:S(2)}, u32[]{:S(2)}) collective-permute-start(bf16[576,384]{1,0:T(8,128)(2,1)} %get-tuple-element.34), channel_id=1, source_target_pairs={{0,192},{64,0},{128,64},{192,128},{1,193},{65,1},{129,65},{193,129... | collective-permute-start | bytes 1327112 | tf_op jit(solution)/shard_map/ppermute | solution.py:445
  308.0 0.8 copy-start.10
  308.0 1.1 copy-start.4
  308.0 1.6 copy-start.5
  308.1 1.9 copy-start.6
  310.0 1.0 copy-start.7
